TPU v7x, 32 devices: a whole 2x2x4 slice. The times are simulated.
32 devices in a mesh: dp: 8 (over y, x, core), tensor: 4 (over z).
Axes of the slice: x: 2, y: 2, z: 4, core: 2. Of those that a mesh axis runs over, the one named last changes fastest.
Arguments:
- tokens: bfloat16 [2, 4096, 2048], P(None, ('dp', 'tensor')), may hold values from -6 to 6
- lengths: int32 [2, 8, 2], P(None, 'dp'), may hold values from 0 to 512, as said below
- mixer_gain: float32 [2048], replicated, may hold values from 0.5 to 1.5
- query_weight: bfloat16 [2048, 2048], P('dp', 'tensor'), may hold values from -0.125 to 0.125
- key_weight: bfloat16 [2048, 2048], P('dp', 'tensor'), may hold values from -0.125 to 0.125
- value_weight: bfloat16 [2048, 4096], P('dp', 'tensor'), may hold values from -0.125 to 0.125
- outgate_weight: bfloat16 [2048, 4096], P('dp', 'tensor'), may hold values from -0.125 to 0.125
- alpha_weight: bfloat16 [2048, 16], P('dp', 'tensor'), may hold values from -0.125 to 0.125
- beta_weight: bfloat16 [2048, 16], P('dp', 'tensor'), may hold values from -0.125 to 0.125
- query_conv: float32 [4, 2048], replicated, may hold values from -3 to 3
- key_conv: float32 [4, 2048], replicated, may hold values from -3 to 3
- value_conv: float32 [4, 4096], replicated, may hold values from -3 to 3
- log_rate: float32 [16], replicated, may hold values from -3 to 0
- rate_bias: float32 [16], replicated, may hold values from -5 to -2
- head_gain: float32 [256], replicated, may hold values from 0.5 to 1.5
- output_weight: bfloat16 [4096, 2048], P('tensor', 'dp'), may hold values from -0.125 to 0.125
- feed_gain: float32 [2048], replicated, may hold values from 0.5 to 1.5
- gate_weight: bfloat16 [2048, 5632], P('dp', 'tensor'), may hold values from -0.125 to 0.125
- up_weight: bfloat16 [2048, 5632], P('dp', 'tensor'), may hold values from -0.125 to 0.125
- down_weight: bfloat16 [5632, 2048], P('tensor', 'dp'), may hold values from -0.078125 to 0.078125
- cotangent: bfloat16 [2, 4096, 2048], P(None, ('dp', 'tensor')), may hold values from -6 to 6
Outputs:
- layer_out: bfloat16 [2, 4096, 2048], P(None, ('dp', 'tensor'))
- grad_tokens: float32 [2, 4096, 2048], P(None, ('dp', 'tensor'))
- grad_mixer_gain: float32 [2048], replicated
- grad_query_weight: float32 [2048, 2048], P('dp', 'tensor')
- grad_key_weight: float32 [2048, 2048], P('dp', 'tensor')
- grad_value_weight: float32 [2048, 4096], P('dp', 'tensor')
- grad_outgate_weight: float32 [2048, 4096], P('dp', 'tensor')
- grad_alpha_weight: float32 [2048, 16], P('dp', 'tensor')
- grad_beta_weight: float32 [2048, 16], P('dp', 'tensor')
- grad_query_conv: float32 [4, 2048], replicated
- grad_key_conv: float32 [4, 2048], replicated
- grad_value_conv: float32 [4, 4096], replicated
- grad_log_rate: float32 [16], replicated
- grad_rate_bias: float32 [16], replicated
- grad_head_gain: float32 [256], replicated
- grad_output_weight: float32 [4096, 2048], P('tensor', 'dp')
- grad_feed_gain: float32 [2048], replicated
- grad_gate_weight: float32 [2048, 5632], P('dp', 'tensor')
- grad_up_weight: float32 [2048, 5632], P('dp', 'tensor')
- grad_down_weight: float32 [5632, 2048], P('tensor', 'dp')
Inputs may be any that keep to these rules, and one draw needn't show every extreme that they name: Each pair is the lengths of two sequences packed into 512 rows: the first starts at row 0 and has 256 to 512 rows; the second starts at the first length rounded up to a multiple of 64, has 0 or at least 256 rows and ends within 512; the pair of micro-batch 0 and data group 0 is (512, 0).
All inputs are finite; a program needn't handle non-finite values.
Results may differ from a plain program's by a relative error of at most 0.014.
Values may be sent and summed in bfloat16 or wider, within the bound.
No kernel may reach another device: no remote copies, remote signals or barrier semaphores. Data moves between devices by JAX's collectives and lax.ppermute only.
A program may use at most 384 MiB of HBM per device.

v0:
```python
from functools import reduce

import jax
import jax.numpy as jnp
from jax import lax
from jax.sharding import PartitionSpec as P

DK = 128
DV = 256
STRETCH = 64


precise = lax.Precision.HIGHEST


def product(left_rows, matrix):
    return jnp.dot(left_rows, matrix, preferred_element_type=jnp.float32)


def product_nt(left_rows, matrix):
    return lax.dot_general(
        left_rows, matrix, (((1,), (1,)), ((), ())), preferred_element_type=jnp.float32
    )


def product_tn(left_rows, right_rows):
    return lax.dot_general(
        left_rows, right_rows, (((0,), (0,)), ((), ())), preferred_element_type=jnp.float32
    )


def rms_rows(rows_in, gain_row):
    return (
        rows_in * lax.rsqrt(jnp.mean(rows_in * rows_in, axis=-1, keepdims=True) + 1e-06) * gain_row
    )


def unit_norm(source_rows):
    return source_rows * lax.rsqrt(
        jnp.sum(source_rows * source_rows, axis=-1, keepdims=True) + 1e-06
    )


def causal_conv(raw_rows, weight, seq_start):
    positions = jnp.arange(raw_rows.shape[0], dtype=jnp.int32)
    result = raw_rows * weight[0]
    for tap_shift in range(1, weight.shape[0]):
        shifted = jnp.concatenate(
            [jnp.zeros((tap_shift, raw_rows.shape[1]), jnp.float32), raw_rows[:-tap_shift]], axis=0
        )
        valid_taps = positions - tap_shift >= seq_start
        result = result + jnp.where(valid_taps[:, None], shifted, 0.0) * weight[tap_shift]
    return result


def unit_inverse(lower_part):
    identity = jnp.eye(STRETCH, dtype=jnp.float32)
    inverse = identity - lower_part
    power_term = jnp.einsum("hts,hsu->htu", lower_part, lower_part, precision=precise)
    repeats = STRETCH.bit_length() - 2
    for repeat in range(repeats):
        inverse = inverse + jnp.einsum("hts,hsu->htu", inverse, power_term, precision=precise)
        if repeat + 1 < repeats:
            power_term = jnp.einsum("hts,hsu->htu", power_term, power_term, precision=precise)
    return inverse


def stretch_step(carry_state, inputs):
    query_block, key_block, value_block, beta_block, decay_block, keep_flag = inputs
    carry_state = carry_state * keep_flag
    inclusive = jnp.tri(STRETCH, dtype=bool)
    strict = jnp.tri(STRETCH, k=-1, dtype=bool)
    cumulative = jnp.cumsum(decay_block, axis=-1)
    spread = cumulative[:, :, None] - cumulative[:, None, :]
    within = jnp.where(inclusive, jnp.exp(jnp.where(inclusive, spread, 0.0)), 0.0)
    key_inner = jnp.einsum("htd,hsd->hts", key_block, key_block, precision=precise)
    lower_part = jnp.where(strict, beta_block[:, :, None] * key_inner * within, 0.0)
    inverse = unit_inverse(lower_part)
    growth = jnp.exp(cumulative)
    right_side = jnp.concatenate(
        [(beta_block * growth)[:, :, None] * key_block, beta_block[:, :, None] * value_block],
        axis=-1,
    )
    solved = jnp.einsum("hts,hsd->htd", inverse, right_side, precision=precise)
    key_part = solved[:, :, :DK]
    value_part = solved[:, :, DK:]
    fresh_rows = value_part - jnp.einsum("htd,hde->hte", key_part, carry_state, precision=precise)
    scores = jnp.einsum("htd,hsd->hts", query_block, key_block, precision=precise) * within
    block_out = growth[:, :, None] * jnp.einsum(
        "htd,hde->hte", query_block, carry_state, precision=precise
    )
    block_out = block_out + jnp.einsum("hts,hse->hte", scores, fresh_rows, precision=precise)
    last_sum = cumulative[:, -1:]
    tail_decay = jnp.exp(last_sum - cumulative)
    new_state = jnp.exp(last_sum)[:, :, None] * carry_state
    new_state = new_state + jnp.einsum(
        "htd,hte->hde", key_block * tail_decay[:, :, None], fresh_rows, precision=precise
    )
    return (new_state, block_out)


def delta_rule(queries, key_rows, values, beta_rows, decays, keep_state):
    stretch_count = keep_state.shape[0]
    head_count = queries.shape[1]

    def split_stretches(source):
        shaped = source.reshape((stretch_count, STRETCH) + source.shape[1:])
        return jnp.moveaxis(shaped, 2, 1)

    inputs = (
        split_stretches(queries),
        split_stretches(key_rows),
        split_stretches(values),
        split_stretches(beta_rows),
        split_stretches(decays),
        keep_state,
    )
    first_state = jnp.zeros((head_count, DK, DV), jnp.float32)
    final_state, outputs = lax.scan(jax.checkpoint(stretch_step), first_state, inputs)
    return jnp.moveaxis(outputs, 1, 2).reshape(stretch_count * STRETCH, head_count, DV)


def mixer_core(raw_parts, small_parts, seq_start, keep_state):
    query_raw, key_raw, value_raw, gate_raw, alpha_raw, beta_raw = raw_parts
    query_conv, key_conv, value_conv, log_rate, rate_bias, head_gain = small_parts
    row_count = query_raw.shape[0]
    head_count = alpha_raw.shape[1]
    queries = unit_norm(
        jax.nn.silu(causal_conv(query_raw, query_conv, seq_start)).reshape(
            row_count, head_count, DK
        )
    ) * DK ** (-0.5)
    key_rows = unit_norm(
        jax.nn.silu(causal_conv(key_raw, key_conv, seq_start)).reshape(row_count, head_count, DK)
    )
    values = jax.nn.silu(causal_conv(value_raw, value_conv, seq_start)).reshape(
        row_count, head_count, DV
    )
    beta_rows = jax.nn.sigmoid(beta_raw)
    decays = -jnp.exp(log_rate) * jax.nn.softplus(alpha_raw + rate_bias)
    delta_out = delta_rule(queries, key_rows, values, beta_rows, decays, keep_state)
    normed = (
        delta_out
        * lax.rsqrt(jnp.mean(delta_out * delta_out, axis=-1, keepdims=True) + 1e-05)
        * head_gain
    )
    gated_out = normed * jax.nn.silu(gate_raw.reshape(row_count, head_count, DV))
    return gated_out.reshape(row_count, head_count * DV)


def layout(pack_lengths, pack_rows):
    positions = jnp.arange(pack_rows, dtype=jnp.int32)
    first_len = pack_lengths[0]
    second_len = pack_lengths[1]
    second_start = (first_len + STRETCH - 1) // STRETCH * STRETCH
    seq_start = jnp.where(positions >= second_start, second_start, 0)
    live_rows = (positions < first_len) | (positions >= second_start) & (
        positions < second_start + second_len
    )
    stretch_starts = jnp.arange(pack_rows // STRETCH, dtype=jnp.int32) * STRETCH
    keep_state = jnp.where(
        (stretch_starts == 0) | (stretch_starts == second_start), 0.0, 1.0
    ).astype(jnp.float32)
    return (seq_start, keep_state, jnp.where(live_rows, 1.0, 0.0).astype(jnp.float32))


def place_cols(local_grad, full_param, tensor_index):
    empty_full = jnp.zeros(full_param.shape, jnp.float32)
    col_width = local_grad.shape[-1]
    return lax.dynamic_update_slice_in_dim(
        empty_full, local_grad, tensor_index * col_width, local_grad.ndim - 1
    )


def gather_rows(rows_in):
    return lax.all_gather(rows_in, "tensor", axis=0, tiled=True)


def gather_grads(rows_in):
    return lax.all_gather(rows_in, "tensor", axis=0, tiled=True)


def shards(
    tokens,
    lengths,
    mixer_gain,
    query_weight,
    key_weight,
    value_weight,
    outgate_weight,
    alpha_weight,
    beta_weight,
    query_conv,
    key_conv,
    value_conv,
    log_rate,
    rate_bias,
    head_gain,
    output_weight,
    feed_gain,
    gate_weight,
    up_weight,
    down_weight,
    cotangent,
):
    tensor_index = lax.axis_index("tensor")
    tensor_count = lax.axis_size("tensor")
    micro_count = tokens.shape[0]
    local_rows = tokens.shape[1]
    pack_rows = local_rows * tensor_count
    query_full, key_full, value_full, outgate_full, alpha_full, beta_full, gate_full, up_full = (
        lax.all_gather(query_weight, "dp", axis=0, tiled=True),
        lax.all_gather(key_weight, "dp", axis=0, tiled=True),
        lax.all_gather(value_weight, "dp", axis=0, tiled=True),
        lax.all_gather(outgate_weight, "dp", axis=0, tiled=True),
        lax.all_gather(alpha_weight, "dp", axis=0, tiled=True),
        lax.all_gather(beta_weight, "dp", axis=0, tiled=True),
        lax.all_gather(gate_weight, "dp", axis=0, tiled=True),
        lax.all_gather(up_weight, "dp", axis=0, tiled=True),
    )
    output_full, down_full = (
        lax.all_gather(output_weight, "dp", axis=1, tiled=True),
        lax.all_gather(down_weight, "dp", axis=1, tiled=True),
    )
    mixer_in = (query_full, key_full, value_full, outgate_full, alpha_full, beta_full)
    key_width = query_weight.shape[1]
    value_width = value_weight.shape[1]
    head_count = alpha_weight.shape[1]
    small_local = (
        lax.dynamic_slice_in_dim(query_conv, tensor_index * key_width, key_width, 1),
        lax.dynamic_slice_in_dim(key_conv, tensor_index * key_width, key_width, 1),
        lax.dynamic_slice_in_dim(value_conv, tensor_index * value_width, value_width, 1),
        lax.dynamic_slice_in_dim(log_rate, tensor_index * head_count, head_count, 0),
        lax.dynamic_slice_in_dim(rate_bias, tensor_index * head_count, head_count, 0),
        head_gain,
    )
    row_init = tuple(
        (
            jnp.zeros(matrix.shape, jnp.float32)
            for matrix in (
                query_full,
                key_full,
                value_full,
                outgate_full,
                alpha_full,
                beta_full,
                gate_full,
                up_full,
            )
        )
    )
    col_init = (jnp.zeros(output_full.shape, jnp.float32), jnp.zeros(down_full.shape, jnp.float32))
    small_init = (
        (jnp.zeros_like(mixer_gain),)
        + tuple((jnp.zeros_like(small_part) for small_part in small_local))
        + (jnp.zeros_like(feed_gain),)
    )
    out_init = jnp.zeros(tokens.shape, jnp.bfloat16)
    grad_init = jnp.zeros(tokens.shape, jnp.float32)

    def one_pack(micro_step, loop_carry):
        row_acc, col_acc, small_acc, outputs, input_grads = loop_carry
        token_rows = lax.dynamic_index_in_dim(tokens, micro_step, 0, keepdims=False).astype(
            jnp.float32
        )
        pack_lengths = lax.dynamic_index_in_dim(lengths, micro_step, 0, keepdims=False)[0]
        seq_start, keep_state, row_mask = layout(pack_lengths, pack_rows)
        own_mask = lax.dynamic_slice_in_dim(row_mask, tensor_index * local_rows, local_rows, 0)[
            :, None
        ]
        norm_one, norm_one_back = jax.vjp(rms_rows, token_rows, mixer_gain)
        first_rows = gather_rows(norm_one.astype(jnp.bfloat16))
        raw_parts = tuple((product(first_rows, matrix) for matrix in mixer_in))

        def core_apply(raw_inputs, small_inputs):
            return mixer_core(raw_inputs, small_inputs, seq_start, keep_state)

        gated, core_back = jax.vjp(core_apply, raw_parts, small_local)
        gated_low = gated.astype(jnp.bfloat16)
        middle = token_rows + lax.psum_scatter(
            product(gated_low, output_full), "tensor", scatter_dimension=0, tiled=True
        )
        norm_two, norm_two_back = jax.vjp(rms_rows, middle, feed_gain)
        second_rows = gather_rows(norm_two.astype(jnp.bfloat16))
        gate_pre = product(second_rows, gate_full)
        up_pre = product(second_rows, up_full)
        gate_sig = jax.nn.sigmoid(gate_pre)
        gate_act = gate_pre * gate_sig
        hidden_low = (gate_act * up_pre).astype(jnp.bfloat16)
        result = (
            middle
            + lax.psum_scatter(
                product(hidden_low, down_full).astype(jnp.bfloat16),
                "tensor",
                scatter_dimension=0,
                tiled=True,
            ).astype(jnp.float32)
        ) * own_mask
        outputs = lax.dynamic_update_index_in_dim(
            outputs, result.astype(jnp.bfloat16), micro_step, 0
        )
        out_grad = (
            lax.dynamic_index_in_dim(cotangent, micro_step, 0, keepdims=False).astype(jnp.float32)
            * own_mask
        )
        feed_grad_rows = gather_grads(out_grad.astype(jnp.bfloat16))
        hidden_grad = product_nt(feed_grad_rows, down_full)
        down_term = product_tn(hidden_low, feed_grad_rows)
        gate_grad = (hidden_grad * up_pre * gate_sig * (1.0 + gate_pre * (1.0 - gate_sig))).astype(
            jnp.bfloat16
        )
        up_grad = (hidden_grad * gate_act).astype(jnp.bfloat16)
        second_grad = lax.psum_scatter(
            product_nt(gate_grad, gate_full) + product_nt(up_grad, up_full),
            "tensor",
            scatter_dimension=0,
            tiled=True,
        )
        middle_norm_grad, feed_gain_grad = norm_two_back(second_grad)
        middle_grad = out_grad + middle_norm_grad
        mixer_grad_rows = gather_grads(middle_grad.astype(jnp.bfloat16))
        gated_grad = product_nt(mixer_grad_rows, output_full)
        output_term = product_tn(gated_low, mixer_grad_rows)
        raw_grads, small_grads = core_back(gated_grad)
        raw_low = tuple((grad_part.astype(jnp.bfloat16) for grad_part in raw_grads))
        term_list = [product_nt(grad_part, matrix) for grad_part, matrix in zip(raw_low, mixer_in)]
        first_grad = lax.psum_scatter(
            reduce(jnp.add, term_list).astype(jnp.bfloat16),
            "tensor",
            scatter_dimension=0,
            tiled=True,
        ).astype(jnp.float32)
        token_norm_grad, mixer_gain_grad = norm_one_back(first_grad)
        input_grads = lax.dynamic_update_index_in_dim(
            input_grads, middle_grad + token_norm_grad, micro_step, 0
        )
        query_term = product_tn(first_rows, raw_low[0])
        key_term = product_tn(first_rows, raw_low[1])
        value_term = product_tn(first_rows, raw_low[2])
        outgate_term = product_tn(first_rows, raw_low[3])
        alpha_term = product_tn(first_rows, raw_low[4])
        beta_term = product_tn(first_rows, raw_low[5])
        gate_term = product_tn(second_rows, gate_grad)
        up_term = product_tn(second_rows, up_grad)
        row_terms = (
            query_term,
            key_term,
            value_term,
            outgate_term,
            alpha_term,
            beta_term,
            gate_term,
            up_term,
        )
        col_terms = (output_term, down_term)
        row_acc = jax.tree.map(jnp.add, row_acc, tuple(row_terms))
        col_acc = jax.tree.map(jnp.add, col_acc, tuple(col_terms))
        small_terms = (mixer_gain_grad,) + tuple(small_grads) + (feed_gain_grad,)
        small_acc = jax.tree.map(jnp.add, small_acc, small_terms)
        return (row_acc, col_acc, small_acc, outputs, input_grads)

    row_acc, col_acc, small_acc, outputs, input_grads = lax.fori_loop(
        0, micro_count, one_pack, (row_init, col_init, small_init, out_init, grad_init)
    )
    row_final = (
        lax.psum_scatter(row_acc[0], "dp", scatter_dimension=0, tiled=True),
        lax.psum_scatter(row_acc[1], "dp", scatter_dimension=0, tiled=True),
        lax.psum_scatter(row_acc[2], "dp", scatter_dimension=0, tiled=True),
        lax.psum_scatter(row_acc[3], "dp", scatter_dimension=0, tiled=True),
        lax.psum_scatter(row_acc[4], "dp", scatter_dimension=0, tiled=True),
        lax.psum_scatter(row_acc[5], "dp", scatter_dimension=0, tiled=True),
        lax.psum_scatter(row_acc[6], "dp", scatter_dimension=0, tiled=True),
        lax.psum_scatter(row_acc[7], "dp", scatter_dimension=0, tiled=True),
    )
    col_final = (
        lax.psum_scatter(
            col_acc[0].astype(jnp.bfloat16), "dp", scatter_dimension=1, tiled=True
        ).astype(jnp.float32),
        lax.psum_scatter(
            col_acc[1].astype(jnp.bfloat16), "dp", scatter_dimension=1, tiled=True
        ).astype(jnp.float32),
    )
    small_final = lax.psum(
        (
            small_acc[0],
            place_cols(small_acc[1], query_conv, tensor_index),
            place_cols(small_acc[2], key_conv, tensor_index),
            place_cols(small_acc[3], value_conv, tensor_index),
            place_cols(small_acc[4], log_rate, tensor_index),
            place_cols(small_acc[5], rate_bias, tensor_index),
            small_acc[6],
            small_acc[7],
        ),
        ("dp", "tensor"),
    )
    return (
        outputs,
        input_grads,
        small_final[0],
        row_final[0],
        row_final[1],
        row_final[2],
        row_final[3],
        row_final[4],
        row_final[5],
        small_final[1],
        small_final[2],
        small_final[3],
        small_final[4],
        small_final[5],
        small_final[6],
        col_final[0],
        small_final[7],
        row_final[6],
        row_final[7],
        col_final[1],
    )


def solution(mesh):
    return jax.shard_map(
        shards,
        mesh=mesh,
        in_specs=(
            P(None, ("dp", "tensor"), None),
            P(None, "dp", None),
            P(),
            P("dp", "tensor"),
            P("dp", "tensor"),
            P("dp", "tensor"),
            P("dp", "tensor"),
            P("dp", "tensor"),
            P("dp", "tensor"),
            P(),
            P(),
            P(),
            P(),
            P(),
            P(),
            P("tensor", "dp"),
            P(),
            P("dp", "tensor"),
            P("dp", "tensor"),
            P("tensor", "dp"),
            P(None, ("dp", "tensor"), None),
        ),
        out_specs=(
            P(None, ("dp", "tensor"), None),
            P(None, ("dp", "tensor"), None),
            P(),
            P("dp", "tensor"),
            P("dp", "tensor"),
            P("dp", "tensor"),
            P("dp", "tensor"),
            P("dp", "tensor"),
            P("dp", "tensor"),
            P(),
            P(),
            P(),
            P(),
            P(),
            P(),
            P("tensor", "dp"),
            P(),
            P("dp", "tensor"),
            P("dp", "tensor"),
            P("tensor", "dp"),
        ),
        check_vma=False,
    )
```

profile of v0, /device:TPU:0, one launch (start us, length us, event | category | flops | bytes accessed | tf_op | source)
XLA Modules:
  0.0 3247.6 jit_solution(5939715157883670601)
XLA Ops:
  70.4 38.6 %all-gather.19.cloned.1.call-done = bf16[2048,1024]{1,0:T(8,128)(2,1)} async-done(((bf16[256,1024]{1,0:T(8,128)(2,1)}), bf16[2048,1024]{1,0:T(8,128)(2,1)}) %all-gather.19.cloned.1.call-update) | async-done | bytes 4194320 | tf_op jit(solution)/shard_map/all_gather | solution.py:214
  109.0 38.5 %all-gather.21.cloned.1.call-done = bf16[2048,1024]{1,0:T(8,128)(2,1)} async-done(((bf16[256,1024]{1,0:T(8,128)(2,1)}), bf16[2048,1024]{1,0:T(8,128)(2,1)}) %all-gather.21.cloned.1.call-update) | async-done | bytes 4194320 | tf_op jit(solution)/shard_map/all_gather | solution.py:215
  147.5 39.2 %all-gather.23.cloned.1.call-done = bf16[1024,2048]{1,0:T(8,128)(2,1)} async-done(((bf16[1024,256]{1,0:T(8,128)(2,1)}), bf16[1024,2048]{1,0:T(8,128)(2,1)}) %all-gather.23.cloned.1.call-update) | async-done | bytes 4194320 | tf_op jit(solution)/shard_map/all_gather | solution.py:222
  186.7 46.1 %all-gather.13.cloned.1.call-done = bf16[1408,2048]{1,0:T(8,128)(2,1)} async-done(((bf16[1408,256]{1,0:T(8,128)(2,1)}), bf16[1408,2048]{1,0:T(8,128)(2,1)}) %all-gather.13.cloned.1.call-update) | async-done | bytes 5767184 | tf_op jit(solution)/shard_map/all_gather | solution.py:223
  232.8 45.2 %all-gather.25.cloned.1.call-done = bf16[2048,1408]{1,0:T(8,128)(2,1)} async-done(((bf16[256,1408]{1,0:T(8,128)(2,1)}), bf16[2048,1408]{1,0:T(8,128)(2,1)}) %all-gather.25.cloned.1.call-update) | async-done | bytes 5767184 | tf_op jit(solution)/shard_map/all_gather | solution.py:219
  278.1 45.2 %all-gather.27.cloned.1.call-done = bf16[2048,1408]{1,0:T(8,128)(2,1)} async-done(((bf16[256,1408]{1,0:T(8,128)(2,1)}), bf16[2048,1408]{1,0:T(8,128)(2,1)}) %all-gather.27.cloned.1.call-update) | async-done | bytes 5767184 | tf_op jit(solution)/shard_map/all_gather | solution.py:218
  323.3 2009.2 %while.201 = (s32[]{:T(128)}, f32[2048,512]{1,0:T(8,128)}, f32[2048,512]{1,0:T(8,128)}, f32[2048,1024]{1,0:T(8,128)}, f32[2048,1024]{1,0:T(8,128)}, /*index=5*/f...) while((s32[]{:T(128)}, f32[2048,512]{1,0:T(8,128)}, ...), condition=%wide.region_48.49_spmd.clone, body=%wide.region_0.48_spmd.clone.sunk | while | flops 54809341952 | bytes 1332332928 | solution.py:362
  327.3 45.3 %all-gather.29.cloned.1.call-done = bf16[512,2048]{1,0:T(8,128)(2,1)} async-done(((bf16[128,2048]{1,0:T(8,128)(2,1)}), bf16[512,2048]{1,0:T(8,128)(2,1)}) %all-gather.29.cloned.1.call-update) | async-done | bytes 2097168 | tf_op jit(solution)/shard_map/while/body/eval_jaxpr/all_gather | solution.py:176
  419.1 131.3 %while.202 = (s32[]{:T(128)}, f32[4,128,256]{2,1,0:T(8,128)S(1)}, f32[8,4,64,256]{3,2,1,0:T(8,128)}, f32[8,4,128,256]{3,2,1,0:T(8,128)}, f32[8,4,64]{2,1,0:T(4,1...) while((s32[]{:T(128)}, f32[4,128,256]{2,1,0:T(8,128)S(1)}, ...), condition=%wide.region_6.6_spmd.clone.clone, body=%wide.region_4.5_spmd.clone.clone.sunk | while | flops 605872384 | bytes 9327374 | solution.py:119
  571.1 73.1 %reduce-scatter.39.cloned.1.call-done = f32[128,2048]{1,0:T(8,128)} async-done(((f32[512,2048]{1,0:T(8,128)}), f32[128,2048]{1,0:T(8,128)}) %reduce-scatter.39.cloned.1.call-update) | async-done | bytes 1048592 | tf_op jit(solution)/shard_map/while/body/eval_jaxpr/reduce_scatter | solution.py:280
  646.9 46.0 %all-gather.33.cloned.1.call-done = bf16[512,2048]{1,0:T(8,128)(2,1)} async-done(((bf16[128,2048]{1,0:T(8,128)(2,1)}), bf16[512,2048]{1,0:T(8,128)(2,1)}) %all-gather.33.cloned.1.call-update) | async-done | bytes 2097168 | tf_op jit(solution)/shard_map/while/body/eval_jaxpr/all_gather | solution.py:180
  780.0 59.1 %reduce-scatter.41.cloned.1.call-done = f32[128,2048]{1,0:T(8,128)} async-done(((f32[512,2048]{1,0:T(8,128)}), f32[128,2048]{1,0:T(8,128)}) %reduce-scatter.41.cloned.1.call-update) | async-done | bytes 1048592 | tf_op jit(solution)/shard_map/while/body/eval_jaxpr/reduce_scatter | solution.py:313
  887.7 45.3 %all-gather.35.cloned.1.call-done = bf16[512,2048]{1,0:T(8,128)(2,1)} async-done(((bf16[128,2048]{1,0:T(8,128)(2,1)}), bf16[512,2048]{1,0:T(8,128)(2,1)}) %all-gather.35.cloned.1.call-update) | async-done | bytes 2097168 | tf_op jit(solution)/shard_map/while/body/eval_jaxpr/all_gather | solution.py:180
  954.6 258.8 %while.203 = (s32[]{:T(128)}, f32[4,128,256]{2,1,0:T(8,128)S(1)}, f32[8,4,64,128]{3,2,1,0:T(8,128)}, f32[8,4,64,128]{3,2,1,0:T(8,128)}, f32[8,4,64,256]{3,2,1,0:...) while((s32[]{:T(128)}, f32[4,128,256]{2,1,0:T(8,128)S(1)}, ...), condition=%wide.region_25.25_spmd.clone, body=%wide.region_13.24_spmd.clone.sunk | while | flops 1665665024 | bytes 28596752 | solution.py:119
  1330.7 44.4 %all-gather.29.cloned.1.call-done = bf16[512,2048]{1,0:T(8,128)(2,1)} async-done(((bf16[128,2048]{1,0:T(8,128)(2,1)}), bf16[512,2048]{1,0:T(8,128)(2,1)}) %all-gather.29.cloned.1.call-update) | async-done | bytes 2097168 | tf_op jit(solution)/shard_map/while/body/eval_jaxpr/all_gather | solution.py:176
  1421.5 131.1 %while.202 = (s32[]{:T(128)}, f32[4,128,256]{2,1,0:T(8,128)S(1)}, f32[8,4,64,256]{3,2,1,0:T(8,128)}, f32[8,4,128,256]{3,2,1,0:T(8,128)}, f32[8,4,64]{2,1,0:T(4,1...) while((s32[]{:T(128)}, f32[4,128,256]{2,1,0:T(8,128)S(1)}, ...), condition=%wide.region_6.6_spmd.clone.clone, body=%wide.region_4.5_spmd.clone.clone.sunk | while | flops 605872384 | bytes 9327374 | solution.py:119
  1573.4 73.1 %reduce-scatter.39.cloned.1.call-done = f32[128,2048]{1,0:T(8,128)} async-done(((f32[512,2048]{1,0:T(8,128)}), f32[128,2048]{1,0:T(8,128)}) %reduce-scatter.39.cloned.1.call-update) | async-done | bytes 1048592 | tf_op jit(solution)/shard_map/while/body/eval_jaxpr/reduce_scatter | solution.py:280
  1649.1 46.0 %all-gather.33.cloned.1.call-done = bf16[512,2048]{1,0:T(8,128)(2,1)} async-done(((bf16[128,2048]{1,0:T(8,128)(2,1)}), bf16[512,2048]{1,0:T(8,128)(2,1)}) %all-gather.33.cloned.1.call-update) | async-done | bytes 2097168 | tf_op jit(solution)/shard_map/while/body/eval_jaxpr/all_gather | solution.py:180
  1703.4 38.4 %all-gather.31.cloned.1.call-done = bf16[512,2048]{1,0:T(8,128)(2,1)} async-done(((bf16[128,2048]{1,0:T(8,128)(2,1)}), bf16[512,2048]{1,0:T(8,128)(2,1)}) %all-gather.31.cloned.1.call-update) | async-done | bytes 2097168 | tf_op jit(solution)/shard_map/while/body/eval_jaxpr/all_gather | solution.py:176
  1782.2 59.0 %reduce-scatter.41.cloned.1.call-done = f32[128,2048]{1,0:T(8,128)} async-done(((f32[512,2048]{1,0:T(8,128)}), f32[128,2048]{1,0:T(8,128)}) %reduce-scatter.41.cloned.1.call-update) | async-done | bytes 1048592 | tf_op jit(solution)/shard_map/while/body/eval_jaxpr/reduce_scatter | solution.py:313
  1890.0 45.5 %all-gather.35.cloned.1.call-done = bf16[512,2048]{1,0:T(8,128)(2,1)} async-done(((bf16[128,2048]{1,0:T(8,128)(2,1)}), bf16[512,2048]{1,0:T(8,128)(2,1)}) %all-gather.35.cloned.1.call-update) | async-done | bytes 2097168 | tf_op jit(solution)/shard_map/while/body/eval_jaxpr/all_gather | solution.py:180
  1957.1 258.8 %while.203 = (s32[]{:T(128)}, f32[4,128,256]{2,1,0:T(8,128)S(1)}, f32[8,4,64,128]{3,2,1,0:T(8,128)}, f32[8,4,64,128]{3,2,1,0:T(8,128)}, f32[8,4,64,256]{3,2,1,0:...) while((s32[]{:T(128)}, f32[4,128,256]{2,1,0:T(8,128)S(1)}, ...), condition=%wide.region_25.25_spmd.clone, body=%wide.region_13.24_spmd.clone.sunk | while | flops 1665665024 | bytes 28596752 | solution.py:119
  2413.8 53.0 %reduce-scatter.27.cloned.1.call-done = bf16[1024,256]{1,0:T(8,128)(2,1)} async-done(((bf16[1024,2048]{1,0:T(8,128)(2,1)}), bf16[1024,256]{1,0:T(8,128)(2,1)}) %reduce-scatter.27.cloned.1.call-update) | async-done | bytes 524304 | tf_op jit(solution)/shard_map/reduce_scatter | solution.py:376
  2468.8 60.8 %reduce-scatter.33.cloned.1.call-done = bf16[1408,256]{1,0:T(8,128)(2,1)} async-done(((bf16[1408,2048]{1,0:T(8,128)(2,1)}), bf16[1408,256]{1,0:T(8,128)(2,1)}) %reduce-scatter.33.cloned.1.call-update) | async-done | bytes 720912 | tf_op jit(solution)/shard_map/reduce_scatter | solution.py:379
  2532.0 121.4 %all-reduce.37.cloned.1.call-done = f32[4,4096]{1,0:T(4,128)} async-done(((f32[4,4096]{1,0:T(4,128)}), f32[4,4096]{1,0:T(4,128)}) %all-reduce.37.cloned.1.call-update) | async-done | bytes 65552 | tf_op jit(solution)/shard_map/psum | solution.py:383
  2653.4 131.7 %all-reduce.39.cloned.1.call-done = (f32[2048]{0:T(1024)}, f32[4,2048]{1,0:T(4,128)}, f32[4,2048]{1,0:T(4,128)}, f32[16]{0:T(128)}, f32[16]{0:T(128)}, /*index=5*/f32[256]{0:T(256)}, f32[2048]{0:T(1024)}) async-done(((f32[2048]{0:T(1024)}, f32[4,2048]{1,0:T(4,128)}, f32[4,2048]{1,0:T(4,128)}, f32[16]{0:T(128)}, f32[16]{0:T(128)}, /*index=5*/f32[256]{0:T(256)}, f32[2048]{0:T(1024)}), (f32[2048]{0:T(1024)}, ...) | async-done | bytes 83088 | tf_op jit(solution)/shard_map/psum | solution.py:383
  2785.1 56.8 %reduce-scatter.19.cloned.1.call-done = f32[256,512]{1,0:T(8,128)} async-done(((f32[2048,512]{1,0:T(8,128)}), f32[256,512]{1,0:T(8,128)}) %reduce-scatter.19.cloned.1.call-update) | async-done | bytes 524304 | tf_op jit(solution)/shard_map/reduce_scatter | solution.py:366
  2841.9 55.3 %reduce-scatter.21.cloned.1.call-done = f32[256,512]{1,0:T(8,128)} async-done(((f32[2048,512]{1,0:T(8,128)}), f32[256,512]{1,0:T(8,128)}) %reduce-scatter.21.cloned.1.call-update) | async-done | bytes 524304 | tf_op jit(solution)/shard_map/reduce_scatter | solution.py:367
  2897.2 75.6 %reduce-scatter.23.cloned.1.call-done = f32[256,1024]{1,0:T(8,128)} async-done(((f32[2048,1024]{1,0:T(8,128)}), f32[256,1024]{1,0:T(8,128)}) %reduce-scatter.23.cloned.1.call-update) | async-done | bytes 1048592 | tf_op jit(solution)/shard_map/reduce_scatter | solution.py:368
  2972.8 75.4 %reduce-scatter.25.cloned.1.call-done = f32[256,1024]{1,0:T(8,128)} async-done(((f32[2048,1024]{1,0:T(8,128)}), f32[256,1024]{1,0:T(8,128)}) %reduce-scatter.25.cloned.1.call-update) | async-done | bytes 1048592 | tf_op jit(solution)/shard_map/reduce_scatter | solution.py:369
  3048.1 91.3 %reduce-scatter.29.cloned.1.call-done = f32[256,1408]{1,0:T(8,128)} async-done(((f32[2048,1408]{1,0:T(8,128)}), f32[256,1408]{1,0:T(8,128)}) %reduce-scatter.29.cloned.1.call-update) | async-done | bytes 1441808 | tf_op jit(solution)/shard_map/reduce_scatter | solution.py:372
  3139.4 91.1 %reduce-scatter.31.cloned.1.call-done = f32[256,1408]{1,0:T(8,128)} async-done(((f32[2048,1408]{1,0:T(8,128)}), f32[256,1408]{1,0:T(8,128)}) %reduce-scatter.31.cloned.1.call-update) | async-done | bytes 1441808 | tf_op jit(solution)/shard_map/reduce_scatter | solution.py:373
  (2635 shorter events, 1571.0 us)
Async XLA Ops:
  8.0 62.4 %all-gather.17.cloned.1.call-start = ((), (), s32[]{:S(2)}) async-start(), calls=%async_computation.16 | async-start | bytes 2359296 | tf_op jit(solution)/shard_map/all_gather | solution.py:213
  8.8 100.3 %all-gather.19.cloned.1.call-start = ((), (), s32[]{:S(2)}) async-start(), calls=%async_computation.17 | async-start | bytes 4718592 | tf_op jit(solution)/shard_map/all_gather | solution.py:214
  9.5 138.0 %all-gather.21.cloned.1.call-start = ((), (), s32[]{:S(2)}) async-start(), calls=%async_computation.18 | async-start | bytes 4718592 | tf_op jit(solution)/shard_map/all_gather | solution.py:215
  10.1 176.6 %all-gather.23.cloned.1.call-start = ((), (), s32[]{:S(2)}) async-start(), calls=%async_computation.19 | async-start | bytes 4718592 | tf_op jit(solution)/shard_map/all_gather | solution.py:222
  10.7 222.2 %all-gather.13.cloned.1.call-start = ((), (), s32[]{:S(2)}) async-start(), calls=%async_computation.14 | async-start | bytes 6488064 | tf_op jit(solution)/shard_map/all_gather | solution.py:223
  11.3 266.8 %all-gather.25.cloned.1.call-start = ((), (), s32[]{:S(2)}) async-start(), calls=%async_computation.20 | async-start | bytes 6488064 | tf_op jit(solution)/shard_map/all_gather | solution.py:219
  12.0 311.3 %all-gather.27.cloned.1.call-start = ((), (), s32[]{:S(2)}) async-start(), calls=%async_computation.21 | async-start | bytes 6488064 | tf_op jit(solution)/shard_map/all_gather | solution.py:218
  324.9 319.4 %reduce-scatter.39.cloned.1.call-start = ((), (), s32[]{:S(2)}) async-start(), calls=%async_computation.35 | async-start | bytes 5242880 | tf_op jit(solution)/shard_map/while/body/eval_jaxpr/reduce_scatter | solution.py:280
  568.6 124.3 %all-gather.33.cloned.1.call-start = ((), (), s32[]{:S(2)}) async-start(), calls=%async_computation.37 | async-start | bytes 2621440 | tf_op jit(solution)/shard_map/while/body/eval_jaxpr/all_gather | solution.py:180
  571.1 168.5 %all-gather.31.cloned.1.call-start = ((), (), s32[]{:S(2)}) async-start(), calls=%async_computation.36 | async-start | bytes 2621440 | tf_op jit(solution)/shard_map/while/body/eval_jaxpr/all_gather | solution.py:176
  646.8 192.2 %reduce-scatter.41.cloned.1.call-start = ((), (), s32[]{:S(2)}) async-start(), calls=%async_computation.38 | async-start | bytes 5242880 | tf_op jit(solution)/shard_map/while/body/eval_jaxpr/reduce_scatter | solution.py:313
  763.4 122.3 %reduce-scatter.45.cloned.1.call-start = ((), (), s32[]{:S(2)}) async-start(), calls=%async_computation.41 | async-start | bytes 2621440 | tf_op jit(solution)/shard_map/while/body/eval_jaxpr/reduce_scatter | solution.py:292
  771.3 161.7 %all-gather.35.cloned.1.call-start = ((), (), s32[]{:S(2)}) async-start(), calls=%async_computation.39 | async-start | bytes 2621440 | tf_op jit(solution)/shard_map/while/body/eval_jaxpr/all_gather | solution.py:180
  842.4 479.9 %reduce-scatter.43.cloned.1.call-start = ((), (), s32[]{:S(2)}) async-start(), calls=%async_computation.40 | async-start | bytes 2621440 | tf_op jit(solution)/shard_map/while/body/eval_jaxpr/reduce_scatter | solution.py:327
  1328.3 318.2 %reduce-scatter.39.cloned.1.call-start = ((), (), s32[]{:S(2)}) async-start(), calls=%async_computation.35 | async-start | bytes 5242880 | tf_op jit(solution)/shard_map/while/body/eval_jaxpr/reduce_scatter | solution.py:280
  1570.9 124.2 %all-gather.33.cloned.1.call-start = ((), (), s32[]{:S(2)}) async-start(), calls=%async_computation.37 | async-start | bytes 2621440 | tf_op jit(solution)/shard_map/while/body/eval_jaxpr/all_gather | solution.py:180
  1573.3 168.4 %all-gather.31.cloned.1.call-start = ((), (), s32[]{:S(2)}) async-start(), calls=%async_computation.36 | async-start | bytes 2621440 | tf_op jit(solution)/shard_map/while/body/eval_jaxpr/all_gather | solution.py:176
  1649.0 192.2 %reduce-scatter.41.cloned.1.call-start = ((), (), s32[]{:S(2)}) async-start(), calls=%async_computation.38 | async-start | bytes 5242880 | tf_op jit(solution)/shard_map/while/body/eval_jaxpr/reduce_scatter | solution.py:313
  1765.6 122.4 %reduce-scatter.45.cloned.1.call-start = ((), (), s32[]{:S(2)}) async-start(), calls=%async_computation.41 | async-start | bytes 2621440 | tf_op jit(solution)/shard_map/while/body/eval_jaxpr/reduce_scatter | solution.py:292
  1773.5 162.0 %all-gather.35.cloned.1.call-start = ((), (), s32[]{:S(2)}) async-start(), calls=%async_computation.39 | async-start | bytes 2621440 | tf_op jit(solution)/shard_map/while/body/eval_jaxpr/all_gather | solution.py:180
  1844.6 480.2 %reduce-scatter.43.cloned.1.call-start = ((), (), s32[]{:S(2)}) async-start(), calls=%async_computation.40 | async-start | bytes 2621440 | tf_op jit(solution)/shard_map/while/body/eval_jaxpr/reduce_scatter | solution.py:327
  2334.7 77.5 %reduce-scatter.37.cloned.1.call-start = ((), (), s32[]{:S(2)}) async-start(), calls=%async_computation.32 | async-start | bytes 1179648
  2336.2 130.6 %reduce-scatter.27.cloned.1.call-start = ((), (), s32[]{:S(2)}) async-start(), calls=%async_computation.27 | async-start | bytes 4718592 | tf_op jit(solution)/shard_map/reduce_scatter | solution.py:376
  2342.3 187.3 %reduce-scatter.33.cloned.1.call-start = ((), (), s32[]{:S(2)}) async-start(), calls=%async_computation.30 | async-start | bytes 6488064 | tf_op jit(solution)/shard_map/reduce_scatter | solution.py:379
  2350.4 302.9 %all-reduce.37.cloned.1.call-start = ((), (), s32[]{:S(2)}) async-start(), calls=%async_computation.26 | async-start | bytes 131072 | tf_op jit(solution)/shard_map/psum | solution.py:383
  2351.8 433.3 %all-reduce.39.cloned.1.call-start = ((), (), s32[]{:S(2)}) async-start(), calls=%async_computation.33 | async-start | bytes 167936 | tf_op jit(solution)/shard_map/psum | solution.py:383
  2352.9 488.9 %reduce-scatter.19.cloned.1.call-start = ((), (), s32[]{:S(2)}) async-start(), calls=%async_computation.22 | async-start | bytes 4718592 | tf_op jit(solution)/shard_map/reduce_scatter | solution.py:366
  2353.7 543.5 %reduce-scatter.21.cloned.1.call-start = ((), (), s32[]{:S(2)}) async-start(), calls=%async_computation.23 | async-start | bytes 4718592 | tf_op jit(solution)/shard_map/reduce_scatter | solution.py:367
  2354.4 618.4 %reduce-scatter.23.cloned.1.call-start = ((), (), s32[]{:S(2)}) async-start(), calls=%async_computation.24 | async-start | bytes 9437184 | tf_op jit(solution)/shard_map/reduce_scatter | solution.py:368
  2355.0 693.1 %reduce-scatter.25.cloned.1.call-start = ((), (), s32[]{:S(2)}) async-start(), calls=%async_computation.25 | async-start | bytes 9437184 | tf_op jit(solution)/shard_map/reduce_scatter | solution.py:369
  2355.7 783.7 %reduce-scatter.29.cloned.1.call-start = ((), (), s32[]{:S(2)}) async-start(), calls=%async_computation.28 | async-start | bytes 12976128 | tf_op jit(solution)/shard_map/reduce_scatter | solution.py:372
  2356.5 874.0 %reduce-scatter.31.cloned.1.call-start = ((), (), s32[]{:S(2)}) async-start(), calls=%async_computation.29 | async-start | bytes 12976128 | tf_op jit(solution)/shard_map/reduce_scatter | solution.py:373
  (308 other events, 5770.0 us)
Sparse Core Ops, SparseCore 0:
  72.3 36.7 all-gather.18
  110.8 36.7 all-gather.20
  149.3 37.4 all-gather.22
  188.5 44.3 all-gather.12
  234.7 43.3 all-gather.24
  280.0 43.3 all-gather.26
  326.7 45.9 all-gather.28
  568.7 75.4 reduce-scatter.38
  646.4 46.4 all-gather.32
  694.9 44.6 all-gather.30
  763.5 75.4 reduce-scatter.40
  841.3 44.3 reduce-scatter.44
  887.7 45.2 all-gather.34
  1279.7 42.5 reduce-scatter.42
  1329.8 45.2 all-gather.28
  1571.0 75.4 reduce-scatter.38
  1648.6 46.4 all-gather.32
  1697.1 44.6 all-gather.30
  1765.7 75.4 reduce-scatter.40
  1843.6 44.3 reduce-scatter.44
  1890.2 45.2 all-gather.34
  2282.2 42.5 reduce-scatter.42
  2415.4 51.2 reduce-scatter.26
  2470.6 59.0 reduce-scatter.32
  2535.8 117.4 all-reduce.36
  2660.8 124.2 all-reduce.38
  2789.4 52.4 reduce-scatter.18
  2845.8 51.3 reduce-scatter.20
  2901.4 71.2 reduce-scatter.22
  2976.8 71.2 reduce-scatter.24
  3052.6 86.7 reduce-scatter.28
  3143.7 86.7 reduce-scatter.30
  (4 shorter events, 129.7 us)
where the time goes:
time: 3260 us; the launch traced here: 3250 us
  waiting for transfers between devices  1840 us (56%)
  matrix products  862 us (26%)
  local copies, waits for them, and re-layouts  259 us (8%)
  other arithmetic  231 us (7%)
    psum x2, waiting for transfers between devices, shards(): lax.psum((small_acc[0], place_cols(small_acc[1], query_conv, tensor_index...  253 us
    all_gather x4, waiting for transfers between devices, gather_grads(): return lax.all_gather(rows_in, 'tensor', axis=0, tiled=True)  183 us
    all_gather x4, waiting for transfers between devices, gather_rows(): return lax.all_gather(rows_in, 'tensor', axis=0, tiled=True)  166 us
    reduce_scatter x2, waiting for transfers between devices, one_pack(): lax.psum_scatter(product(gated_low, output_full), 'tensor', scatter_dimen...  146 us
    reduce_scatter x2, waiting for transfers between devices, one_pack(): lax.psum_scatter(product_nt(gate_grad, gate_full) + product_nt(up_grad, u...  118 us
    dot_general x320, matrix products, unit_inverse(): jnp.einsum('hts,hsu->htu', inverse, power_term, precision=precise)  104 us
    dot_general x20, matrix products, product_nt(): lax.dot_general(left_rows, matrix, (((1,), (1,)), ((), ())), preferred_el...  99.6 us
    dot_general x64, matrix products, stretch_step(): jnp.einsum('htd,hde->hte', query_block, carry_state, precision=precise)  94 us
  transfers between devices with their start and end apart: 36, of which 36 were waited for; matrix products, arithmetic and copies ran while one was open for 6% of the time, Pallas kernels for 0%

commit v1 on v0

v1 whole, which is shorter than its diff:
```python
import jax
import jax.numpy as jnp
from jax import lax
from jax.sharding import PartitionSpec as P

DK = 128
DV = 256
STRETCH = 64


precise = lax.Precision.HIGHEST


def product(left_rows, matrix):
    return jnp.dot(left_rows, matrix, preferred_element_type=jnp.float32)


def product_nt(left_rows, matrix):
    return lax.dot_general(
        left_rows, matrix, (((1,), (1,)), ((), ())), preferred_element_type=jnp.float32
    )


def product_tn(left_rows, right_rows):
    return lax.dot_general(
        left_rows, right_rows, (((0,), (0,)), ((), ())), preferred_element_type=jnp.float32
    )


def rms_rows(rows_in, gain_row):
    return (
        rows_in * lax.rsqrt(jnp.mean(rows_in * rows_in, axis=-1, keepdims=True) + 1e-06) * gain_row
    )


def unit_norm(source_rows):
    return source_rows * lax.rsqrt(
        jnp.sum(source_rows * source_rows, axis=-1, keepdims=True) + 1e-06
    )


def causal_conv(raw_rows, weight, seq_start):
    positions = jnp.arange(raw_rows.shape[0], dtype=jnp.int32)
    result = raw_rows * weight[0]
    for tap_shift in range(1, weight.shape[0]):
        shifted = jnp.concatenate(
            [jnp.zeros((tap_shift, raw_rows.shape[1]), jnp.float32), raw_rows[:-tap_shift]], axis=0
        )
        valid_taps = positions - tap_shift >= seq_start
        result = result + jnp.where(valid_taps[:, None], shifted, 0.0) * weight[tap_shift]
    return result


def unit_inverse(lower_part):
    identity = jnp.eye(STRETCH, dtype=jnp.float32)
    inverse = identity - lower_part
    power_term = jnp.einsum("hts,hsu->htu", lower_part, lower_part, precision=precise)
    repeats = STRETCH.bit_length() - 2
    for repeat in range(repeats):
        inverse = inverse + jnp.einsum("hts,hsu->htu", inverse, power_term, precision=precise)
        if repeat + 1 < repeats:
            power_term = jnp.einsum("hts,hsu->htu", power_term, power_term, precision=precise)
    return inverse


def stretch_step(carry_state, inputs):
    query_block, key_block, value_block, beta_block, decay_block, keep_flag = inputs
    carry_state = carry_state * keep_flag
    inclusive = jnp.tri(STRETCH, dtype=bool)
    strict = jnp.tri(STRETCH, k=-1, dtype=bool)
    cumulative = jnp.einsum("ts,hs->ht", inclusive.astype(jnp.float32), decay_block, precision=precise)
    spread = cumulative[:, :, None] - cumulative[:, None, :]
    within = jnp.where(inclusive, jnp.exp(jnp.where(inclusive, spread, 0.0)), 0.0)
    key_inner = jnp.einsum("htd,hsd->hts", key_block, key_block, precision=precise)
    lower_part = jnp.where(strict, beta_block[:, :, None] * key_inner * within, 0.0)
    inverse = unit_inverse(lower_part)
    growth = jnp.exp(cumulative)
    right_side = jnp.concatenate(
        [(beta_block * growth)[:, :, None] * key_block, beta_block[:, :, None] * value_block],
        axis=-1,
    )
    solved = jnp.einsum("hts,hsd->htd", inverse, right_side, precision=precise)
    key_part = solved[:, :, :DK]
    value_part = solved[:, :, DK:]
    fresh_rows = value_part - jnp.einsum("htd,hde->hte", key_part, carry_state, precision=precise)
    scores = jnp.einsum("htd,hsd->hts", query_block, key_block, precision=precise) * within
    block_out = growth[:, :, None] * jnp.einsum(
        "htd,hde->hte", query_block, carry_state, precision=precise
    )
    block_out = block_out + jnp.einsum("hts,hse->hte", scores, fresh_rows, precision=precise)
    last_sum = cumulative[:, -1:]
    tail_decay = jnp.exp(last_sum - cumulative)
    new_state = jnp.exp(last_sum)[:, :, None] * carry_state
    new_state = new_state + jnp.einsum(
        "htd,hte->hde", key_block * tail_decay[:, :, None], fresh_rows, precision=precise
    )
    return (new_state, block_out)


def delta_rule(queries, key_rows, values, beta_rows, decays, keep_state):
    stretch_count = keep_state.shape[0]
    head_count = queries.shape[1]

    def split_stretches(source):
        shaped = source.reshape((stretch_count, STRETCH) + source.shape[1:])
        return jnp.moveaxis(shaped, 2, 1)

    inputs = (
        split_stretches(queries),
        split_stretches(key_rows),
        split_stretches(values),
        split_stretches(beta_rows),
        split_stretches(decays),
        keep_state,
    )
    first_state = jnp.zeros((head_count, DK, DV), jnp.float32)
    final_state, outputs = lax.scan(jax.checkpoint(stretch_step), first_state, inputs)
    return jnp.moveaxis(outputs, 1, 2).reshape(stretch_count * STRETCH, head_count, DV)


def mixer_core(raw_parts, small_parts, seq_start, keep_state):
    query_raw, key_raw, value_raw, gate_raw, alpha_raw, beta_raw = raw_parts
    query_conv, key_conv, value_conv, log_rate, rate_bias, head_gain = small_parts
    row_count = query_raw.shape[0]
    head_count = alpha_raw.shape[1]
    queries = unit_norm(
        jax.nn.silu(causal_conv(query_raw, query_conv, seq_start)).reshape(
            row_count, head_count, DK
        )
    ) * DK ** (-0.5)
    key_rows = unit_norm(
        jax.nn.silu(causal_conv(key_raw, key_conv, seq_start)).reshape(row_count, head_count, DK)
    )
    values = jax.nn.silu(causal_conv(value_raw, value_conv, seq_start)).reshape(
        row_count, head_count, DV
    )
    beta_rows = jax.nn.sigmoid(beta_raw)
    decays = -jnp.exp(log_rate) * jax.nn.softplus(alpha_raw + rate_bias)
    delta_out = delta_rule(queries, key_rows, values, beta_rows, decays, keep_state)
    normed = (
        delta_out
        * lax.rsqrt(jnp.mean(delta_out * delta_out, axis=-1, keepdims=True) + 1e-05)
        * head_gain
    )
    gated_out = normed * jax.nn.silu(gate_raw.reshape(row_count, head_count, DV))
    return gated_out.reshape(row_count, head_count * DV)


def layout(pack_lengths, pack_rows):
    positions = jnp.arange(pack_rows, dtype=jnp.int32)
    first_len = pack_lengths[0]
    second_len = pack_lengths[1]
    second_start = (first_len + STRETCH - 1) // STRETCH * STRETCH
    seq_start = jnp.where(positions >= second_start, second_start, 0)
    live_rows = (positions < first_len) | (positions >= second_start) & (
        positions < second_start + second_len
    )
    stretch_starts = jnp.arange(pack_rows // STRETCH, dtype=jnp.int32) * STRETCH
    keep_state = jnp.where(
        (stretch_starts == 0) | (stretch_starts == second_start), 0.0, 1.0
    ).astype(jnp.float32)
    return (seq_start, keep_state, jnp.where(live_rows, 1.0, 0.0).astype(jnp.float32))


LANES = 128


def z_gather(own):
    count = lax.axis_size("tensor")
    if count != 4:
        return lax.all_gather(own, "tensor", axis=0, tiled=True)
    t = lax.axis_index("tensor")
    right = lax.ppermute(own, "tensor", [(0, 1), (1, 2), (2, 3)])
    left = lax.ppermute(own, "tensor", [(1, 0), (2, 1), (3, 2)])
    right2 = lax.ppermute(right, "tensor", [(1, 2), (2, 3)])
    left2 = lax.ppermute(left, "tensor", [(1, 0), (2, 1)])
    far = lax.ppermute(jnp.where(t == 1, right, left), "tensor", [(1, 3), (2, 0)])

    def pick(a, b, c, d):
        return jnp.where(t == 0, a, jnp.where(t == 1, b, jnp.where(t == 2, c, d)))

    return jnp.concatenate(
        [
            pick(own, right, right2, far),
            pick(left, own, right, right2),
            pick(left2, left, own, right),
            pick(far, left2, left, own),
        ],
        axis=0,
    )


def z_scatter(partial):
    count = lax.axis_size("tensor")
    if count != 4:
        return lax.psum_scatter(
            partial.astype(jnp.bfloat16), "tensor", scatter_dimension=0, tiled=True
        ).astype(jnp.float32)
    t = lax.axis_index("tensor")
    rows = partial.shape[0] // count
    parts = partial.reshape(count, rows, partial.shape[1])
    low = parts.astype(jnp.bfloat16)

    def take(source, index):
        return lax.dynamic_index_in_dim(source, jnp.clip(index, 0, count - 1), 0, keepdims=False)

    far = lax.ppermute(jnp.where(t == 3, low[0], low[3]), "tensor", [(3, 1), (0, 2)])
    left = lax.ppermute(take(low, t - 2), "tensor", [(3, 2), (2, 1)])
    right = lax.ppermute(take(low, t + 2), "tensor", [(0, 1), (1, 2)])
    wide = jnp.float32
    to_left = take(parts, t - 1) + left.astype(wide) + jnp.where(t == 1, far, 0).astype(wide)
    to_right = take(parts, t + 1) + right.astype(wide) + jnp.where(t == 2, far, 0).astype(wide)
    from_right = lax.ppermute(to_left.astype(jnp.bfloat16), "tensor", [(1, 0), (2, 1), (3, 2)])
    from_left = lax.ppermute(to_right.astype(jnp.bfloat16), "tensor", [(0, 1), (1, 2), (2, 3)])
    return take(parts, t) + from_right.astype(wide) + from_left.astype(wide)


def sum_over(values, axis):
    count = lax.axis_size(axis)
    if count & (count - 1):
        return lax.psum(values, axis)
    step = 1
    while step < count:
        values = values + lax.ppermute(values, axis, [(i, i ^ step) for i in range(count)])
        step *= 2
    return values


def gather_rows(local):
    return lax.all_gather(local, "dp", axis=0, tiled=True)


def scatter_rows(partial):
    return lax.psum_scatter(
        partial.astype(jnp.bfloat16), "dp", scatter_dimension=0, tiled=True
    ).astype(jnp.float32)


def shards(
    tokens,
    lengths,
    mixer_gain,
    query_weight,
    key_weight,
    value_weight,
    outgate_weight,
    alpha_weight,
    beta_weight,
    query_conv,
    key_conv,
    value_conv,
    log_rate,
    rate_bias,
    head_gain,
    output_weight,
    feed_gain,
    gate_weight,
    up_weight,
    down_weight,
    cotangent,
):
    tensor_index = lax.axis_index("tensor")
    tensor_count = lax.axis_size("tensor")
    micro_count, local_rows, width = tokens.shape
    pack_rows = local_rows * tensor_count
    key_width = query_weight.shape[1]
    value_width = value_weight.shape[1]
    head_count = alpha_weight.shape[1]
    hidden_width = gate_weight.shape[1]
    low = jnp.bfloat16

    edges = (key_width, 2 * key_width, 2 * key_width + value_width, 2 * key_width + 2 * value_width)
    pad = -(2 * head_count) % LANES
    in_local = jnp.concatenate(
        [
            query_weight,
            key_weight,
            value_weight,
            outgate_weight,
            alpha_weight,
            beta_weight,
            jnp.zeros((query_weight.shape[0], pad), low),
        ],
        axis=1,
    )
    in_full = gather_rows(in_local)
    out_full = gather_rows(output_weight.T)
    feed_full = gather_rows(jnp.concatenate([gate_weight, up_weight], axis=1))
    down_full = gather_rows(down_weight.T)

    small_local = (
        lax.dynamic_slice_in_dim(query_conv, tensor_index * key_width, key_width, 1),
        lax.dynamic_slice_in_dim(key_conv, tensor_index * key_width, key_width, 1),
        lax.dynamic_slice_in_dim(value_conv, tensor_index * value_width, value_width, 1),
        lax.dynamic_slice_in_dim(log_rate, tensor_index * head_count, head_count, 0),
        lax.dynamic_slice_in_dim(rate_bias, tensor_index * head_count, head_count, 0),
        head_gain,
    )
    packs = range(micro_count)
    wide = jnp.float32
    token_rows = [tokens[m].astype(wide) for m in packs]
    layouts = [layout(lengths[m, 0], pack_rows) for m in packs]
    own_masks = [
        lax.dynamic_slice_in_dim(row_mask, tensor_index * local_rows, local_rows, 0)[:, None]
        for _, _, row_mask in layouts
    ]
    out_grads = [cotangent[m].astype(wide) * own_masks[m] for m in packs]
    norm_ones = [jax.vjp(rms_rows, token_rows[m], mixer_gain) for m in packs]
    first_rows = [z_gather(norm_ones[m][0].astype(low)) for m in packs]
    grad_rows = [z_gather(out_grads[m].astype(low)) for m in packs]

    cores, gated, middle, norm_twos, second_rows = [], [], [], [], []
    for m in packs:
        raw = product(first_rows[m], in_full)
        raw_parts = (
            raw[:, : edges[0]],
            raw[:, edges[0] : edges[1]],
            raw[:, edges[1] : edges[2]],
            raw[:, edges[2] : edges[3]],
            raw[:, edges[3] : edges[3] + head_count],
            raw[:, edges[3] + head_count : edges[3] + 2 * head_count],
        )
        seq_start, keep_state, _ = layouts[m]

        def core_apply(raw_inputs, small_inputs, seq_start=seq_start, keep_state=keep_state):
            return mixer_core(raw_inputs, small_inputs, seq_start, keep_state)

        mixed, core_back = jax.vjp(core_apply, raw_parts, small_local)
        cores.append(core_back)
        gated.append(mixed.astype(low))
    for m in packs:
        middle.append(token_rows[m] + z_scatter(product_nt(gated[m], out_full)))
        norm_twos.append(jax.vjp(rms_rows, middle[m], feed_gain))
        second_rows.append(z_gather(norm_twos[m][0].astype(low)))

    outputs, hidden, feed_grads, middle_grads, mix_rows = [], [], [], [], []
    small_terms = []
    for m in packs:
        pre = product(second_rows[m], feed_full)
        gate_pre, up_pre = pre[:, :hidden_width], pre[:, hidden_width:]
        gate_sig = jax.nn.sigmoid(gate_pre)
        gate_act = gate_pre * gate_sig
        hidden.append((gate_act * up_pre).astype(low))
        hidden_grad = product(grad_rows[m], down_full)
        gate_grad = hidden_grad * up_pre * gate_sig * (1.0 + gate_pre * (1.0 - gate_sig))
        feed_grads.append(jnp.concatenate([gate_grad, hidden_grad * gate_act], axis=1).astype(low))
        second_grad = z_scatter(product_nt(feed_grads[m], feed_full))
        middle_norm_grad, feed_gain_grad = norm_twos[m][1](second_grad)
        middle_grads.append(out_grads[m] + middle_norm_grad)
        mix_rows.append(z_gather(middle_grads[m].astype(low)))
        result = middle[m] + z_scatter(product_nt(hidden[m], down_full))
        outputs.append((result * own_masks[m]).astype(low))
        small_terms.append([feed_gain_grad])
    joined = lambda parts: jnp.concatenate(parts, axis=0)
    feed_final = scatter_rows(product_tn(joined(second_rows), joined(feed_grads)))
    down_final = scatter_rows(product_tn(joined(grad_rows), joined(hidden)))
    out_final = scatter_rows(product_tn(joined(mix_rows), joined(gated)))

    raw_grads, input_grads = [], []
    for m in packs:
        parts, small_grads = cores[m](product(mix_rows[m], out_full))
        raw_grads.append(
            jnp.concatenate([*parts, jnp.zeros((pack_rows, pad), wide)], axis=1).astype(low)
        )
        first_grad = z_scatter(product_nt(raw_grads[m], in_full))
        token_norm_grad, mixer_gain_grad = norm_ones[m][1](first_grad)
        input_grads.append(middle_grads[m] + token_norm_grad)
        small_terms[m] += [mixer_gain_grad, *small_grads]
    in_final = scatter_rows(product_tn(joined(first_rows), joined(raw_grads)))

    feed_gain_grad, mixer_gain_grad, *core_grads = [sum(terms) for terms in zip(*small_terms)]
    conv_grads = jnp.concatenate(core_grads[:3], axis=1)
    rates = jnp.concatenate(core_grads[3:5])
    everywhere = jnp.concatenate([feed_gain_grad, mixer_gain_grad, core_grads[5]])
    per_slice = jnp.concatenate([conv_grads.reshape(-1), rates])
    packed = sum_over(jnp.concatenate([per_slice, everywhere]), "dp")
    slices = jnp.zeros((tensor_count, per_slice.size), wide)
    slices = lax.dynamic_update_index_in_dim(slices, packed[: per_slice.size], tensor_index, 0)
    packed = sum_over(jnp.concatenate([slices.reshape(-1), packed[per_slice.size :]]), "tensor")
    slices = packed[: slices.size].reshape(tensor_count, per_slice.size)
    taps = query_conv.shape[0]
    conv_all = slices[:, : conv_grads.size].reshape(tensor_count, taps, -1)

    def all_columns(begin, end):
        return jnp.moveaxis(conv_all[:, :, begin:end], 0, 1).reshape(taps, -1)

    rate_all = slices[:, conv_grads.size :]
    everywhere = packed[slices.size :]
    return (
        jnp.stack(outputs),
        jnp.stack(input_grads),
        everywhere[width : 2 * width],
        in_final[:, : edges[0]],
        in_final[:, edges[0] : edges[1]],
        in_final[:, edges[1] : edges[2]],
        in_final[:, edges[2] : edges[3]],
        in_final[:, edges[3] : edges[3] + head_count],
        in_final[:, edges[3] + head_count : edges[3] + 2 * head_count],
        all_columns(0, edges[0]),
        all_columns(edges[0], edges[1]),
        all_columns(edges[1], edges[2]),
        rate_all[:, :head_count].reshape(-1),
        rate_all[:, head_count:].reshape(-1),
        everywhere[2 * width :],
        out_final.T,
        everywhere[:width],
        feed_final[:, :hidden_width],
        feed_final[:, hidden_width:],
        down_final.T,
    )


def solution(mesh):
    return jax.shard_map(
        shards,
        mesh=mesh,
        in_specs=(
            P(None, ("dp", "tensor"), None),
            P(None, "dp", None),
            P(),
            P("dp", "tensor"),
            P("dp", "tensor"),
            P("dp", "tensor"),
            P("dp", "tensor"),
            P("dp", "tensor"),
            P("dp", "tensor"),
            P(),
            P(),
            P(),
            P(),
            P(),
            P(),
            P("tensor", "dp"),
            P(),
            P("dp", "tensor"),
            P("dp", "tensor"),
            P("tensor", "dp"),
            P(None, ("dp", "tensor"), None),
        ),
        out_specs=(
            P(None, ("dp", "tensor"), None),
            P(None, ("dp", "tensor"), None),
            P(),
            P("dp", "tensor"),
            P("dp", "tensor"),
            P("dp", "tensor"),
            P("dp", "tensor"),
            P("dp", "tensor"),
            P("dp", "tensor"),
            P(),
            P(),
            P(),
            P(),
            P(),
            P(),
            P("tensor", "dp"),
            P(),
            P("dp", "tensor"),
            P("dp", "tensor"),
            P("tensor", "dp"),
        ),
        check_vma=False,
    )
```

time: 3260 us -> 1890 us (0.58)
  waiting for transfers between devices: 1840 us -> 311 us
  starting transfers between devices: 1.51 us -> 204 us
  matrix products: 862 us -> 774 us
  other arithmetic: 231 us -> 273 us
    reduce_scatter x16 -> x4, waiting for transfers between devices: 885 us -> 0.01 us  [scatter_rows(): lax.psum_scatter(partial.astype(jnp.bfloat16), 'dp', scatter_dimension=0,...]
    all_gather x16 -> x4, waiting for transfers between devices: 637 us -> 0.01 us  [gather_rows(): return lax.all_gather(local, 'dp', axis=0, tiled=True)]
    ppermute x0 -> x85, waiting for transfers between devices: none -> 311 us  [the longest x8 67.6 us: z_gather(): left2 = lax.ppermute(left, 'tensor', [(1, 0), (2, 1)])]
    psum x2 -> x0, waiting for transfers between devices: 253 us -> none  [shards(): lax.psum((small_acc[0], place_cols(small_acc[1], query_conv, tensor_index...]
    ppermute x0 -> x85, starting transfers between devices: none -> 203 us  [the longest x8 52.7 us: z_gather(): right = lax.ppermute(own, 'tensor', [(0, 1), (1, 2), (2, 3)])]
    unnamed x22 -> x8, waiting for transfers between devices: 62.5 us -> 0.13 us
    while x576 -> x0, local copies, waits for them, and re-layouts: 58.5 us -> none
    unnamed x18 -> x37, other arithmetic: 0.03 us -> 53.3 us
  transfers between devices with their start and end apart: 36 -> 93, of which waited for: 36 -> 47; matrix products, arithmetic and copies ran while one was open for 6% -> 67% of each run, Pallas kernels for 0% -> 0%
where the time goes in v1:
time: 1890 us; the launch traced here: 1870 us
  matrix products  774 us (41%)
  waiting for transfers between devices  311 us (16%)
  local copies, waits for them, and re-layouts  277 us (15%)
  other arithmetic  273 us (14%)
  starting transfers between devices  204 us (11%)
  between operations  20.9 us (1%)
    dot_general x320, matrix products, unit_inverse(): jnp.einsum('hts,hsu->htu', inverse, power_term, precision=precise)  104 us
    dot_general x64, matrix products, stretch_step(): jnp.einsum('htd,hde->hte', query_block, carry_state, precision=precise)  94.5 us
    dot_general x256, matrix products, unit_inverse(): jnp.einsum('hts,hsu->htu', power_term, power_term, precision=precise)  80 us
    dot_general x8, matrix products, product(): return jnp.dot(left_rows, matrix, preferred_element_type=jnp.float32)  77.3 us
    dot_general x64, matrix products, stretch_step(): jnp.einsum('htd,hde->hte', key_part, carry_state, precision=precise)  76.9 us
    ppermute x8, waiting for transfers between devices, z_gather(): left2 = lax.ppermute(left, 'tensor', [(1, 0), (2, 1)])  67.6 us
    ppermute x8, waiting for transfers between devices, z_scatter(): right = lax.ppermute(take(low, t + 2), 'tensor', [(0, 1), (1, 2)])  66.1 us
    squeeze x64, local copies, waits for them, and re-layouts, delta_rule(): lax.scan(jax.checkpoint(stretch_step), first_state, inputs)  62.3 us
  transfers between devices with their start and end apart: 93, of which 47 were waited for; matrix products, arithmetic and copies ran while one was open for 67% of the time, Pallas kernels for 0%

profile of v1, /device:TPU:0, one launch (start us, length us, event | category | flops | bytes accessed | tf_op | source)
XLA Modules:
  0.0 1870.6 jit_solution(11723046324336985886)
XLA Ops:
  78.6 8.6 collective-permute-done.3
  92.2 26.3 %collective-permute-done.4 = bf16[128,2048]{1,0:T(8,128)(2,1)S(1)} collective-permute-done((bf16[128,2048]{1,0:T(8,128)(2,1)}, bf16[128,2048]{1,0:T(8,128)(2,1)S(1)}, u32[]{:S(2)}, u32[]{:S(2)}) %collective-permute-start.4) | collective-permute-done | bytes 524320 | tf_op jit(solution)/shard_map/ppermute | solution.py:176
  133.5 11.8 fusion.323
  166.8 11.1 fusion.339
  227.3 9.4 fusion.391
  247.5 124.7 %while.88 = (s32[]{:T(128)}, f32[4,128,256]{2,1,0:T(8,128)S(1)}, f32[8,4,64,256]{3,2,1,0:T(8,128)S(1)}, f32[8,4,128,256]{3,2,1,0:T(8,128)}, f32[8,4,64]{2,1,0:T(...) while((s32[]{:T(128)}, f32[4,128,256]{2,1,0:T(8,128)S(1)}, ...), condition=%wide.region_4.6_spmd.clone.clone, body=%wide.region_3.5_spmd.clone.clone.sunk | while | flops 606061056 | bytes 9389342 | solution.py:117
  414.0 124.6 %while.89 = (s32[]{:T(128)}, f32[4,128,256]{2,1,0:T(8,128)S(1)}, f32[8,4,64,256]{3,2,1,0:T(8,128)S(1)}, f32[8,4,128,256]{3,2,1,0:T(8,128)}, f32[8,4,64]{2,1,0:T(...) while((s32[]{:T(128)}, f32[4,128,256]{2,1,0:T(8,128)S(1)}, ...), condition=%wide.region_11.13_spmd.clone.clone, body=%wide.region_10.12_spmd.clone.clone.sunk | while | flops 606061056 | bytes 9389342 | solution.py:117
  566.2 11.2 collective-permute-done.28
  602.0 10.3 collective-permute-start.10
  634.2 13.7 collective-permute-done.13
  661.3 11.6 fusion.331
  672.9 10.5 multiply_convert_fusion.3
  733.2 11.2 collective-permute-done.18
  755.7 9.7 collective-permute-done.19
  767.5 12.5 collective-permute-start.30
  799.5 13.1 collective-permute-done.33
  823.2 11.1 fusion.347
  834.3 9.5 multiply_convert_fusion.1
  845.3 9.0 fusion.296
  875.2 9.1 collective-permute-done.68
  895.6 11.2 collective-permute-done.38
  965.0 9.0 collective-permute-done.53
  976.3 18.9 %collective-permute-done.54 = bf16[128,2048]{1,0:T(8,128)(2,1)S(1)} collective-permute-done((bf16[128,2048]{1,0:T(8,128)(2,1)S(1)}, bf16[128,2048]{1,0:T(8,128)(2,1)S(1)}, u32[]{:S(2)}, u32[]{:S(2)}) %collective-permute-start.54) | collective-permute-done | bytes 524320 | tf_op jit(solution)/shard_map/ppermute | solution.py:176
  1017.3 10.9 convolution_convert_fusion.2
  1042.4 17.9 convolution_convert_fusion.1
  1090.5 261.6 %while.87 = (s32[]{:T(128)}, f32[4,128,256]{2,1,0:T(8,128)S(1)}, f32[8,4,64,128]{3,2,1,0:T(8,128)}, f32[8,4,64,128]{3,2,1,0:T(8,128)}, f32[8,4,64,256]{3,2,1,0:T...) while((s32[]{:T(128)}, f32[4,128,256]{2,1,0:T(8,128)S(1)}, ...), condition=%wide.region_42.44_spmd.clone, body=%wide.region_32.43_spmd.clone.sunk | while | flops 1666034176 | bytes 28601848 | solution.py:117
  1359.5 261.1 %while.86 = (s32[]{:T(128)}, f32[4,128,256]{2,1,0:T(8,128)S(1)}, f32[8,4,64,128]{3,2,1,0:T(8,128)}, f32[8,4,64,128]{3,2,1,0:T(8,128)}, f32[8,4,64,256]{3,2,1,0:T...) while((s32[]{:T(128)}, f32[4,128,256]{2,1,0:T(8,128)S(1)}, ...), condition=%wide.region_26.28_spmd.clone, body=%wide.region_16.27_spmd.clone.sunk | while | flops 1666034176 | bytes 28601848 | solution.py:117
  1711.9 21.3 %convolution_convert_fusion = bf16[2048,3200]{1,0:T(8,128)(2,1)} fusion(bf16[1024,2048]{1,0:T(8,128)(2,1)} %get-tuple-element.1798, bf16[512,3200]{1,0:T(8,128)(2,1)} %concatenate.198, bf16[512,3200]{1,0:T(8,128)(2,1)} %concatenate.194), kind=kOutput, calls=%fused_computation.432 | convolution fusion | flops 13441433600 | bytes 23855104 | tf_op jit(solution)/shard_map/dot_general | solution.py:25
  1735.1 11.3 fusion.622
  1753.3 10.5 fusion.623
  1786.8 11.2 collective-permute-done.78
  1809.3 8.5 collective-permute-done.79
  (2532 shorter events, 1499.0 us)
Async XLA Ops:
  7.2 126.3 %all-gather.5.cloned.1.call-start = ((), (), s32[]{:S(2)}) async-start(), calls=%async_computation.4 | async-start | bytes 14745600 | tf_op jit(solution)/shard_map/all_gather | solution.py:230
  12.8 368.5 %all-gather.7.cloned.1.call-start = ((), (), s32[]{:S(2)}) async-start(), calls=%async_computation.5 | async-start | bytes 4718592 | tf_op jit(solution)/shard_map/all_gather | solution.py:230
  13.9 647.4 %all-gather.9.cloned.1.call-start = ((), (), s32[]{:S(2)}) async-start(), calls=%async_computation.6 | async-start | bytes 12976128 | tf_op jit(solution)/shard_map/all_gather | solution.py:230
  15.5 657.4 %all-gather.11.cloned.1.call-start = ((), (), s32[]{:S(2)}) async-start(), calls=%async_computation.7 | async-start | bytes 6488064 | tf_op jit(solution)/shard_map/all_gather | solution.py:230
  16.7 31.4 %collective-permute-start = (bf16[128,2048]{1,0:T(8,128)(2,1)S(1)}, bf16[128,2048]{1,0:T(8,128)(2,1)}, u32[]{:S(2)}, u32[]{:S(2)}) collective-permute-start(bf16[128,2048]{1,0:T(8,128)(2,1)S(1)} %get-tuple-element.1981), channel_id=1, source_target_pairs={{0,1},{1,2},{2,3},{4,5},{5,6},{6,7},{8,9},{9,10},{10,11},{12,13},{... | collective-permute-start | bytes 1572872 | tf_op jit(solution)/shard_map/ppermute | solution.py:173
  23.7 31.4 %collective-permute-start.20 = (bf16[128,2048]{1,0:T(8,128)(2,1)S(1)}, bf16[128,2048]{1,0:T(8,128)(2,1)}, u32[]{:S(2)}, u32[]{:S(2)}) collective-permute-start(bf16[128,2048]{1,0:T(8,128)(2,1)S(1)} %get-tuple-element.1980), channel_id=1, source_target_pairs={{0,1},{1,2},{2,3},{4,5},{5,6},{6,7},{8,9},{9,10},{10,11},{12,13},{... | collective-permute-start | bytes 1572872 | tf_op jit(solution)/shard_map/ppermute | solution.py:173
  42.0 1807.1 %reduce-scatter.7.cloned.1.call-start = ((), (), s32[]{:S(2)}) async-start(), calls=%async_computation.9 | async-start | bytes 4718592 | tf_op jit(solution)/shard_map/reduce_scatter | solution.py:234
  58.9 64.9 %collective-permute-start.23 = (bf16[128,2048]{1,0:T(8,128)(2,1)S(1)}, bf16[128,2048]{1,0:T(8,128)(2,1)S(1)}, u32[]{:S(2)}, u32[]{:S(2)}) collective-permute-start(bf16[128,2048]{1,0:T(8,128)(2,1)S(1)} %broadcast_select_fusion.7), channel_id=1, source_target_pairs={{1,3},{2,0},{5,7},{6,4},{9,11},{10,8},{13,15},{14,12},{17,19},{18,... | collective-permute-start | bytes 1572872 | tf_op jit(solution)/shard_map/ppermute | solution.py:177
  66.5 483.6 %collective-permute-start.43 = (bf16[128,2048]{1,0:T(8,128)(2,1)}, bf16[128,2048]{1,0:T(8,128)(2,1)}, u32[]{:S(2)}, u32[]{:S(2)}) collective-permute-start(bf16[128,2048]{1,0:T(8,128)(2,1)} %broadcast_select_fusion.5), channel_id=1, source_target_pairs={{1,3},{2,0},{5,7},{6,4},{9,11},{10,8},{13,15},{14,12},{17,19},{18,... | collective-permute-start | bytes 1572872 | tf_op jit(solution)/shard_map/ppermute | solution.py:177
  75.7 42.9 %collective-permute-start.4 = (bf16[128,2048]{1,0:T(8,128)(2,1)}, bf16[128,2048]{1,0:T(8,128)(2,1)S(1)}, u32[]{:S(2)}, u32[]{:S(2)}) collective-permute-start(bf16[128,2048]{1,0:T(8,128)(2,1)} %collective-permute-done.2), channel_id=1, source_target_pairs={{1,0},{2,1},{5,4},{6,5},{9,8},{10,9},{13,12},{14,13},{17,16},{18,1... | collective-permute-start | bytes 1572872 | tf_op jit(solution)/shard_map/ppermute | solution.py:176
  77.9 46.0 %collective-permute-start.21 = (bf16[128,2048]{1,0:T(8,128)(2,1)}, bf16[128,2048]{1,0:T(8,128)(2,1)S(1)}, u32[]{:S(2)}, u32[]{:S(2)}) collective-permute-start(bf16[128,2048]{1,0:T(8,128)(2,1)} %collective-permute-done.20), channel_id=1, source_target_pairs={{1,2},{2,3},{5,6},{6,7},{9,10},{10,11},{13,14},{14,15},{17,18},{18... | collective-permute-start | bytes 1572872 | tf_op jit(solution)/shard_map/ppermute | solution.py:175
  87.2 42.5 %collective-permute-start.24 = (bf16[128,2048]{1,0:T(8,128)(2,1)}, bf16[128,2048]{1,0:T(8,128)(2,1)S(1)}, u32[]{:S(2)}, u32[]{:S(2)}) collective-permute-start(bf16[128,2048]{1,0:T(8,128)(2,1)} %collective-permute-done.22), channel_id=1, source_target_pairs={{1,0},{2,1},{5,4},{6,5},{9,8},{10,9},{13,12},{14,13},{17,16},{18,1... | collective-permute-start | bytes 1572872 | tf_op jit(solution)/shard_map/ppermute | solution.py:176
  118.6 430.7 %collective-permute-start.41 = (bf16[128,2048]{1,0:T(8,128)(2,1)}, bf16[128,2048]{1,0:T(8,128)(2,1)}, u32[]{:S(2)}, u32[]{:S(2)}) collective-permute-start(bf16[128,2048]{1,0:T(8,128)(2,1)} %collective-permute-done.40), channel_id=1, source_target_pairs={{1,2},{2,3},{5,6},{6,7},{9,10},{10,11},{13,14},{14,15},{17,18},{18... | collective-permute-start | bytes 1572872 | tf_op jit(solution)/shard_map/ppermute | solution.py:175
  389.3 164.5 %collective-permute-start.5 = (bf16[128,2048]{1,0:T(8,128)(2,1)}, bf16[128,2048]{1,0:T(8,128)(2,1)}, u32[]{:S(2)}, u32[]{:S(2)}) collective-permute-start(bf16[128,2048]{1,0:T(8,128)(2,1)} %get-tuple-element.1962), channel_id=1, source_target_pairs={{3,2},{2,1},{7,6},{6,5},{11,10},{10,9},{15,14},{14,13},{19,18},{18... | collective-permute-start | bytes 1572872 | tf_op jit(solution)/shard_map/ppermute | solution.py:208
  390.9 166.5 %collective-permute-start.6 = (bf16[128,2048]{1,0:T(8,128)(2,1)}, bf16[128,2048]{1,0:T(8,128)(2,1)}, u32[]{:S(2)}, u32[]{:S(2)}) collective-permute-start(bf16[128,2048]{1,0:T(8,128)(2,1)} %get-tuple-element.1963), channel_id=1, source_target_pairs={{3,1},{0,2},{7,5},{4,6},{11,9},{8,10},{15,13},{12,14},{19,17},{16,... | collective-permute-start | bytes 1572872 | tf_op jit(solution)/shard_map/ppermute | solution.py:207
  397.4 161.3 %collective-permute-start.8 = (bf16[128,2048]{1,0:T(8,128)(2,1)}, bf16[128,2048]{1,0:T(8,128)(2,1)}, u32[]{:S(2)}, u32[]{:S(2)}) collective-permute-start(bf16[128,2048]{1,0:T(8,128)(2,1)} %get-tuple-element.1964), channel_id=1, source_target_pairs={{0,1},{1,2},{4,5},{5,6},{8,9},{9,10},{12,13},{13,14},{16,17},{17,1... | collective-permute-start | bytes 1572872 | tf_op jit(solution)/shard_map/ppermute | solution.py:209
  557.4 147.4 %collective-permute-start.63 = (bf16[128,2048]{1,0:T(8,128)(2,1)}, bf16[128,2048]{1,0:T(8,128)(2,1)S(1)}, u32[]{:S(2)}, u32[]{:S(2)}) collective-permute-start(bf16[128,2048]{1,0:T(8,128)(2,1)} %broadcast_select_fusion.3), channel_id=1, source_target_pairs={{1,3},{2,0},{5,7},{6,4},{9,11},{10,8},{13,15},{14,12},{17,19},{18,... | collective-permute-start | bytes 1572872 | tf_op jit(solution)/shard_map/ppermute | solution.py:177
  563.4 31.6 %collective-permute-start.7 = (bf16[128,2048]{1,0:T(8,128)(2,1)S(1)}, bf16[128,2048]{1,0:T(8,128)(2,1)S(1)}, u32[]{:S(2)}, u32[]{:S(2)}) collective-permute-start(bf16[128,2048]{1,0:T(8,128)(2,1)S(1)} %get-tuple-element.1940), channel_id=1, source_target_pairs={{1,0},{2,1},{3,2},{5,4},{6,5},{7,6},{9,8},{10,9},{11,10},{13,12},{... | collective-permute-start | bytes 1572872 | tf_op jit(solution)/shard_map/ppermute | solution.py:213
  594.9 109.0 %collective-permute-start.61 = (bf16[128,2048]{1,0:T(8,128)(2,1)S(1)}, bf16[128,2048]{1,0:T(8,128)(2,1)}, u32[]{:S(2)}, u32[]{:S(2)}) collective-permute-start(bf16[128,2048]{1,0:T(8,128)(2,1)S(1)} %copy-done.63), channel_id=1, source_target_pairs={{1,2},{2,3},{5,6},{6,7},{9,10},{10,11},{13,14},{14,15},{17,18},{18... | collective-permute-start | bytes 1572872 | tf_op jit(solution)/shard_map/ppermute | solution.py:175
  709.9 34.5 %collective-permute-start.18 = (bf16[128,2048]{1,0:T(8,128)(2,1)S(1)}, bf16[128,2048]{1,0:T(8,128)(2,1)S(1)}, u32[]{:S(2)}, u32[]{:S(2)}) collective-permute-start(bf16[128,2048]{1,0:T(8,128)(2,1)S(1)} %get-tuple-element.1958), channel_id=1, source_target_pairs={{0,1},{1,2},{4,5},{5,6},{8,9},{9,10},{12,13},{13,14},{16,17},{17,1... | collective-permute-start | bytes 1572872 | tf_op jit(solution)/shard_map/ppermute | solution.py:209
  712.4 68.9 %collective-permute-start.64 = (bf16[128,2048]{1,0:T(8,128)(2,1)S(1)}, bf16[128,2048]{1,0:T(8,128)(2,1)S(1)}, u32[]{:S(2)}, u32[]{:S(2)}) collective-permute-start(bf16[128,2048]{1,0:T(8,128)(2,1)S(1)} %copy-done.61), channel_id=1, source_target_pairs={{1,0},{2,1},{5,4},{6,5},{9,8},{10,9},{13,12},{14,13},{17,16},{18,1... | collective-permute-start | bytes 1572872 | tf_op jit(solution)/shard_map/ppermute | solution.py:176
  722.3 33.3 %collective-permute-start.49 = (bf16[128,2048]{1,0:T(8,128)(2,1)S(1)}, bf16[128,2048]{1,0:T(8,128)(2,1)S(1)}, u32[]{:S(2)}, u32[]{:S(2)}) collective-permute-start(bf16[128,2048]{1,0:T(8,128)(2,1)S(1)} %get-tuple-element.1933), channel_id=1, source_target_pairs={{0,1},{1,2},{2,3},{4,5},{5,6},{6,7},{8,9},{9,10},{10,11},{12,13},{... | collective-permute-start | bytes 1572872 | tf_op jit(solution)/shard_map/ppermute | solution.py:214
  873.9 32.9 %collective-permute-start.38 = (bf16[128,2048]{1,0:T(8,128)(2,1)S(1)}, bf16[128,2048]{1,0:T(8,128)(2,1)S(1)}, u32[]{:S(2)}, u32[]{:S(2)}) collective-permute-start(bf16[128,2048]{1,0:T(8,128)(2,1)S(1)} %get-tuple-element.1961), channel_id=1, source_target_pairs={{0,1},{1,2},{4,5},{5,6},{8,9},{9,10},{12,13},{13,14},{16,17},{17,1... | collective-permute-start | bytes 1572872 | tf_op jit(solution)/shard_map/ppermute | solution.py:209
  884.7 33.3 %collective-permute-start.69 = (bf16[128,2048]{1,0:T(8,128)(2,1)S(1)}, bf16[128,2048]{1,0:T(8,128)(2,1)S(1)}, u32[]{:S(2)}, u32[]{:S(2)}) collective-permute-start(bf16[128,2048]{1,0:T(8,128)(2,1)S(1)} %get-tuple-element.1935), channel_id=1, source_target_pairs={{0,1},{1,2},{2,3},{4,5},{5,6},{6,7},{8,9},{9,10},{10,11},{12,13},{... | collective-permute-start | bytes 1572872 | tf_op jit(solution)/shard_map/ppermute | solution.py:214
  960.3 37.2 %collective-permute-start.73 = (bf16[128,2048]{1,0:T(8,128)(2,1)S(1)}, bf16[128,2048]{1,0:T(8,128)(2,1)S(1)}, u32[]{:S(2)}, u32[]{:S(2)}) collective-permute-start(bf16[128,2048]{1,0:T(8,128)(2,1)S(1)} %broadcast_select_fusion.2), channel_id=1, source_target_pairs={{1,3},{2,0},{5,7},{6,4},{9,11},{10,8},{13,15},{14,12},{17,19},{18,... | collective-permute-start | bytes 1572872 | tf_op jit(solution)/shard_map/ppermute | solution.py:177
  961.6 33.5 %collective-permute-start.54 = (bf16[128,2048]{1,0:T(8,128)(2,1)S(1)}, bf16[128,2048]{1,0:T(8,128)(2,1)S(1)}, u32[]{:S(2)}, u32[]{:S(2)}) collective-permute-start(bf16[128,2048]{1,0:T(8,128)(2,1)S(1)} %collective-permute-done.52), channel_id=1, source_target_pairs={{1,0},{2,1},{5,4},{6,5},{9,8},{10,9},{13,12},{14,13},{17,16},{18,1... | collective-permute-start | bytes 1572872 | tf_op jit(solution)/shard_map/ppermute | solution.py:176
  962.9 34.6 %collective-permute-start.71 = (bf16[128,2048]{1,0:T(8,128)(2,1)S(1)}, bf16[128,2048]{1,0:T(8,128)(2,1)S(1)}, u32[]{:S(2)}, u32[]{:S(2)}) collective-permute-start(bf16[128,2048]{1,0:T(8,128)(2,1)S(1)} %collective-permute-done.70), channel_id=1, source_target_pairs={{1,2},{2,3},{5,6},{6,7},{9,10},{10,11},{13,14},{14,15},{17,18},{18... | collective-permute-start | bytes 1572872 | tf_op jit(solution)/shard_map/ppermute | solution.py:175
  963.7 42.7 %collective-permute-start.74 = (bf16[128,2048]{1,0:T(8,128)(2,1)S(1)}, bf16[128,2048]{1,0:T(8,128)(2,1)S(1)}, u32[]{:S(2)}, u32[]{:S(2)}) collective-permute-start(bf16[128,2048]{1,0:T(8,128)(2,1)S(1)} %collective-permute-done.72), channel_id=1, source_target_pairs={{1,0},{2,1},{5,4},{6,5},{9,8},{10,9},{13,12},{14,13},{17,16},{18,1... | collective-permute-start | bytes 1572872 | tf_op jit(solution)/shard_map/ppermute | solution.py:176
  1015.5 836.0 %reduce-scatter.11.cloned.1.call-start = ((), (), s32[]{:S(2)}) async-start(), calls=%async_computation.11 | async-start | bytes 6488064 | tf_op jit(solution)/shard_map/reduce_scatter | solution.py:234
  1028.2 826.1 %reduce-scatter.9.cloned.1.call-start = ((), (), s32[]{:S(2)}) async-start(), calls=%async_computation.10 | async-start | bytes 12976128 | tf_op jit(solution)/shard_map/reduce_scatter | solution.py:234
  1060.3 797.0 %reduce-scatter.5.cloned.1.call-start = ((), (), s32[]{:S(2)}) async-start(), calls=%async_computation.8 | async-start | bytes 14745600 | tf_op jit(solution)/shard_map/reduce_scatter | solution.py:234
  1775.9 33.3 %collective-permute-start.59 = (bf16[128,2048]{1,0:T(8,128)(2,1)S(1)}, bf16[128,2048]{1,0:T(8,128)(2,1)S(1)}, u32[]{:S(2)}, u32[]{:S(2)}) collective-permute-start(bf16[128,2048]{1,0:T(8,128)(2,1)S(1)} %get-tuple-element.1931), channel_id=1, source_target_pairs={{0,1},{1,2},{2,3},{4,5},{5,6},{6,7},{8,9},{9,10},{10,11},{12,13},{... | collective-permute-start | bytes 1572872 | tf_op jit(solution)/shard_map/ppermute | solution.py:214
  (290 other events, 5726.8 us)
Sparse Core Ops, SparseCore 0:
  12.9 77.0 all-gather.4
  91.9 36.6 all-gather.6
  131.1 67.6 all-gather.8
  200.6 44.3 all-gather.10
  1015.7 49.7 reduce-scatter.6
  1069.1 59.0 reduce-scatter.10
  1131.8 86.8 reduce-scatter.8
  1733.3 94.4 reduce-scatter.4

commit v2 on v1

--- a/solution.py
+++ b/solution.py
@@ -1,149 +1,376 @@
+import functools
 import jax
 import jax.numpy as jnp
 from jax import lax
+from jax.experimental import pallas as pl
+from jax.experimental.pallas import tpu as pltpu
 from jax.sharding import PartitionSpec as P
 
 DK = 128
 DV = 256
 STRETCH = 64
-
-
-precise = lax.Precision.HIGHEST
+LANES = 128
+HALO = 8
+F32 = jnp.float32
+LOW = jnp.bfloat16
+
+NN = (((1,), (0,)), ((), ()))
+NT = (((1,), (1,)), ((), ()))
+TN = (((0,), (0,)), ((), ()))
+
+
+def split(a):
+    hi = a.astype(LOW)
+    return hi, (a - hi.astype(F32)).astype(LOW)
+
+
+def mm(a, b, dims=NN, passes=1):
+    if passes == 6:
+        return lax.dot_general(a, b, dims, precision=lax.Precision.HIGHEST, preferred_element_type=F32)
+    dot = functools.partial(lax.dot_general, dimension_numbers=dims, preferred_element_type=F32)
+    if passes == 1:
+        return dot(a.astype(LOW), b.astype(LOW))
+    ah, al = split(a)
+    bh, bl = split(b)
+    return dot(ah, bh) + (dot(ah, bl) + dot(al, bh))
+
+
+def block_masks():
+    row = lax.broadcasted_iota(jnp.int32, (STRETCH, STRETCH), 0)
+    col = lax.broadcasted_iota(jnp.int32, (STRETCH, STRETCH), 1)
+    return row, col
+
+
+def sigmoid(v):
+    return 1.0 / (1.0 + jnp.exp(-v))
+
+
+def softplus(v):
+    return jnp.maximum(v, 0.0) + jnp.log1p(jnp.exp(-jnp.abs(v)))
+
+
+def unit_inverses(lowers, passes):
+    row, col = block_masks()
+    eye = jnp.where(row == col, 1.0, 0.0)
+    pair = (row // 2 == col // 2) & (row > col)
+    inverses = [eye - jnp.where(pair, lower, 0.0) for lower in lowers]
+    size = 2
+    while size < STRETCH:
+        off = (row // (2 * size) == col // (2 * size)) & (row // size > col // size)
+        offs = [jnp.where(off, lower, 0.0) for lower in lowers]
+        halves = [mm(inv, o, NN, passes) for inv, o in zip(inverses, offs)]
+        inverses = [inv - mm(h, inv, NN, passes) for inv, h in zip(inverses, halves)]
+        size *= 2
+    return inverses
+
+
+def decay_parts(mixed, rates, heads):
+    lane = lax.broadcasted_iota(jnp.int32, (STRETCH, LANES), 1)
+    row, col = block_masks()
+    soft_in = mixed + rates[1:2, :]
+    decay = jnp.where(lane < heads, -jnp.exp(rates[0:1, :]) * softplus(soft_in), 0.0)
+    tri = jnp.where(row >= col, 1.0, 0.0)
+    upper = jnp.where(row <= col, 1.0, 0.0)
+    sum_col = mm(tri, decay, NN, 6)
+    sum_row = mm(decay[:, :HALO], upper, TN, 6)
+    return decay, soft_in, sum_col, sum_row
+
+
+def forward_kernel(heads, keep_ref, raw_ref, conv_ref, rates_ref, gain_ref,
+                   gated_ref, conved_ref, fresh_ref, out_ref, inv_ref, start_ref, state, ext):
+    n = pl.program_id(0)
+    keep = keep_ref[n].astype(F32)
+    kw, vw = heads * DK, heads * DV
+    qkv = 2 * kw + vw
+    span = STRETCH
+
+    @pl.when(n == 0)
+    def _():
+        state[...] = jnp.zeros_like(state)
+        ext[...] = jnp.zeros_like(ext)
+
+    ext[0:HALO, :] = ext[span:span + HALO, :] * keep
+    ext[HALO:HALO + span, :] = raw_ref[:, :qkv]
+
+    def conv(begin, width):
+        total = ext[HALO:HALO + span, begin:begin + width] * conv_ref[0:1, begin:begin + width]
+        for j in range(1, 4):
+            total = total + ext[HALO - j:HALO - j + span, begin:begin + width] * conv_ref[j:j + 1, begin:begin + width]
+        conved_ref[:, begin:begin + width] = total
+        return total * sigmoid(total)
+
+    mixed = raw_ref[:, qkv + vw:]
+    decay, _, sum_col, sum_row = decay_parts(mixed, rates_ref[...], heads)
+    beta_all = sigmoid(mixed)
+    row, col = block_masks()
+    incl, strict = row >= col, row > col
+    qs, ks, lowers, scores, betas = [], [], [], [], []
+    for h in range(heads):
+        zq = conv(h * DK, DK)
+        zk = conv(kw + h * DK, DK)
+        q = zq * lax.rsqrt(jnp.sum(zq * zq, axis=-1, keepdims=True) + 1e-6) * DK ** -0.5
+        k = zk * lax.rsqrt(jnp.sum(zk * zk, axis=-1, keepdims=True) + 1e-6)
+        within = jnp.exp(jnp.where(incl, sum_col[:, h:h + 1] - sum_row[h:h + 1, :], -1e30))
+        beta = beta_all[:, heads + h:heads + h + 1]
+        scores.append(mm(q, k, NT, 3) * within)
+        lowers.append(jnp.where(strict, beta * mm(k, k, NT, 3) * within, 0.0))
+        qs.append(q); ks.append(k); betas.append(beta)
+    inverses = unit_inverses(lowers, 3)
+    for h in range(heads):
+        q, k, beta = qs[h], ks[h], betas[h]
+        start = state[h] * keep
+        total = sum_col[:, h:h + 1]
+        growth = jnp.exp(total)
+        last = total[span - 1:span, :]
+        v = conv(2 * kw + h * DV, DV)
+        k_state = mm(k, start, NN, 3)
+        q_state = mm(q, start, NN, 3)
+        fresh = mm(inverses[h], beta * (v - growth * k_state), NN, 3)
+        out = growth * q_state + mm(scores[h], fresh, NN, 3)
+        tail = jnp.exp(last - total)
+        state[h] = jnp.exp(last) * start + mm(k * tail, fresh, TN, 3)
+        cols = slice(h * DV, (h + 1) * DV)
+        fresh_ref[:, cols] = fresh.astype(fresh_ref.dtype)
+        out_ref[:, cols] = out
+        inv_ref[0, h] = inverses[h].astype(inv_ref.dtype)
+        start_ref[0, h] = start.astype(start_ref.dtype)
+        gate = raw_ref[:, qkv + h * DV:qkv + (h + 1) * DV]
+        normed = out * lax.rsqrt(jnp.mean(out * out, axis=-1, keepdims=True) + 1e-5) * gain_ref[...]
+        gated_ref[:, cols] = (normed * (gate * sigmoid(gate))).astype(LOW)
+
+
+def mixer_forward(raw, keep, conv, rates, gain, heads):
+    rows, width = raw.shape
+    count = rows // STRETCH
+    kw, vw = heads * DK, heads * DV
+    qkv = 2 * kw + vw
+    at = lambda n, keep_ref: (n, 0)
+    fixed = lambda n, keep_ref: (0, 0)
+    at4 = lambda n, keep_ref: (n, 0, 0, 0)
+    spec = pl.BlockSpec
+    return pl.pallas_call(
+        functools.partial(forward_kernel, heads),
+        grid_spec=pltpu.PrefetchScalarGridSpec(
+            num_scalar_prefetch=1,
+            grid=(count,),
+            in_specs=[spec((STRETCH, width), at), spec((4, qkv), fixed), spec((HALO, LANES), fixed), spec((1, DV), fixed)],
+            out_specs=[
+                spec((STRETCH, vw), at),
+                spec((STRETCH, qkv), at),
+                spec((STRETCH, vw), at),
+                spec((STRETCH, vw), at),
+                spec((1, heads, STRETCH, STRETCH), at4),
+                spec((1, heads, DK, DV), at4),
+            ],
+            scratch_shapes=[pltpu.VMEM((heads, DK, DV), F32), pltpu.VMEM((STRETCH + HALO, qkv), F32)],
+        ),
+        out_shape=[
+            jax.ShapeDtypeStruct((rows, vw), LOW),
+            jax.ShapeDtypeStruct((rows, qkv), F32),
+            jax.ShapeDtypeStruct((rows, vw), F32),
+            jax.ShapeDtypeStruct((rows, vw), F32),
+            jax.ShapeDtypeStruct((count, heads, STRETCH, STRETCH), F32),
+            jax.ShapeDtypeStruct((count, heads, DK, DV), F32),
+        ],
+        compiler_params=pltpu.CompilerParams(dimension_semantics=("arbitrary",), vmem_limit_bytes=32 << 20),
+        cost_estimate=pl.CostEstimate(flops=3 * 10**10, bytes_accessed=30 << 20, transcendentals=0),
+        name="mixer_forward",
+    )(keep, raw, conv, rates, gain)
+
+
+def backward_kernel(heads, keep_ref, raw_ref, conved_ref, fresh_ref, out_ref, inv_ref, start_ref, grad_ref,
+                    conv_ref, rates_ref, gain_ref,
+                    draw_ref, dconv_ref, drates_ref, dgain_ref, dstate, ext):
+    i = pl.program_id(0)
+    count = pl.num_programs(0)
+    n = count - 1 - i
+    keep_next = keep_ref[n + 1].astype(F32)
+    kw, vw = heads * DK, heads * DV
+    qkv = 2 * kw + vw
+    span = STRETCH
+
+    @pl.when(i == 0)
+    def _():
+        dstate[...] = jnp.zeros_like(dstate)
+        ext[...] = jnp.zeros_like(ext)
+        dconv_ref[...] = jnp.zeros_like(dconv_ref)
+        drates_ref[...] = jnp.zeros_like(drates_ref)
+        dgain_ref[...] = jnp.zeros_like(dgain_ref)
+
+    ext[span:span + HALO, :] = ext[0:HALO, :] * keep_next
+    rates = rates_ref[...]
+    mixed = raw_ref[:, qkv + vw:]
+    decay, soft_in, sum_col, sum_row = decay_parts(mixed, rates, heads)
+    beta_all = sigmoid(mixed)
+    row, col = block_masks()
+    incl, strict = row >= col, row > col
+    lane = lax.broadcasted_iota(jnp.int32, (span, LANES), 1)
+    last_row = lax.broadcasted_iota(jnp.int32, (span, 1), 0) == span - 1
+    gain = gain_ref[...]
+    dgain = jnp.zeros((1, DV), F32)
+    dsum_all = jnp.zeros((span, LANES), F32)
+    dbeta_all = jnp.zeros((span, LANES), F32)
+    down_rows = []
+
+    def act(begin, width):
+        c = conved_ref[:, begin:begin + width]
+        s = sigmoid(c)
+        return c * s, s * (1.0 + c * (1.0 - s))
+
+    for h in range(heads):
+        cols = slice(h * DV, (h + 1) * DV)
+        zq, slope_q = act(h * DK, DK)
+        zk, slope_k = act(kw + h * DK, DK)
+        v, slope_v = act(2 * kw + h * DV, DV)
+        rq = lax.rsqrt(jnp.sum(zq * zq, axis=-1, keepdims=True) + 1e-6)
+        rk = lax.rsqrt(jnp.sum(zk * zk, axis=-1, keepdims=True) + 1e-6)
+        q = zq * rq * DK ** -0.5
+        k = zk * rk
+        within = jnp.exp(jnp.where(incl, sum_col[:, h:h + 1] - sum_row[h:h + 1, :], -1e30))
+        beta = beta_all[:, heads + h:heads + h + 1]
+        total = sum_col[:, h:h + 1]
+        growth = jnp.exp(total)
+        last = total[span - 1:span, :]
+        growth_last = jnp.exp(last)
+        tail = jnp.exp(last - total)
+        start = start_ref[0, h].astype(F32)
+        fresh = fresh_ref[:, cols].astype(F32)
+        inv = inv_ref[0, h]
+        scores = mm(q, k, NT, 3) * within
+        inner = mm(k, k, NT, 3)
+        k_state = mm(k, start, NN, 3)
+        q_state = mm(q, start, NN, 3)
+        out = out_ref[:, cols]
+        gate = raw_ref[:, qkv + h * DV:qkv + (h + 1) * DV]
+        gate_sig = sigmoid(gate)
+        gate_act = gate * gate_sig
+        dgated = grad_ref[:, cols].astype(F32)
+        r = lax.rsqrt(jnp.mean(out * out, axis=-1, keepdims=True) + 1e-5)
+        unit = out * r
+        dnormed = dgated * gate_act
+        draw_ref[:, qkv + h * DV:qkv + (h + 1) * DV] = (
+            dgated * (unit * gain) * (gate_sig * (1.0 + gate * (1.0 - gate_sig)))
+        ).astype(LOW)
+        dgain = dgain + jnp.sum(dnormed * unit, axis=0, keepdims=True)
+        dunit = dnormed * gain
+        dout = r * (dunit - unit * jnp.mean(dunit * unit, axis=-1, keepdims=True))
+        dnext = dstate[h] * keep_next
+        dfresh = mm(scores, dout, TN, 3) + mm(k * tail, dnext, NN, 3)
+        dright = mm(inv, dfresh, TN, 3)
+        dscores = jnp.where(incl, mm(dout, fresh, NT, 3), 0.0)
+        dlower = jnp.where(strict, -mm(dright, fresh, NT, 3), 0.0)
+        scaled = beta * growth * dright
+        dstate[h] = growth_last * dnext + mm(q * growth, dout, TN, 3) - mm(k, scaled, TN, 3)
+        dv = beta * dright
+        dbeta = jnp.sum(dright * (v - growth * k_state), axis=-1, keepdims=True)
+        dgrowth = jnp.sum(dout * q_state - dv * k_state, axis=-1, keepdims=True)
+        dsw = dscores * within
+        dq = growth * mm(dout, start, NT, 3) + mm(dsw, k, NN, 3)
+        into_k = mm(fresh, dnext, NT, 3)
+        dinner = dlower * within
+        dbeta = dbeta + jnp.sum(dinner * inner, axis=-1, keepdims=True)
+        weighted = beta * dinner
+        dk = (
+            tail * into_k
+            - mm(scaled, start, NT, 3)
+            + mm(dsw, q, TN, 3)
+            + mm(weighted, k, NN, 3)
+            + mm(weighted, k, TN, 3)
+        )
+        tailed = tail * jnp.sum(k * into_k, axis=-1, keepdims=True)
+        pairs = dscores * scores + weighted * inner
+        at_last = growth_last * jnp.sum(start * dnext, keepdims=True) + jnp.sum(tailed, keepdims=True)
+        dsum = jnp.sum(pairs, axis=-1, keepdims=True) + growth * dgrowth - tailed + jnp.where(last_row, at_last, 0.0)
+        down_rows.append(jnp.sum(pairs, axis=0, keepdims=True))
+        dsum_all = jnp.where(lane == h, dsum, dsum_all)
+        dbeta_all = jnp.where(lane == heads + h, dbeta, dbeta_all)
+        dzq = (DK ** -0.5 * rq) * (dq - zq * (rq * rq * jnp.sum(dq * zq, axis=-1, keepdims=True)))
+        dzk = rk * (dk - zk * (rk * rk * jnp.sum(dk * zk, axis=-1, keepdims=True)))
+        ext[0:span, h * DK:(h + 1) * DK] = dzq * slope_q
+        ext[0:span, kw + h * DK:kw + (h + 1) * DK] = dzk * slope_k
+        ext[0:span, 2 * kw + h * DV:2 * kw + (h + 1) * DV] = dv * slope_v
+
+    dgain_ref[...] += dgain
+    upper = jnp.where(row <= col, 1.0, 0.0)
+    down = jnp.concatenate(down_rows + [jnp.zeros((LANES - heads, span), F32)], axis=0)
+    ddecay = mm(upper, dsum_all, NN, 6) - mm(upper, down, NT, 6)
+    ddecay = jnp.where(lane < heads, ddecay, 0.0)
+    dalpha = ddecay * (-jnp.exp(rates[0:1, :])) * sigmoid(soft_in)
+    dbeta_raw = jnp.where((lane >= heads) & (lane < 2 * heads), dbeta_all * beta_all * (1.0 - beta_all), 0.0)
+    draw_ref[:, qkv + vw:] = (dalpha + dbeta_raw).astype(LOW)
+    drates_ref[0:1, :] += jnp.sum(ddecay * decay, axis=0, keepdims=True)
+    drates_ref[1:2, :] += jnp.sum(dalpha, axis=0, keepdims=True)
+    wide = 256
+    for begin in range(0, qkv, wide):
+        cols = slice(begin, begin + wide)
+        raw = raw_ref[:, cols]
+        total = None
+        for j in range(4):
+            shifted = ext[j:j + span, cols]
+            term = shifted * conv_ref[j:j + 1, cols]
+            total = term if total is None else total + term
+            dconv_ref[j:j + 1, cols] += jnp.sum(raw * shifted, axis=0, keepdims=True)
+        draw_ref[:, cols] = total.astype(LOW)
+
+
+def mixer_backward(raw, kept, grad, keep, conv, rates, gain, heads):
+    conved, fresh, out, inv, start = kept
+    rows, width = raw.shape
+    count = rows // STRETCH
+    kw, vw = heads * DK, heads * DV
+    qkv = 2 * kw + vw
+    at = lambda i, keep_ref: (count - 1 - i, 0)
+    fixed = lambda i, keep_ref: (0, 0)
+    at4 = lambda i, keep_ref: (count - 1 - i, 0, 0, 0)
+    spec = pl.BlockSpec
+    return pl.pallas_call(
+        functools.partial(backward_kernel, heads),
+        grid_spec=pltpu.PrefetchScalarGridSpec(
+            num_scalar_prefetch=1,
+            grid=(count,),
+            in_specs=[
+                spec((STRETCH, width), at),
+                spec((STRETCH, qkv), at),
+                spec((STRETCH, vw), at),
+                spec((STRETCH, vw), at),
+                spec((1, heads, STRETCH, STRETCH), at4),
+                spec((1, heads, DK, DV), at4),
+                spec((STRETCH, vw), at),
+                spec((4, qkv), fixed),
+                spec((HALO, LANES), fixed),
+                spec((1, DV), fixed),
+            ],
+            out_specs=[spec((STRETCH, width), at), spec((4, qkv), fixed), spec((HALO, LANES), fixed), spec((1, DV), fixed)],
+            scratch_shapes=[pltpu.VMEM((heads, DK, DV), F32), pltpu.VMEM((STRETCH + HALO, qkv), F32)],
+        ),
+        out_shape=[
+            jax.ShapeDtypeStruct((rows, width), LOW),
+            jax.ShapeDtypeStruct((4, qkv), F32),
+            jax.ShapeDtypeStruct((HALO, LANES), F32),
+            jax.ShapeDtypeStruct((1, DV), F32),
+        ],
+        compiler_params=pltpu.CompilerParams(dimension_semantics=("arbitrary",), vmem_limit_bytes=32 << 20),
+        cost_estimate=pl.CostEstimate(flops=6 * 10**10, bytes_accessed=40 << 20, transcendentals=0),
+        name="mixer_backward",
+    )(jnp.concatenate([keep, jnp.zeros((1,), jnp.int32)]), raw, conved, fresh, out, inv, start, grad, conv, rates, gain)
 
 
 def product(left_rows, matrix):
-    return jnp.dot(left_rows, matrix, preferred_element_type=jnp.float32)
+    return lax.dot_general(left_rows, matrix, NN, preferred_element_type=F32)
 
 
 def product_nt(left_rows, matrix):
-    return lax.dot_general(
-        left_rows, matrix, (((1,), (1,)), ((), ())), preferred_element_type=jnp.float32
-    )
+    return lax.dot_general(left_rows, matrix, NT, preferred_element_type=F32)
 
 
 def product_tn(left_rows, right_rows):
-    return lax.dot_general(
-        left_rows, right_rows, (((0,), (0,)), ((), ())), preferred_element_type=jnp.float32
-    )
+    return lax.dot_general(left_rows, right_rows, TN, preferred_element_type=F32)
 
 
 def rms_rows(rows_in, gain_row):
     return (
         rows_in * lax.rsqrt(jnp.mean(rows_in * rows_in, axis=-1, keepdims=True) + 1e-06) * gain_row
     )
-
-
-def unit_norm(source_rows):
-    return source_rows * lax.rsqrt(
-        jnp.sum(source_rows * source_rows, axis=-1, keepdims=True) + 1e-06
-    )
-
-
-def causal_conv(raw_rows, weight, seq_start):
-    positions = jnp.arange(raw_rows.shape[0], dtype=jnp.int32)
-    result = raw_rows * weight[0]
-    for tap_shift in range(1, weight.shape[0]):
-        shifted = jnp.concatenate(
-            [jnp.zeros((tap_shift, raw_rows.shape[1]), jnp.float32), raw_rows[:-tap_shift]], axis=0
-        )
-        valid_taps = positions - tap_shift >= seq_start
-        result = result + jnp.where(valid_taps[:, None], shifted, 0.0) * weight[tap_shift]
-    return result
-
-
-def unit_inverse(lower_part):
-    identity = jnp.eye(STRETCH, dtype=jnp.float32)
-    inverse = identity - lower_part
-    power_term = jnp.einsum("hts,hsu->htu", lower_part, lower_part, precision=precise)
-    repeats = STRETCH.bit_length() - 2
-    for repeat in range(repeats):
-        inverse = inverse + jnp.einsum("hts,hsu->htu", inverse, power_term, precision=precise)
-        if repeat + 1 < repeats:
-            power_term = jnp.einsum("hts,hsu->htu", power_term, power_term, precision=precise)
-    return inverse
-
-
-def stretch_step(carry_state, inputs):
-    query_block, key_block, value_block, beta_block, decay_block, keep_flag = inputs
-    carry_state = carry_state * keep_flag
-    inclusive = jnp.tri(STRETCH, dtype=bool)
-    strict = jnp.tri(STRETCH, k=-1, dtype=bool)
-    cumulative = jnp.einsum("ts,hs->ht", inclusive.astype(jnp.float32), decay_block, precision=precise)
-    spread = cumulative[:, :, None] - cumulative[:, None, :]
-    within = jnp.where(inclusive, jnp.exp(jnp.where(inclusive, spread, 0.0)), 0.0)
-    key_inner = jnp.einsum("htd,hsd->hts", key_block, key_block, precision=precise)
-    lower_part = jnp.where(strict, beta_block[:, :, None] * key_inner * within, 0.0)
-    inverse = unit_inverse(lower_part)
-    growth = jnp.exp(cumulative)
-    right_side = jnp.concatenate(
-        [(beta_block * growth)[:, :, None] * key_block, beta_block[:, :, None] * value_block],
-        axis=-1,
-    )
-    solved = jnp.einsum("hts,hsd->htd", inverse, right_side, precision=precise)
-    key_part = solved[:, :, :DK]
-    value_part = solved[:, :, DK:]
-    fresh_rows = value_part - jnp.einsum("htd,hde->hte", key_part, carry_state, precision=precise)
-    scores = jnp.einsum("htd,hsd->hts", query_block, key_block, precision=precise) * within
-    block_out = growth[:, :, None] * jnp.einsum(
-        "htd,hde->hte", query_block, carry_state, precision=precise
-    )
-    block_out = block_out + jnp.einsum("hts,hse->hte", scores, fresh_rows, precision=precise)
-    last_sum = cumulative[:, -1:]
-    tail_decay = jnp.exp(last_sum - cumulative)
-    new_state = jnp.exp(last_sum)[:, :, None] * carry_state
-    new_state = new_state + jnp.einsum(
-        "htd,hte->hde", key_block * tail_decay[:, :, None], fresh_rows, precision=precise
-    )
-    return (new_state, block_out)
-
-
-def delta_rule(queries, key_rows, values, beta_rows, decays, keep_state):
-    stretch_count = keep_state.shape[0]
-    head_count = queries.shape[1]
-
-    def split_stretches(source):
-        shaped = source.reshape((stretch_count, STRETCH) + source.shape[1:])
-        return jnp.moveaxis(shaped, 2, 1)
-
-    inputs = (
-        split_stretches(queries),
-        split_stretches(key_rows),
-        split_stretches(values),
-        split_stretches(beta_rows),
-        split_stretches(decays),
-        keep_state,
-    )
-    first_state = jnp.zeros((head_count, DK, DV), jnp.float32)
-    final_state, outputs = lax.scan(jax.checkpoint(stretch_step), first_state, inputs)
-    return jnp.moveaxis(outputs, 1, 2).reshape(stretch_count * STRETCH, head_count, DV)
-
-
-def mixer_core(raw_parts, small_parts, seq_start, keep_state):
-    query_raw, key_raw, value_raw, gate_raw, alpha_raw, beta_raw = raw_parts
-    query_conv, key_conv, value_conv, log_rate, rate_bias, head_gain = small_parts
-    row_count = query_raw.shape[0]
-    head_count = alpha_raw.shape[1]
-    queries = unit_norm(
-        jax.nn.silu(causal_conv(query_raw, query_conv, seq_start)).reshape(
-            row_count, head_count, DK
-        )
-    ) * DK ** (-0.5)
-    key_rows = unit_norm(
-        jax.nn.silu(causal_conv(key_raw, key_conv, seq_start)).reshape(row_count, head_count, DK)
-    )
-    values = jax.nn.silu(causal_conv(value_raw, value_conv, seq_start)).reshape(
-        row_count, head_count, DV
-    )
-    beta_rows = jax.nn.sigmoid(beta_raw)
-    decays = -jnp.exp(log_rate) * jax.nn.softplus(alpha_raw + rate_bias)
-    delta_out = delta_rule(queries, key_rows, values, beta_rows, decays, keep_state)
-    normed = (
-        delta_out
-        * lax.rsqrt(jnp.mean(delta_out * delta_out, axis=-1, keepdims=True) + 1e-05)
-        * head_gain
-    )
-    gated_out = normed * jax.nn.silu(gate_raw.reshape(row_count, head_count, DV))
-    return gated_out.reshape(row_count, head_count * DV)
 
 
 def layout(pack_lengths, pack_rows):
@@ -151,18 +378,14 @@
     first_len = pack_lengths[0]
     second_len = pack_lengths[1]
     second_start = (first_len + STRETCH - 1) // STRETCH * STRETCH
-    seq_start = jnp.where(positions >= second_start, second_start, 0)
     live_rows = (positions < first_len) | (positions >= second_start) & (
         positions < second_start + second_len
     )
     stretch_starts = jnp.arange(pack_rows // STRETCH, dtype=jnp.int32) * STRETCH
     keep_state = jnp.where(
-        (stretch_starts == 0) | (stretch_starts == second_start), 0.0, 1.0
-    ).astype(jnp.float32)
-    return (seq_start, keep_state, jnp.where(live_rows, 1.0, 0.0).astype(jnp.float32))
-
-
-LANES = 128
+        (stretch_starts == 0) | (stretch_starts == second_start), 0, 1
+    ).astype(jnp.int32)
+    return (keep_state, jnp.where(live_rows, 1.0, 0.0).astype(jnp.float32))
 
 
 def z_gather(own):
@@ -302,32 +525,25 @@
     layouts = [layout(lengths[m, 0], pack_rows) for m in packs]
     own_masks = [
         lax.dynamic_slice_in_dim(row_mask, tensor_index * local_rows, local_rows, 0)[:, None]
-        for _, _, row_mask in layouts
+        for _, row_mask in layouts
     ]
     out_grads = [cotangent[m].astype(wide) * own_masks[m] for m in packs]
     norm_ones = [jax.vjp(rms_rows, token_rows[m], mixer_gain) for m in packs]
     first_rows = [z_gather(norm_ones[m][0].astype(low)) for m in packs]
     grad_rows = [z_gather(out_grads[m].astype(low)) for m in packs]
 
-    cores, gated, middle, norm_twos, second_rows = [], [], [], [], []
+    conv_local = jnp.concatenate(small_local[:3], axis=1)
+    rates = jnp.zeros((HALO, LANES), wide)
+    rates = rates.at[0, :head_count].set(small_local[3]).at[1, :head_count].set(small_local[4])
+    gain_row = head_gain[None, :]
+    raws, kept, gated, middle, norm_twos, second_rows = [], [], [], [], [], []
     for m in packs:
-        raw = product(first_rows[m], in_full)
-        raw_parts = (
-            raw[:, : edges[0]],
-            raw[:, edges[0] : edges[1]],
-            raw[:, edges[1] : edges[2]],
-            raw[:, edges[2] : edges[3]],
-            raw[:, edges[3] : edges[3] + head_count],
-            raw[:, edges[3] + head_count : edges[3] + 2 * head_count],
+        raws.append(product(first_rows[m], in_full))
+        mixed, *rest = mixer_forward(
+            raws[m], layouts[m][0], conv_local, rates, gain_row, head_count
         )
-        seq_start, keep_state, _ = layouts[m]
-
-        def core_apply(raw_inputs, small_inputs, seq_start=seq_start, keep_state=keep_state):
-            return mixer_core(raw_inputs, small_inputs, seq_start, keep_state)
-
-        mixed, core_back = jax.vjp(core_apply, raw_parts, small_local)
-        cores.append(core_back)
-        gated.append(mixed.astype(low))
+        kept.append(rest)
+        gated.append(mixed)
     for m in packs:
         middle.append(token_rows[m] + z_scatter(product_nt(gated[m], out_full)))
         norm_twos.append(jax.vjp(rms_rows, middle[m], feed_gain))
@@ -358,21 +574,27 @@
 
     raw_grads, input_grads = [], []
     for m in packs:
-        parts, small_grads = cores[m](product(mix_rows[m], out_full))
-        raw_grads.append(
-            jnp.concatenate([*parts, jnp.zeros((pack_rows, pad), wide)], axis=1).astype(low)
+        raw_grad, conv_grad, rate_grad, gain_grad = mixer_backward(
+            raws[m],
+            kept[m],
+            product(mix_rows[m], out_full),
+            layouts[m][0],
+            conv_local,
+            rates,
+            gain_row,
+            head_count,
         )
+        raw_grads.append(raw_grad)
         first_grad = z_scatter(product_nt(raw_grads[m], in_full))
         token_norm_grad, mixer_gain_grad = norm_ones[m][1](first_grad)
         input_grads.append(middle_grads[m] + token_norm_grad)
-        small_terms[m] += [mixer_gain_grad, *small_grads]
+        small_terms[m] += [mixer_gain_grad, conv_grad, rate_grad[:2, :head_count], gain_grad[0]]
     in_final = scatter_rows(product_tn(joined(first_rows), joined(raw_grads)))
 
     feed_gain_grad, mixer_gain_grad, *core_grads = [sum(terms) for terms in zip(*small_terms)]
-    conv_grads = jnp.concatenate(core_grads[:3], axis=1)
-    rates = jnp.concatenate(core_grads[3:5])
-    everywhere = jnp.concatenate([feed_gain_grad, mixer_gain_grad, core_grads[5]])
-    per_slice = jnp.concatenate([conv_grads.reshape(-1), rates])
+    conv_grads, rate_grads, gain_grads = core_grads
+    everywhere = jnp.concatenate([feed_gain_grad, mixer_gain_grad, gain_grads])
+    per_slice = jnp.concatenate([conv_grads.reshape(-1), rate_grads.reshape(-1)])
     packed = sum_over(jnp.concatenate([per_slice, everywhere]), "dp")
     slices = jnp.zeros((tensor_count, per_slice.size), wide)
     slices = lax.dynamic_update_index_in_dim(slices, packed[: per_slice.size], tensor_index, 0)

time: 1890 us -> 1060 us (0.56)
  matrix products: 774 us -> 191 us
  local copies, waits for them, and re-layouts: 277 us -> 44.3 us
  other arithmetic: 273 us -> 83.4 us
  Pallas kernels: 0 us -> 149 us
  starting transfers between devices: 204 us -> 249 us
    dot_general x1124 -> x20, matrix products: 774 us -> 191 us  [the longest x8 71.8 us: product(): return lax.dot_general(left_rows, matrix, NN, preferred_element_type=F32)]
    pallas_call x0 -> x4, Pallas kernels: none -> 149 us  [the longest x2 85.7 us: mixer_backward(): pl.pallas_call(functools.partial(backward_kernel, heads), grid_spec=pltpu...]
    reduce_sum x81 -> x0, other arithmetic: 63.8 us -> none  [the longest x2 15.3 us: causal_conv(): jnp.where(valid_taps[:, None], shifted, 0.0) * weight[tap_shift]]
    squeeze x64 -> x0, local copies, waits for them, and re-layouts: 62.3 us -> none  [delta_rule(): lax.scan(jax.checkpoint(stretch_step), first_state, inputs)]
    mul x75 -> x0, other arithmetic: 50.7 us -> none  [the longest x32 17.7 us: stretch_step(): (beta_block * growth)[:, :, None] * key_block]
    reshape x40 -> x1, local copies, waits for them, and re-layouts: 41.1 us -> 0.08 us  [shards(): rate_grads.reshape(-1)]
    slice x47 -> x0, local copies, waits for them, and re-layouts: 32.6 us -> none  [the longest x12 22.9 us: causal_conv(): raw_rows[:-tap_shift]]
    dynamic_update_slice x48 -> x0, other arithmetic: 26.8 us -> none  [delta_rule(): lax.scan(jax.checkpoint(stretch_step), first_state, inputs)]
  transfers between devices with their start and end apart: 93 -> 93, of which waited for: 47 -> 46; matrix products, arithmetic and copies ran while one was open for 67% -> 23% of each run, Pallas kernels for 0% -> 14%
where the time goes in v2:
time: 1060 us; the launch traced here: 1050 us
  waiting for transfers between devices  317 us (30%)
  starting transfers between devices  249 us (23%)
  matrix products  191 us (18%)
  Pallas kernels  149 us (14%)
  other arithmetic  83.4 us (8%)
  local copies, waits for them, and re-layouts  44.3 us (4%)
  between operations  19.2 us (2%)
    pallas_call x2, Pallas kernels, mixer_backward(): pl.pallas_call(functools.partial(backward_kernel, heads), grid_spec=pltpu...  85.7 us
    dot_general x8, matrix products, product(): return lax.dot_general(left_rows, matrix, NN, preferred_element_type=F32)  71.8 us
    ppermute x8, waiting for transfers between devices, z_gather(): left2 = lax.ppermute(left, 'tensor', [(1, 0), (2, 1)])  67.8 us
    pallas_call x2, Pallas kernels, mixer_forward(): pl.pallas_call(functools.partial(forward_kernel, heads), grid_spec=pltpu....  63.5 us
    dot_general x8, matrix products, product_nt(): return lax.dot_general(left_rows, matrix, NT, preferred_element_type=F32)  62.9 us
    ppermute x8, starting transfers between devices, z_gather(): right = lax.ppermute(own, 'tensor', [(0, 1), (1, 2), (2, 3)])  59.1 us
    ppermute x8, waiting for transfers between devices, z_gather(): lax.ppermute(jnp.where(t == 1, right, left), 'tensor', [(1, 3), (2, 0)])  58.5 us
    ppermute x8, starting transfers between devices, z_scatter(): lax.ppermute(to_right.astype(jnp.bfloat16), 'tensor', [(0, 1), (1, 2), (2...  58.2 us
  transfers between devices with their start and end apart: 93, of which 46 were waited for; matrix products, arithmetic and copies ran while one was open for 23% of the time, Pallas kernels for 14%

profile of v2, /device:TPU:0, one launch (start us, length us, event | category | flops | bytes accessed | tf_op | source)
XLA Modules:
  0.0 1052.9 jit_solution(11310646441788525140)
XLA Ops:
  75.3 21.1 %collective-permute-done.3 = bf16[128,2048]{1,0:T(8,128)(2,1)S(1)} collective-permute-done((bf16[128,2048]{1,0:T(8,128)(2,1)S(1)}, bf16[128,2048]{1,0:T(8,128)(2,1)S(1)}, u32[]{:S(2)}, u32[]{:S(2)}) %collective-permute-start.3) | collective-permute-done | bytes 524320 | tf_op jit(solution)/shard_map/ppermute | solution.py:400
  101.7 27.3 %collective-permute-done.4 = bf16[128,2048]{1,0:T(8,128)(2,1)S(1)} collective-permute-done((bf16[128,2048]{1,0:T(8,128)(2,1)S(1)}, bf16[128,2048]{1,0:T(8,128)(2,1)S(1)}, u32[]{:S(2)}, u32[]{:S(2)}) %collective-permute-start.4) | collective-permute-done | bytes 524320 | tf_op jit(solution)/shard_map/ppermute | solution.py:399
  139.1 12.2 %fusion.23.raw_ref = f32[512,3200]{1,0:T(8,128)S(1)} fusion(bf16[2048,3200]{1,0:T(8,128)(2,1)} %all-gather.5.cloned.1.call-done, bf16[128,2048]{1,0:T(8,128)(2,1)} %get-tuple-element.173, bf16[128,2048]{1,0:T(8,128)(2,1)} %get-tuple-element.175, bf16[128,2048]{1,0:T(8,128)(2,1)S(1)} %copy-done.58, bf16[128,2048]{1,0:T(8,128)(2,1)S(1)} %copy-done.56), kind=kOutput, calls=%fused_computation.35 | convolution fusion | flops 6719275008 | bytes 21757952 | tf_op jit(solution)/shard_map/dot_general | solution.py:359
  151.4 31.8 %mixer_forward.2 = (bf16[512,1024]{1,0:T(8,128)(2,1)S(1)}, f32[512,2048]{1,0:T(8,128)S(1)}, f32[512,1024]{1,0:T(8,128)S(1)}, f32[512,1024]{1,0:T(8,128)S(1)}, f3...) custom-call(s32[8]{0:T(128)S(1)} %get-tuple-element.270.keep_ref, f32[512,3200]{1,0:T(8,128)S(1)} %fusion.23.raw_ref, ...), custom_call_target="tpu_custom_call" | custom-call | flops 30000001024 | bytes 31457280 | tf_op jit(solution)/shard_map/mixer_forward/pallas_call | solution.py:151
  199.2 12.6 %collective-permute-start.6 = (bf16[128,2048]{1,0:T(8,128)(2,1)}, bf16[128,2048]{1,0:T(8,128)(2,1)S(1)}, u32[]{:S(2)}, u32[]{:S(2)}) collective-permute-start(bf16[128,2048]{1,0:T(8,128)(2,1)} %get-tuple-element.233), channel_id=1, source_target_pairs={{3,1},{0,2},{7,5},{4,6},{11,9},{8,10},{15,13},{12,14},{19,17},{16,... | collective-permute-start | bytes 1572872 | tf_op jit(solution)/shard_map/ppermute | solution.py:430
  213.6 11.1 %fusion.39.raw_ref = f32[512,3200]{1,0:T(8,128)S(1)} fusion(bf16[2048,3200]{1,0:T(8,128)(2,1)} %all-gather.5.cloned.1.call-done, bf16[128,2048]{1,0:T(8,128)(2,1)S(1)} %copy-done.60, bf16[128,2048]{1,0:T(8,128)(2,1)S(1)} %copy-done.59, bf16[128,2048]{1,0:T(8,128)(2,1)S(1)} %copy-done.57, bf16[128,2048]{1,0:T(8,128)(2,1)S(1)} %copy-done.55), kind=kOutput, calls=%fused_computation.51 | convolution fusion | flops 6719275008 | bytes 21757952 | tf_op jit(solution)/shard_map/dot_general | solution.py:359
  224.8 31.8 %mixer_forward.3 = (bf16[512,1024]{1,0:T(8,128)(2,1)S(1)}, f32[512,2048]{1,0:T(8,128)S(1)}, f32[512,1024]{1,0:T(8,128)S(1)}, f32[512,1024]{1,0:T(8,128)S(1)}, f3...) custom-call(s32[8]{0:T(128)S(1)} %get-tuple-element.269.keep_ref, f32[512,3200]{1,0:T(8,128)S(1)} %fusion.39.raw_ref, ...), custom_call_target="tpu_custom_call" | custom-call | flops 30000001024 | bytes 31457280 | tf_op jit(solution)/shard_map/mixer_forward/pallas_call | solution.py:151
  277.4 17.1 %collective-permute-start.9 = (bf16[128,2048]{1,0:T(8,128)(2,1)S(1)}, bf16[128,2048]{1,0:T(8,128)(2,1)S(1)}, u32[]{:S(2)}, u32[]{:S(2)}) collective-permute-start(bf16[128,2048]{1,0:T(8,128)(2,1)S(1)} %get-tuple-element.211), channel_id=1, source_target_pairs={{0,1},{1,2},{2,3},{4,5},{5,6},{6,7},{8,9},{9,10},{10,11},{12,13},{... | collective-permute-start | bytes 1572872 | tf_op jit(solution)/shard_map/ppermute | solution.py:437
  316.7 15.4 %collective-permute-start.10 = (bf16[128,2048]{1,0:T(8,128)(2,1)S(1)}, bf16[128,2048]{1,0:T(8,128)(2,1)S(1)}, u32[]{:S(2)}, u32[]{:S(2)}) collective-permute-start(bf16[128,2048]{1,0:T(8,128)(2,1)S(1)} %multiply_convert_fusion.7), channel_id=1, source_target_pairs={{0,1},{1,2},{2,3},{4,5},{5,6},{6,7},{8,9},{9,10},{10,11},{12,13},{... | collective-permute-start | bytes 1572872 | tf_op jit(solution)/shard_map/ppermute | solution.py:396
  348.9 15.9 %collective-permute-done.13 = bf16[128,2048]{1,0:T(8,128)(2,1)S(1)} collective-permute-done((bf16[128,2048]{1,0:T(8,128)(2,1)S(1)}, bf16[128,2048]{1,0:T(8,128)(2,1)S(1)}, u32[]{:S(2)}, u32[]{:S(2)}) %collective-permute-start.13) | collective-permute-done | bytes 524320 | tf_op jit(solution)/shard_map/ppermute | solution.py:400
  378.2 11.7 %fusion.31 = f32[512,2816]{1,0:T(8,128)} fusion(bf16[2048,2816]{1,0:T(8,128)(2,1)} %all-gather.9.cloned.1.call-done, bf16[128,2048]{1,0:T(8,128)(2,1)} %get-tuple-element.141, bf16[128,2048]{1,0:T(8,128)(2,1)} %get-tuple-element.143, bf16[128,2048]{1,0:T(8,128)(2,1)} %get-tuple-element.145, bf16[128,2048]{1,0:T(8,128)(2,1)} %get-tuple-element.147), kind=kOutput, calls=%fused_computation.43 | convolution fusion | flops 5913968640 | bytes 19398656 | tf_op jit(solution)/shard_map/dot_general | solution.py:359
  389.9 9.3 multiply_convert_fusion.3
  442.2 10.3 collective-permute-start.49
  452.5 10.3 collective-permute-done.18
  486.8 13.1 %collective-permute-start.30 = (bf16[128,2048]{1,0:T(8,128)(2,1)S(1)}, bf16[128,2048]{1,0:T(8,128)(2,1)S(1)}, u32[]{:S(2)}, u32[]{:S(2)}) collective-permute-start(bf16[128,2048]{1,0:T(8,128)(2,1)S(1)} %get-tuple-element.264), channel_id=1, source_target_pairs={{0,1},{1,2},{2,3},{4,5},{5,6},{6,7},{8,9},{9,10},{10,11},{12,13},{... | collective-permute-start | bytes 1572872 | tf_op jit(solution)/shard_map/ppermute | solution.py:396
  516.7 12.0 %collective-permute-done.33 = bf16[128,2048]{1,0:T(8,128)(2,1)S(1)} collective-permute-done((bf16[128,2048]{1,0:T(8,128)(2,1)S(1)}, bf16[128,2048]{1,0:T(8,128)(2,1)S(1)}, u32[]{:S(2)}, u32[]{:S(2)}) %collective-permute-start.33) | collective-permute-done | bytes 524320 | tf_op jit(solution)/shard_map/ppermute | solution.py:400
  539.8 11.4 %fusion.47 = f32[512,2816]{1,0:T(8,128)} fusion(bf16[2048,2816]{1,0:T(8,128)(2,1)} %all-gather.9.cloned.1.call-done, bf16[128,2048]{1,0:T(8,128)(2,1)S(1)} %get-tuple-element.133, bf16[128,2048]{1,0:T(8,128)(2,1)S(1)} %get-tuple-element.135, bf16[128,2048]{1,0:T(8,128)(2,1)S(1)} %get-tuple-element.137, bf16[128,2048]{1,0:T(8,128)(2,1)S(1)} %get-tuple-element.139), kind=kOutput, calls=%fused_computation.59 | convolution fusion | flops 5913968640 | bytes 19398656 | tf_op jit(solution)/shard_map/dot_general | solution.py:359
  559.8 10.5 fusion.14
  593.7 9.2 collective-permute-done.68
  614.2 11.2 %collective-permute-done.38 = bf16[128,2048]{1,0:T(8,128)(2,1)S(1)} collective-permute-done((bf16[128,2048]{1,0:T(8,128)(2,1)S(1)}, bf16[128,2048]{1,0:T(8,128)(2,1)S(1)}, u32[]{:S(2)}, u32[]{:S(2)}) %collective-permute-start.38) | collective-permute-done | bytes 524320 | tf_op jit(solution)/shard_map/ppermute | solution.py:432
  680.0 9.5 collective-permute-done.53
  690.9 23.3 %collective-permute-done.54 = bf16[128,2048]{1,0:T(8,128)(2,1)S(1)} collective-permute-done((bf16[128,2048]{1,0:T(8,128)(2,1)S(1)}, bf16[128,2048]{1,0:T(8,128)(2,1)S(1)}, u32[]{:S(2)}, u32[]{:S(2)}) %collective-permute-start.54) | collective-permute-done | bytes 524320 | tf_op jit(solution)/shard_map/ppermute | solution.py:399
  730.4 11.0 %convolution_convert_fusion.2 = bf16[2048,1408]{1,0:T(8,128)(2,1)} fusion(bf16[1024,2048]{1,0:T(8,128)(2,1)} %get-tuple-element.116, bf16[512,1408]{1,0:T(8,128)(2,1)} %copy-done.85, bf16[512,1408]{1,0:T(8,128)(2,1)} %copy-done.84), kind=kOutput, calls=%fused_computation.2 | convolution fusion | flops 5914230784 | bytes 12845056 | tf_op jit(solution)/shard_map/dot_general | solution.py:367
  741.7 19.1 %convolution_convert_fusion.1 = bf16[2048,2816]{1,0:T(8,128)(2,1)} fusion(bf16[1024,2048]{1,0:T(8,128)(2,1)} %get-tuple-element.132, bf16[512,1408]{1,0:T(8,128)(2,1)} %get-tuple-element.195, bf16[512,1408]{1,0:T(8,128)(2,1)} %copy-done.88, bf16[512,1408]{1,0:T(8,128)(2,1)} %copy-done.87, bf16[512,1408]{1,0:T(8,128)(2,1)} %copy-done.86), kind=kOutput, calls=%fused_computation.1 | convolution fusion | flops 11839995904 | bytes 21495808 | tf_op jit(solution)/shard_map/dot_general | solution.py:367
  770.6 43.4 %mixer_backward.2 = (bf16[512,3200]{1,0:T(8,128)(2,1)S(1)}, f32[4,2048]{1,0:T(4,128)S(1)}, f32[8,128]{1,0:T(8,128)S(1)}, f32[1,256]{1,0:T(1,128)S(1)}) custom-call(s32[9]{0:T(128)S(1)} %pad_add_fusion.1.keep_ref, f32[512,3200]{1,0:T(8,128)} %copy-done.12, f32[512,2048]{1,0:T(8,128)S(1)} %copy-done.16, f32[512,1024]{1,0:T(8,128)S(1)} %get-tuple-element.67.fresh_ref, ...), custom_call_target="tpu_custom_call" | custom-call | flops 60000002048 | bytes 41943040 | tf_op jit(solution)/shard_map/mixer_backward/pallas_call | solution.py:326
  819.6 42.4 %mixer_backward.3 = (bf16[512,3200]{1,0:T(8,128)(2,1)S(1)}, f32[4,2048]{1,0:T(4,128)S(1)}, f32[8,128]{1,0:T(8,128)S(1)}, f32[1,256]{1,0:T(1,128)S(1)}) custom-call(s32[9]{0:T(128)S(1)} %pad_add_fusion.keep_ref, f32[512,3200]{1,0:T(8,128)} %copy-done.13, f32[512,2048]{1,0:T(8,128)S(1)} %copy-done.20, f32[512,1024]{1,0:T(8,128)S(1)} %copy-done.26, ...), custom_call_target="tpu_custom_call" | custom-call | flops 60000002048 | bytes 41943040 | tf_op jit(solution)/shard_map/mixer_backward/pallas_call | solution.py:326
  862.0 20.3 %convolution_convert_fusion = bf16[2048,3200]{1,0:T(8,128)(2,1)} fusion(bf16[1024,2048]{1,0:T(8,128)(2,1)} %get-tuple-element.164, bf16[512,3200]{1,0:T(8,128)(2,1)S(1)} %get-tuple-element.77, bf16[512,3200]{1,0:T(8,128)(2,1)S(1)} %get-tuple-element.71), kind=kOutput, calls=%fused_computation | convolution fusion | flops 13441433600 | bytes 23855104 | tf_op jit(solution)/shard_map/dot_general | solution.py:367
  882.3 11.3 %fusion.209 = f32[512,2048]{1,0:T(8,128)S(1)} fusion(bf16[512,3200]{1,0:T(8,128)(2,1)} %copy-done.14, bf16[2048,3200]{1,0:T(8,128)(2,1)} %all-gather.5.cloned.1.call-done), kind=kOutput, calls=%fused_computation.402 | convolution fusion | flops 6710886400 | bytes 20578304 | tf_op jit(solution)/shard_map/dot_general | solution.py:363
  894.8 9.0 collective-permute-start.56
  905.2 10.6 %fusion.210 = f32[512,2048]{1,0:T(8,128)S(1)} fusion(bf16[512,3200]{1,0:T(8,128)(2,1)S(1)} %get-tuple-element.77, bf16[2048,3200]{1,0:T(8,128)(2,1)} %all-gather.5.cloned.1.call-done), kind=kOutput, calls=%fused_computation.403 | convolution fusion | flops 6710886400 | bytes 20578304 | tf_op jit(solution)/shard_map/dot_general | solution.py:363
  938.7 11.2 %collective-permute-done.78 = bf16[128,2048]{1,0:T(8,128)(2,1)S(1)} collective-permute-done((bf16[128,2048]{1,0:T(8,128)(2,1)S(1)}, bf16[128,2048]{1,0:T(8,128)(2,1)S(1)}, u32[]{:S(2)}, u32[]{:S(2)}) %collective-permute-start.78) | collective-permute-done | bytes 524320 | tf_op jit(solution)/shard_map/ppermute | solution.py:432
  1015.8 23.9 %reduce-scatter.5.cloned.1.call-done = bf16[256,3200]{1,0:T(8,128)(2,1)} async-done(((bf16[2048,3200]{1,0:T(8,128)(2,1)}), bf16[256,3200]{1,0:T(8,128)(2,1)}) %reduce-scatter.5.cloned.1.call-update) | async-done | bytes 1638416 | tf_op jit(solution)/shard_map/reduce_scatter | solution.py:457
  (515 shorter events, 493.3 us)
Async XLA Ops:
  7.2 131.9 %all-gather.5.cloned.1.call-start = ((), (), s32[]{:S(2)}) async-start(), calls=%async_computation.4 | async-start | bytes 14745600 | tf_op jit(solution)/shard_map/all_gather | solution.py:453
  12.9 179.2 %all-gather.7.cloned.1.call-start = ((), (), s32[]{:S(2)}) async-start(), calls=%async_computation.5 | async-start | bytes 4718592 | tf_op jit(solution)/shard_map/all_gather | solution.py:453
  13.7 364.6 %all-gather.9.cloned.1.call-start = ((), (), s32[]{:S(2)}) async-start(), calls=%async_computation.6 | async-start | bytes 12976128 | tf_op jit(solution)/shard_map/all_gather | solution.py:453
  16.1 373.9 %all-gather.11.cloned.1.call-start = ((), (), s32[]{:S(2)}) async-start(), calls=%async_computation.7 | async-start | bytes 6488064 | tf_op jit(solution)/shard_map/all_gather | solution.py:453
  37.8 969.6 %reduce-scatter.7.cloned.1.call-start = ((), (), s32[]{:S(2)}) async-start(), calls=%async_computation.9 | async-start | bytes 4718592 | tf_op jit(solution)/shard_map/reduce_scatter | solution.py:457
  54.7 210.0 %collective-permute-start.43 = (bf16[128,2048]{1,0:T(8,128)(2,1)}, bf16[128,2048]{1,0:T(8,128)(2,1)}, u32[]{:S(2)}, u32[]{:S(2)}) collective-permute-start(bf16[128,2048]{1,0:T(8,128)(2,1)} %broadcast_select_fusion.3), channel_id=1, source_target_pairs={{1,3},{2,0},{5,7},{6,4},{9,11},{10,8},{13,15},{14,12},{17,19},{18,... | collective-permute-start | bytes 1572872 | tf_op jit(solution)/shard_map/ppermute | solution.py:400
  61.2 35.2 %collective-permute-start.3 = (bf16[128,2048]{1,0:T(8,128)(2,1)S(1)}, bf16[128,2048]{1,0:T(8,128)(2,1)S(1)}, u32[]{:S(2)}, u32[]{:S(2)}) collective-permute-start(bf16[128,2048]{1,0:T(8,128)(2,1)S(1)} %broadcast_select_fusion.7), channel_id=1, source_target_pairs={{1,3},{2,0},{5,7},{6,4},{9,11},{10,8},{13,15},{14,12},{17,19},{18,... | collective-permute-start | bytes 1572872 | tf_op jit(solution)/shard_map/ppermute | solution.py:400
  62.7 35.0 %collective-permute-start.1 = (bf16[128,2048]{1,0:T(8,128)(2,1)}, bf16[128,2048]{1,0:T(8,128)(2,1)S(1)}, u32[]{:S(2)}, u32[]{:S(2)}) collective-permute-start(bf16[128,2048]{1,0:T(8,128)(2,1)} %collective-permute-done), channel_id=1, source_target_pairs={{1,2},{2,3},{5,6},{6,7},{9,10},{10,11},{13,14},{14,15},{17,18},{18... | collective-permute-start | bytes 1572872 | tf_op jit(solution)/shard_map/ppermute | solution.py:398
  71.6 62.0 %collective-permute-start.23 = (bf16[128,2048]{1,0:T(8,128)(2,1)S(1)}, bf16[128,2048]{1,0:T(8,128)(2,1)S(1)}, u32[]{:S(2)}, u32[]{:S(2)}) collective-permute-start(bf16[128,2048]{1,0:T(8,128)(2,1)S(1)} %broadcast_select_fusion.5), channel_id=1, source_target_pairs={{1,3},{2,0},{5,7},{6,4},{9,11},{10,8},{13,15},{14,12},{17,19},{18,... | collective-permute-start | bytes 1572872 | tf_op jit(solution)/shard_map/ppermute | solution.py:400
  72.9 192.5 %collective-permute-start.41 = (bf16[128,2048]{1,0:T(8,128)(2,1)}, bf16[128,2048]{1,0:T(8,128)(2,1)}, u32[]{:S(2)}, u32[]{:S(2)}) collective-permute-start(bf16[128,2048]{1,0:T(8,128)(2,1)} %collective-permute-done.40), channel_id=1, source_target_pairs={{1,2},{2,3},{5,6},{6,7},{9,10},{10,11},{13,14},{14,15},{17,18},{18... | collective-permute-start | bytes 1572872 | tf_op jit(solution)/shard_map/ppermute | solution.py:398
  96.4 40.0 %collective-permute-start.24 = (bf16[128,2048]{1,0:T(8,128)(2,1)S(1)}, bf16[128,2048]{1,0:T(8,128)(2,1)S(1)}, u32[]{:S(2)}, u32[]{:S(2)}) collective-permute-start(bf16[128,2048]{1,0:T(8,128)(2,1)S(1)} %collective-permute-done.22), channel_id=1, source_target_pairs={{1,0},{2,1},{5,4},{6,5},{9,8},{10,9},{13,12},{14,13},{17,16},{18,1... | collective-permute-start | bytes 1572872 | tf_op jit(solution)/shard_map/ppermute | solution.py:399
  97.7 31.3 %collective-permute-start.4 = (bf16[128,2048]{1,0:T(8,128)(2,1)S(1)}, bf16[128,2048]{1,0:T(8,128)(2,1)S(1)}, u32[]{:S(2)}, u32[]{:S(2)}) collective-permute-start(bf16[128,2048]{1,0:T(8,128)(2,1)S(1)} %collective-permute-done.2), channel_id=1, source_target_pairs={{1,0},{2,1},{5,4},{6,5},{9,8},{10,9},{13,12},{14,13},{17,16},{18,1... | collective-permute-start | bytes 1572872 | tf_op jit(solution)/shard_map/ppermute | solution.py:399
  198.5 72.1 %collective-permute-start.5 = (bf16[128,2048]{1,0:T(8,128)(2,1)}, bf16[128,2048]{1,0:T(8,128)(2,1)S(1)}, u32[]{:S(2)}, u32[]{:S(2)}) collective-permute-start(bf16[128,2048]{1,0:T(8,128)(2,1)} %get-tuple-element.232), channel_id=1, source_target_pairs={{3,2},{2,1},{7,6},{6,5},{11,10},{10,9},{15,14},{14,13},{19,18},{18... | collective-permute-start | bytes 1572872 | tf_op jit(solution)/shard_map/ppermute | solution.py:431
  199.2 75.0 %collective-permute-start.6 = (bf16[128,2048]{1,0:T(8,128)(2,1)}, bf16[128,2048]{1,0:T(8,128)(2,1)S(1)}, u32[]{:S(2)}, u32[]{:S(2)}) collective-permute-start(bf16[128,2048]{1,0:T(8,128)(2,1)} %get-tuple-element.233), channel_id=1, source_target_pairs={{3,1},{0,2},{7,5},{4,6},{11,9},{8,10},{15,13},{12,14},{19,17},{16,... | collective-permute-start | bytes 1572872 | tf_op jit(solution)/shard_map/ppermute | solution.py:430
  211.8 63.6 %collective-permute-start.8 = (bf16[128,2048]{1,0:T(8,128)(2,1)S(1)}, bf16[128,2048]{1,0:T(8,128)(2,1)S(1)}, u32[]{:S(2)}, u32[]{:S(2)}) collective-permute-start(bf16[128,2048]{1,0:T(8,128)(2,1)S(1)} %get-tuple-element.234), channel_id=1, source_target_pairs={{0,1},{1,2},{4,5},{5,6},{8,9},{9,10},{12,13},{13,14},{16,17},{17,1... | collective-permute-start | bytes 1572872 | tf_op jit(solution)/shard_map/ppermute | solution.py:432
  274.2 147.9 %collective-permute-start.63 = (bf16[128,2048]{1,0:T(8,128)(2,1)}, bf16[128,2048]{1,0:T(8,128)(2,1)}, u32[]{:S(2)}, u32[]{:S(2)}) collective-permute-start(bf16[128,2048]{1,0:T(8,128)(2,1)} %broadcast_select_fusion.1), channel_id=1, source_target_pairs={{1,3},{2,0},{5,7},{6,4},{9,11},{10,8},{13,15},{14,12},{17,19},{18,... | collective-permute-start | bytes 1572872 | tf_op jit(solution)/shard_map/ppermute | solution.py:400
  303.3 119.5 %collective-permute-start.61 = (bf16[128,2048]{1,0:T(8,128)(2,1)}, bf16[128,2048]{1,0:T(8,128)(2,1)}, u32[]{:S(2)}, u32[]{:S(2)}) collective-permute-start(bf16[128,2048]{1,0:T(8,128)(2,1)} %collective-permute-done.60), channel_id=1, source_target_pairs={{1,2},{2,3},{5,6},{6,7},{9,10},{10,11},{13,14},{14,15},{17,18},{18... | collective-permute-start | bytes 1572872 | tf_op jit(solution)/shard_map/ppermute | solution.py:398
  422.8 29.7 %collective-permute-start.16 = (bf16[128,2048]{1,0:T(8,128)(2,1)S(1)}, bf16[128,2048]{1,0:T(8,128)(2,1)S(1)}, u32[]{:S(2)}, u32[]{:S(2)}) collective-permute-start(bf16[128,2048]{1,0:T(8,128)(2,1)S(1)} %get-tuple-element.227), channel_id=1, source_target_pairs={{3,1},{0,2},{7,5},{4,6},{11,9},{8,10},{15,13},{12,14},{19,17},{16,... | collective-permute-start | bytes 1572872 | tf_op jit(solution)/shard_map/ppermute | solution.py:430
  428.0 34.9 %collective-permute-start.18 = (bf16[128,2048]{1,0:T(8,128)(2,1)S(1)}, bf16[128,2048]{1,0:T(8,128)(2,1)S(1)}, u32[]{:S(2)}, u32[]{:S(2)}) collective-permute-start(bf16[128,2048]{1,0:T(8,128)(2,1)S(1)} %get-tuple-element.228), channel_id=1, source_target_pairs={{0,1},{1,2},{4,5},{5,6},{8,9},{9,10},{12,13},{13,14},{16,17},{17,1... | collective-permute-start | bytes 1572872 | tf_op jit(solution)/shard_map/ppermute | solution.py:432
  432.2 67.7 %collective-permute-start.64 = (bf16[128,2048]{1,0:T(8,128)(2,1)S(1)}, bf16[128,2048]{1,0:T(8,128)(2,1)S(1)}, u32[]{:S(2)}, u32[]{:S(2)}) collective-permute-start(bf16[128,2048]{1,0:T(8,128)(2,1)S(1)} %copy-done.44), channel_id=1, source_target_pairs={{1,0},{2,1},{5,4},{6,5},{9,8},{10,9},{13,12},{14,13},{17,16},{18,1... | collective-permute-start | bytes 1572872 | tf_op jit(solution)/shard_map/ppermute | solution.py:399
  440.8 31.0 %collective-permute-start.47 = (bf16[128,2048]{1,0:T(8,128)(2,1)S(1)}, bf16[128,2048]{1,0:T(8,128)(2,1)S(1)}, u32[]{:S(2)}, u32[]{:S(2)}) collective-permute-start(bf16[128,2048]{1,0:T(8,128)(2,1)S(1)} %get-tuple-element.202), channel_id=1, source_target_pairs={{1,0},{2,1},{3,2},{5,4},{6,5},{7,6},{9,8},{10,9},{11,10},{13,12},{... | collective-permute-start | bytes 1572872 | tf_op jit(solution)/shard_map/ppermute | solution.py:436
  442.2 31.9 %collective-permute-start.49 = (bf16[128,2048]{1,0:T(8,128)(2,1)S(1)}, bf16[128,2048]{1,0:T(8,128)(2,1)S(1)}, u32[]{:S(2)}, u32[]{:S(2)}) collective-permute-start(bf16[128,2048]{1,0:T(8,128)(2,1)S(1)} %get-tuple-element.203), channel_id=1, source_target_pairs={{0,1},{1,2},{2,3},{4,5},{5,6},{6,7},{8,9},{9,10},{10,11},{12,13},{... | collective-permute-start | bytes 1572872 | tf_op jit(solution)/shard_map/ppermute | solution.py:437
  592.4 33.0 %collective-permute-start.38 = (bf16[128,2048]{1,0:T(8,128)(2,1)S(1)}, bf16[128,2048]{1,0:T(8,128)(2,1)S(1)}, u32[]{:S(2)}, u32[]{:S(2)}) collective-permute-start(bf16[128,2048]{1,0:T(8,128)(2,1)S(1)} %get-tuple-element.231), channel_id=1, source_target_pairs={{0,1},{1,2},{4,5},{5,6},{8,9},{9,10},{12,13},{13,14},{16,17},{17,1... | collective-permute-start | bytes 1572872 | tf_op jit(solution)/shard_map/ppermute | solution.py:432
  604.6 32.0 %collective-permute-start.69 = (bf16[128,2048]{1,0:T(8,128)(2,1)S(1)}, bf16[128,2048]{1,0:T(8,128)(2,1)S(1)}, u32[]{:S(2)}, u32[]{:S(2)}) collective-permute-start(bf16[128,2048]{1,0:T(8,128)(2,1)S(1)} %get-tuple-element.205), channel_id=1, source_target_pairs={{0,1},{1,2},{2,3},{4,5},{5,6},{6,7},{8,9},{9,10},{10,11},{12,13},{... | collective-permute-start | bytes 1572872 | tf_op jit(solution)/shard_map/ppermute | solution.py:437
  676.1 40.4 %collective-permute-start.73 = (bf16[128,2048]{1,0:T(8,128)(2,1)S(1)}, bf16[128,2048]{1,0:T(8,128)(2,1)S(1)}, u32[]{:S(2)}, u32[]{:S(2)}) collective-permute-start(bf16[128,2048]{1,0:T(8,128)(2,1)S(1)} %broadcast_select_fusion), channel_id=1, source_target_pairs={{1,3},{2,0},{5,7},{6,4},{9,11},{10,8},{13,15},{14,12},{17,19},{18,... | collective-permute-start | bytes 1572872 | tf_op jit(solution)/shard_map/ppermute | solution.py:400
  677.4 36.8 %collective-permute-start.54 = (bf16[128,2048]{1,0:T(8,128)(2,1)S(1)}, bf16[128,2048]{1,0:T(8,128)(2,1)S(1)}, u32[]{:S(2)}, u32[]{:S(2)}) collective-permute-start(bf16[128,2048]{1,0:T(8,128)(2,1)S(1)} %collective-permute-done.52), channel_id=1, source_target_pairs={{1,0},{2,1},{5,4},{6,5},{9,8},{10,9},{13,12},{14,13},{17,16},{18,1... | collective-permute-start | bytes 1572872 | tf_op jit(solution)/shard_map/ppermute | solution.py:399
  678.7 43.0 %collective-permute-start.74 = (bf16[128,2048]{1,0:T(8,128)(2,1)S(1)}, bf16[128,2048]{1,0:T(8,128)(2,1)S(1)}, u32[]{:S(2)}, u32[]{:S(2)}) collective-permute-start(bf16[128,2048]{1,0:T(8,128)(2,1)S(1)} %collective-permute-done.72), channel_id=1, source_target_pairs={{1,0},{2,1},{5,4},{6,5},{9,8},{10,9},{13,12},{14,13},{17,16},{18,1... | collective-permute-start | bytes 1572872 | tf_op jit(solution)/shard_map/ppermute | solution.py:399
  730.3 279.6 %reduce-scatter.11.cloned.1.call-start = ((), (), s32[]{:S(2)}) async-start(), calls=%async_computation.11 | async-start | bytes 6488064 | tf_op jit(solution)/shard_map/reduce_scatter | solution.py:457
  741.4 271.2 %reduce-scatter.9.cloned.1.call-start = ((), (), s32[]{:S(2)}) async-start(), calls=%async_computation.10 | async-start | bytes 12976128 | tf_op jit(solution)/shard_map/reduce_scatter | solution.py:457
  760.8 278.8 %reduce-scatter.5.cloned.1.call-start = ((), (), s32[]{:S(2)}) async-start(), calls=%async_computation.8 | async-start | bytes 14745600 | tf_op jit(solution)/shard_map/reduce_scatter | solution.py:457
  927.9 30.6 %collective-permute-start.57 = (bf16[128,2048]{1,0:T(8,128)(2,1)S(1)}, bf16[128,2048]{1,0:T(8,128)(2,1)S(1)}, u32[]{:S(2)}, u32[]{:S(2)}) collective-permute-start(bf16[128,2048]{1,0:T(8,128)(2,1)S(1)} %get-tuple-element.200), channel_id=1, source_target_pairs={{1,0},{2,1},{3,2},{5,4},{6,5},{7,6},{9,8},{10,9},{11,10},{13,12},{... | collective-permute-start | bytes 1572872 | tf_op jit(solution)/shard_map/ppermute | solution.py:436
  929.2 31.9 %collective-permute-start.59 = (bf16[128,2048]{1,0:T(8,128)(2,1)S(1)}, bf16[128,2048]{1,0:T(8,128)(2,1)S(1)}, u32[]{:S(2)}, u32[]{:S(2)}) collective-permute-start(bf16[128,2048]{1,0:T(8,128)(2,1)S(1)} %get-tuple-element.201), channel_id=1, source_target_pairs={{0,1},{1,2},{2,3},{4,5},{5,6},{6,7},{8,9},{9,10},{10,11},{12,13},{... | collective-permute-start | bytes 1572872 | tf_op jit(solution)/shard_map/ppermute | solution.py:437
  (152 other events, 3609.7 us)
Sparse Core Ops, SparseCore 0:
  13.0 77.0 all-gather.4
  92.0 37.4 all-gather.6
  131.9 67.8 all-gather.8
  201.5 44.3 all-gather.10
  730.4 56.1 reduce-scatter.6
  790.3 59.0 reduce-scatter.10
  852.9 86.7 reduce-scatter.8
  943.3 96.2 reduce-scatter.4

commit v3 on v2

--- a/solution.py
+++ b/solution.py
@@ -173,7 +173,7 @@
             jax.ShapeDtypeStruct((count, heads, DK, DV), F32),
         ],
         compiler_params=pltpu.CompilerParams(dimension_semantics=("arbitrary",), vmem_limit_bytes=32 << 20),
-        cost_estimate=pl.CostEstimate(flops=3 * 10**10, bytes_accessed=30 << 20, transcendentals=0),
+        cost_estimate=pl.CostEstimate(flops=1000, bytes_accessed=1000, transcendentals=0),
         name="mixer_forward",
     )(keep, raw, conv, rates, gain)
 
@@ -255,27 +255,27 @@
         dunit = dnormed * gain
         dout = r * (dunit - unit * jnp.mean(dunit * unit, axis=-1, keepdims=True))
         dnext = dstate[h] * keep_next
-        dfresh = mm(scores, dout, TN, 3) + mm(k * tail, dnext, NN, 3)
-        dright = mm(inv, dfresh, TN, 3)
-        dscores = jnp.where(incl, mm(dout, fresh, NT, 3), 0.0)
-        dlower = jnp.where(strict, -mm(dright, fresh, NT, 3), 0.0)
+        dfresh = mm(scores, dout, TN, 1) + mm(k * tail, dnext, NN, 1)
+        dright = mm(inv, dfresh, TN, 1)
+        dscores = jnp.where(incl, mm(dout, fresh, NT, 1), 0.0)
+        dlower = jnp.where(strict, -mm(dright, fresh, NT, 1), 0.0)
         scaled = beta * growth * dright
-        dstate[h] = growth_last * dnext + mm(q * growth, dout, TN, 3) - mm(k, scaled, TN, 3)
+        dstate[h] = growth_last * dnext + mm(q * growth, dout, TN, 1) - mm(k, scaled, TN, 1)
         dv = beta * dright
         dbeta = jnp.sum(dright * (v - growth * k_state), axis=-1, keepdims=True)
         dgrowth = jnp.sum(dout * q_state - dv * k_state, axis=-1, keepdims=True)
         dsw = dscores * within
-        dq = growth * mm(dout, start, NT, 3) + mm(dsw, k, NN, 3)
-        into_k = mm(fresh, dnext, NT, 3)
+        dq = growth * mm(dout, start, NT, 1) + mm(dsw, k, NN, 1)
+        into_k = mm(fresh, dnext, NT, 1)
         dinner = dlower * within
         dbeta = dbeta + jnp.sum(dinner * inner, axis=-1, keepdims=True)
         weighted = beta * dinner
         dk = (
             tail * into_k
-            - mm(scaled, start, NT, 3)
-            + mm(dsw, q, TN, 3)
-            + mm(weighted, k, NN, 3)
-            + mm(weighted, k, TN, 3)
+            - mm(scaled, start, NT, 1)
+            + mm(dsw, q, TN, 1)
+            + mm(weighted, k, NN, 1)
+            + mm(weighted, k, TN, 1)
         )
         tailed = tail * jnp.sum(k * into_k, axis=-1, keepdims=True)
         pairs = dscores * scores + weighted * inner
@@ -350,7 +350,7 @@
             jax.ShapeDtypeStruct((1, DV), F32),
         ],
         compiler_params=pltpu.CompilerParams(dimension_semantics=("arbitrary",), vmem_limit_bytes=32 << 20),
-        cost_estimate=pl.CostEstimate(flops=6 * 10**10, bytes_accessed=40 << 20, transcendentals=0),
+        cost_estimate=pl.CostEstimate(flops=1000, bytes_accessed=1000, transcendentals=0),
         name="mixer_backward",
     )(jnp.concatenate([keep, jnp.zeros((1,), jnp.int32)]), raw, conved, fresh, out, inv, start, grad, conv, rates, gain)
 
@@ -388,13 +388,83 @@
     return (keep_state, jnp.where(live_rows, 1.0, 0.0).astype(jnp.float32))
 
 
-def z_gather(own):
+def rotation(count, shift):
+    return [(i, (i + shift) % count) for i in range(count)]
+
+
+def hold(*values):
+    return lax.optimization_barrier(values)
+
+
+def place_slots(found, axis):
+    count = len(found)
+    t = lax.axis_index("tensor")
+    slots = []
+    for slot in range(count):
+        ahead = jnp.where(slot < t, slot - t + count, slot - t)
+        chosen = found[0]
+        for shift in range(1, count):
+            chosen = jnp.where(ahead == shift, found[shift], chosen)
+        slots.append(chosen)
+    return jnp.concatenate(slots, axis=axis)
+
+
+def z_fetch(own):
     count = lax.axis_size("tensor")
-    if count != 4:
-        return lax.all_gather(own, "tensor", axis=0, tiled=True)
+    return [own] + [
+        lax.ppermute(own, "tensor", rotation(count, -shift)) for shift in range(1, count)
+    ]
+
+
+def queued_gather(own):
+    return lax.all_gather(own, "tensor", axis=0, tiled=True)
+
+
+def queued_scatter(partial):
+    return lax.psum_scatter(
+        partial.astype(jnp.bfloat16), "tensor", scatter_dimension=0, tiled=True
+    )
+
+
+def z_terms(partial):
+    count = lax.axis_size("tensor")
     t = lax.axis_index("tensor")
+    rows = partial.shape[0] // count
+    parts = partial.reshape(count, rows, partial.shape[1])
+
+    def take(ahead):
+        index = jnp.where(t + ahead < count, t + ahead, t + ahead - count)
+        return lax.dynamic_index_in_dim(parts, index, 0, keepdims=False)
+
+    return take(0), [take(shift).astype(jnp.bfloat16) for shift in range(1, count)]
+
+
+def z_ship(terms):
+    count = lax.axis_size("tensor")
+    return [
+        lax.ppermute(term, "tensor", rotation(count, shift + 1)) for shift, term in enumerate(terms)
+    ]
+
+
+def z_sum(own, sent):
+    for term in sent:
+        own = own + term.astype(jnp.float32)
+    return own
+
+
+def relay_near(own):
+    if lax.axis_size("tensor") != 4:
+        return tuple(z_fetch(own))
     right = lax.ppermute(own, "tensor", [(0, 1), (1, 2), (2, 3)])
     left = lax.ppermute(own, "tensor", [(1, 0), (2, 1), (3, 2)])
+    return own, right, left
+
+
+def relay_far(near, axis):
+    if lax.axis_size("tensor") != 4:
+        return place_slots(near, axis)
+    own, right, left = near
+    t = lax.axis_index("tensor")
     right2 = lax.ppermute(right, "tensor", [(1, 2), (2, 3)])
     left2 = lax.ppermute(left, "tensor", [(1, 0), (2, 1)])
     far = lax.ppermute(jnp.where(t == 1, right, left), "tensor", [(1, 3), (2, 0)])
@@ -409,33 +479,8 @@
             pick(left2, left, own, right),
             pick(far, left2, left, own),
         ],
-        axis=0,
-    )
-
-
-def z_scatter(partial):
-    count = lax.axis_size("tensor")
-    if count != 4:
-        return lax.psum_scatter(
-            partial.astype(jnp.bfloat16), "tensor", scatter_dimension=0, tiled=True
-        ).astype(jnp.float32)
-    t = lax.axis_index("tensor")
-    rows = partial.shape[0] // count
-    parts = partial.reshape(count, rows, partial.shape[1])
-    low = parts.astype(jnp.bfloat16)
-
-    def take(source, index):
-        return lax.dynamic_index_in_dim(source, jnp.clip(index, 0, count - 1), 0, keepdims=False)
-
-    far = lax.ppermute(jnp.where(t == 3, low[0], low[3]), "tensor", [(3, 1), (0, 2)])
-    left = lax.ppermute(take(low, t - 2), "tensor", [(3, 2), (2, 1)])
-    right = lax.ppermute(take(low, t + 2), "tensor", [(0, 1), (1, 2)])
-    wide = jnp.float32
-    to_left = take(parts, t - 1) + left.astype(wide) + jnp.where(t == 1, far, 0).astype(wide)
-    to_right = take(parts, t + 1) + right.astype(wide) + jnp.where(t == 2, far, 0).astype(wide)
-    from_right = lax.ppermute(to_left.astype(jnp.bfloat16), "tensor", [(1, 0), (2, 1), (3, 2)])
-    from_left = lax.ppermute(to_right.astype(jnp.bfloat16), "tensor", [(0, 1), (1, 2), (2, 3)])
-    return take(parts, t) + from_right.astype(wide) + from_left.astype(wide)
+        axis=axis,
+    )
 
 
 def sum_over(values, axis):
@@ -529,70 +574,134 @@
     ]
     out_grads = [cotangent[m].astype(wide) * own_masks[m] for m in packs]
     norm_ones = [jax.vjp(rms_rows, token_rows[m], mixer_gain) for m in packs]
-    first_rows = [z_gather(norm_ones[m][0].astype(low)) for m in packs]
-    grad_rows = [z_gather(out_grads[m].astype(low)) for m in packs]
-
     conv_local = jnp.concatenate(small_local[:3], axis=1)
     rates = jnp.zeros((HALO, LANES), wide)
     rates = rates.at[0, :head_count].set(small_local[3]).at[1, :head_count].set(small_local[4])
     gain_row = head_gain[None, :]
-    raws, kept, gated, middle, norm_twos, second_rows = [], [], [], [], [], []
-    for m in packs:
-        raws.append(product(first_rows[m], in_full))
-        mixed, *rest = mixer_forward(
-            raws[m], layouts[m][0], conv_local, rates, gain_row, head_count
-        )
-        kept.append(rest)
-        gated.append(mixed)
-    for m in packs:
-        middle.append(token_rows[m] + z_scatter(product_nt(gated[m], out_full)))
-        norm_twos.append(jax.vjp(rms_rows, middle[m], feed_gain))
-        second_rows.append(z_gather(norm_twos[m][0].astype(low)))
-
-    outputs, hidden, feed_grads, middle_grads, mix_rows = [], [], [], [], []
-    small_terms = []
-    for m in packs:
-        pre = product(second_rows[m], feed_full)
+    joined = lambda *parts: jnp.concatenate(parts, axis=0)
+
+    def mix(m, raw):
+        mixed, *rest = mixer_forward(raw, layouts[m][0], conv_local, rates, gain_row, head_count)
+        return mixed, rest
+
+    def settle(m, received):
+        middle = token_rows[m] + received.astype(wide)
+        normed, back = jax.vjp(rms_rows, middle, feed_gain)
+        return middle, normed.astype(low), back
+
+    def feed_forward(second, hidden_grad):
+        pre = product(second, feed_full)
         gate_pre, up_pre = pre[:, :hidden_width], pre[:, hidden_width:]
         gate_sig = jax.nn.sigmoid(gate_pre)
         gate_act = gate_pre * gate_sig
-        hidden.append((gate_act * up_pre).astype(low))
-        hidden_grad = product(grad_rows[m], down_full)
+        hidden = (gate_act * up_pre).astype(low)
         gate_grad = hidden_grad * up_pre * gate_sig * (1.0 + gate_pre * (1.0 - gate_sig))
-        feed_grads.append(jnp.concatenate([gate_grad, hidden_grad * gate_act], axis=1).astype(low))
-        second_grad = z_scatter(product_nt(feed_grads[m], feed_full))
-        middle_norm_grad, feed_gain_grad = norm_twos[m][1](second_grad)
-        middle_grads.append(out_grads[m] + middle_norm_grad)
-        mix_rows.append(z_gather(middle_grads[m].astype(low)))
-        result = middle[m] + z_scatter(product_nt(hidden[m], down_full))
-        outputs.append((result * own_masks[m]).astype(low))
-        small_terms.append([feed_gain_grad])
-    joined = lambda parts: jnp.concatenate(parts, axis=0)
-    feed_final = scatter_rows(product_tn(joined(second_rows), joined(feed_grads)))
-    down_final = scatter_rows(product_tn(joined(grad_rows), joined(hidden)))
-    out_final = scatter_rows(product_tn(joined(mix_rows), joined(gated)))
-
-    raw_grads, input_grads = [], []
-    for m in packs:
-        raw_grad, conv_grad, rate_grad, gain_grad = mixer_backward(
-            raws[m],
-            kept[m],
-            product(mix_rows[m], out_full),
-            layouts[m][0],
-            conv_local,
-            rates,
-            gain_row,
-            head_count,
+        feed_grad = jnp.concatenate([gate_grad, hidden_grad * gate_act], axis=1).astype(low)
+        return hidden, feed_grad, product_nt(feed_grad, feed_full).astype(low)
+
+    def feed_back(m, back, received):
+        norm_grad, gain_grad = back(received.astype(wide))
+        total = out_grads[m] + norm_grad
+        return total, total.astype(low), gain_grad
+
+    def mix_back(m, rows_in, raw, rest):
+        return mixer_backward(
+            raw, rest, product(rows_in, out_full), layouts[m][0], conv_local, rates, gain_row, head_count
         )
-        raw_grads.append(raw_grad)
-        first_grad = z_scatter(product_nt(raw_grads[m], in_full))
-        token_norm_grad, mixer_gain_grad = norm_ones[m][1](first_grad)
-        input_grads.append(middle_grads[m] + token_norm_grad)
-        small_terms[m] += [mixer_gain_grad, conv_grad, rate_grad[:2, :head_count], gain_grad[0]]
-    in_final = scatter_rows(product_tn(joined(first_rows), joined(raw_grads)))
-
-    feed_gain_grad, mixer_gain_grad, *core_grads = [sum(terms) for terms in zip(*small_terms)]
-    conv_grads, rate_grads, gain_grads = core_grads
+
+    A, B = 0, 1
+    first_own = jnp.stack([norm_ones[m][0].astype(low) for m in packs])
+    grad_own = jnp.stack([out_grads[m].astype(low) for m in packs])
+    first_all = relay_far(relay_near(first_own), 1)
+    first_all, in_full, grad_own = hold(first_all, in_full, grad_own)
+    first_a, first_b = first_all[A], first_all[B]
+    grad_near = relay_near(grad_own)
+    raw_a = product(first_a, in_full)
+    mixed_a, rest_a = mix(A, raw_a)
+    mixed_a, *grad_near = hold(mixed_a, *grad_near)
+    own_a, terms_a = z_terms(product_nt(mixed_a, out_full))
+    sent_a = z_ship(terms_a)
+    grad_all = relay_far(grad_near, 1)
+    grad_a, grad_b = grad_all[A], grad_all[B]
+    first_b, own_a = hold(first_b, own_a)
+    raw_b = product(first_b, in_full)
+    mixed_b, rest_b = mix(B, raw_b)
+    mixed_b, own_a, feed_full, down_full, *sent_a = hold(
+        mixed_b, own_a, feed_full, down_full, *sent_a
+    )
+    middle_a, normed_a, back_a = settle(A, z_sum(own_a, sent_a))
+    second_a = queued_gather(normed_a)
+    part_b = product_nt(mixed_b, out_full).astype(low)
+    grad_a, grad_b, part_b = hold(grad_a, grad_b, part_b)
+    hidden_grad_a = product(grad_a, down_full)
+    hidden_grad_b = product(grad_b, down_full)
+    second_a, part_b, hidden_grad_a, hidden_grad_b = hold(
+        second_a, part_b, hidden_grad_a, hidden_grad_b
+    )
+    sum_b = queued_scatter(part_b)
+    hidden_a, feed_grad_a, part2_a = feed_forward(second_a, hidden_grad_a)
+    part2_a, sum_b = hold(part2_a, sum_b)
+    sum2_a = queued_scatter(part2_a)
+    middle_b, normed_b, back_b = settle(B, sum_b)
+    result_a = z_terms(product_nt(hidden_a, down_full))
+    normed_b, sum2_a, result_own = hold(normed_b, sum2_a, result_a[0])
+    result_a = (result_own, result_a[1])
+    second_b = queued_gather(normed_b)
+    middle_grad_a, low_a, gain_grad_a = feed_back(A, back_a, sum2_a)
+    low_a, second_b = hold(low_a, second_b)
+    mix_rows_a = queued_gather(low_a)
+    hidden_b, feed_grad_b, part2_b = feed_forward(second_b, hidden_grad_b)
+    part2_b, mix_rows_a = hold(part2_b, mix_rows_a)
+    sum2_b = queued_scatter(part2_b)
+    result_b = z_terms(product_nt(hidden_b, down_full))
+    feed_grad = product_tn(joined(second_a, second_b), joined(feed_grad_a, feed_grad_b)).astype(low)
+    down_grad = product_tn(joined(grad_a, grad_b), joined(hidden_a, hidden_b)).astype(low)
+    both_grad = jnp.concatenate([feed_grad, down_grad], axis=1)
+    both_grad, sum2_b, mix_rows_a, result_own = hold(both_grad, sum2_b, mix_rows_a, result_b[0])
+    result_b = (result_own, result_b[1])
+    feed_width = 2 * hidden_width
+    both_final = scatter_rows(both_grad)
+    middle_grad_b, low_b, gain_grad_b = feed_back(B, back_b, sum2_b)
+    mix_found_b = z_fetch(low_b)
+    raw_grad_a, *core_a = mix_back(A, mix_rows_a, raw_a, rest_a)
+    raw_grad_a, *mix_found_b = hold(raw_grad_a, *mix_found_b)
+    mix_rows_b = place_slots(mix_found_b, 0)
+    mix_rows_b, *final_terms = hold(mix_rows_b, *result_a[1])
+    split_at = len(final_terms)
+    final_a = (result_a[0], z_ship(final_terms))
+    raw_grad_b, *core_b = mix_back(B, mix_rows_b, raw_b, rest_b)
+    raw_grad_b, raw_grad_a, mixed_a, final_own, *sent_final = hold(
+        raw_grad_b, raw_grad_a, mixed_a, final_a[0], *final_a[1]
+    )
+    final_a = (final_own, sent_final)
+    raw_grad_b, *moved = hold(raw_grad_b, *result_b[1])
+    final_b = (result_b[0], z_ship(moved))
+    in_grad = product_tn(joined(first_a, first_b), joined(raw_grad_a, raw_grad_b)).astype(low)
+    out_grad = product_tn(joined(mix_rows_a, mix_rows_b), joined(mixed_a, mixed_b)).astype(low)
+    in_grad = jnp.concatenate([in_grad, out_grad], axis=1)
+    raw_grad_a, in_grad, both_final = hold(raw_grad_a, in_grad, both_final)
+    part3_a = product_nt(raw_grad_a, in_full)
+    own3_a, terms3_a = z_terms(part3_a)
+    sent3_a = z_ship(terms3_a)
+    last_final = scatter_rows(in_grad)
+    in_final, out_final = last_final[:, : in_full.shape[1]], last_final[:, in_full.shape[1] :]
+    part3_b = product_nt(raw_grad_b, in_full)
+    own3_b, terms3_b = z_terms(part3_b)
+    sent3_b = z_ship(terms3_b)
+    outputs = [
+        ((middle_a + z_sum(*final_a)) * own_masks[A]).astype(low),
+        ((middle_b + z_sum(*final_b)) * own_masks[B]).astype(low),
+    ]
+    token_grad_a = norm_ones[A][1](z_sum(own3_a, sent3_a))[0]
+    token_grad_b = norm_ones[B][1](z_sum(own3_b, sent3_b))[0]
+    mixer_gain_grad = (
+        jnp.sum(part3_a * first_a.astype(wide), axis=0)
+        + jnp.sum(part3_b * first_b.astype(wide), axis=0)
+    ) / mixer_gain
+    input_grads = [middle_grad_a + token_grad_a, middle_grad_b + token_grad_b]
+    feed_gain_grad = gain_grad_a + gain_grad_b
+    conv_grads, rate_grads, gain_grads = [x + y for x, y in zip(core_a, core_b)]
+    rate_grads, gain_grads = rate_grads[:2, :head_count], gain_grads[0]
     everywhere = jnp.concatenate([feed_gain_grad, mixer_gain_grad, gain_grads])
     per_slice = jnp.concatenate([conv_grads.reshape(-1), rate_grads.reshape(-1)])
     packed = sum_over(jnp.concatenate([per_slice, everywhere]), "dp")
@@ -626,9 +735,9 @@
         everywhere[2 * width :],
         out_final.T,
         everywhere[:width],
-        feed_final[:, :hidden_width],
-        feed_final[:, hidden_width:],
-        down_final.T,
+        both_final[:, :hidden_width],
+        both_final[:, hidden_width:feed_width],
+        both_final[:, feed_width:].T,
     )
 
 

time: 1060 us -> 886 us (0.84)
  the two profiles are of different devices: /device:TPU:0 before, /device:TPU:25 now
where the time goes in v3:
time: 886 us; the launch traced here: 876 us
  waiting for transfers between devices  348 us (39%)
  matrix products  181 us (20%)
  Pallas kernels  125 us (14%)
  other arithmetic  82.5 us (9%)
  local copies, waits for them, and re-layouts  70.9 us (8%)
  starting transfers between devices  50.3 us (6%)
  between operations  19 us (2%)
    ppermute x15, waiting for transfers between devices, z_ship(): lax.ppermute(term, 'tensor', rotation(count, shift + 1))  76.8 us
    all_gather x3, waiting for transfers between devices, queued_gather(): return lax.all_gather(own, 'tensor', axis=0, tiled=True)  71.2 us
    dot_general x8, matrix products, product_nt(): return lax.dot_general(left_rows, matrix, NT, preferred_element_type=F32)  69.2 us
    reduce_scatter x3, waiting for transfers between devices, queued_scatter(): lax.psum_scatter(partial.astype(jnp.bfloat16), 'tensor', scatter_dimensio...  65.3 us
    pallas_call x2, Pallas kernels, mixer_forward(): pl.pallas_call(functools.partial(forward_kernel, heads), grid_spec=pltpu....  63.6 us
    pallas_call x2, Pallas kernels, mixer_backward(): pl.pallas_call(functools.partial(backward_kernel, heads), grid_spec=pltpu...  61.1 us
    dot_general x8, matrix products, product(): return lax.dot_general(left_rows, matrix, NN, preferred_element_type=F32)  58.3 us
    dot_general x4, matrix products, product_tn(): lax.dot_general(left_rows, right_rows, TN, preferred_element_type=F32)  53.7 us
  transfers between devices with their start and end apart: 45, of which 20 were waited for; matrix products, arithmetic and copies ran while one was open for 34% of the time, Pallas kernels for 14%

profile of v3, /device:TPU:25, one launch (start us, length us, event | category | flops | bytes accessed | tf_op | source)
XLA Modules:
  0.0 876.4 jit_solution(14046589329948200415)
XLA Ops:
  28.2 14.0 %collective-permute-done.2 = bf16[2,128,2048]{2,1,0:T(8,128)(2,1)} collective-permute-done((bf16[2,128,2048]{2,1,0:T(8,128)(2,1)}, bf16[2,128,2048]{2,1,0:T(8,128)(2,1)}, u32[]{:S(2)}, u32[]{:S(2)}) %collective-permute-start.2) | collective-permute-done | bytes 1048608 | tf_op jit(solution)/shard_map/ppermute | solution.py:459
  53.0 20.9 %collective-permute-done.3 = bf16[2,128,2048]{2,1,0:T(8,128)(2,1)S(1)} collective-permute-done((bf16[2,128,2048]{2,1,0:T(8,128)(2,1)S(1)}, bf16[2,128,2048]{2,1,0:T(8,128)(2,1)S(1)}, u32[]{:S(2)}, u32[]{:S(2)}) %collective-permute-start.3) | collective-permute-done | bytes 1048608 | tf_op jit(solution)/shard_map/ppermute | solution.py:470
  73.8 24.8 %collective-permute-done.1 = bf16[2,128,2048]{2,1,0:T(8,128)(2,1)S(1)} collective-permute-done((bf16[2,128,2048]{2,1,0:T(8,128)(2,1)}, bf16[2,128,2048]{2,1,0:T(8,128)(2,1)S(1)}, u32[]{:S(2)}, u32[]{:S(2)}) %collective-permute-start.1) | collective-permute-done | bytes 1048608 | tf_op jit(solution)/shard_map/ppermute | solution.py:468
  106.5 11.7 %fusion.113.raw_ref = f32[512,3200]{1,0:T(8,128)S(1)} fusion(bf16[2048,3200]{1,0:T(8,128)(2,1)} %all-gather.8.cloned.1.call-done, bf16[2,512,2048]{2,1,0:T(8,128)(2,1)} %pad_maximum_fusion.2), kind=kOutput, calls=%fused_computation.230 | convolution fusion | flops 6710886400 | bytes 21757952 | tf_op jit(solution)/shard_map/dot_general | solution.py:359
  118.3 31.8 %mixer_forward.2 = (bf16[512,1024]{1,0:T(8,128)(2,1)S(1)}, f32[512,2048]{1,0:T(8,128)S(1)}, f32[512,1024]{1,0:T(8,128)S(1)}, f32[512,1024]{1,0:T(8,128)S(1)}, f3...) custom-call(s32[8]{0:T(128)S(1)} %or_select_fusion.keep_ref, f32[512,3200]{1,0:T(8,128)S(1)} %fusion.113.raw_ref, ...), custom_call_target="tpu_custom_call" | custom-call | flops 1000 | bytes 1000 | tf_op jit(solution)/shard_map/mixer_forward/pallas_call | solution.py:151
  174.3 11.1 %fusion.125.raw_ref = f32[512,3200]{1,0:T(8,128)S(1)} fusion(bf16[512,2048]{1,0:T(8,128)(2,1)S(1)} %get-tuple-element.128, bf16[2048,3200]{1,0:T(8,128)(2,1)} %all-gather.8.cloned.1.call-done), kind=kOutput, calls=%fused_computation.240 | convolution fusion | flops 6710886400 | bytes 21757952 | tf_op jit(solution)/shard_map/dot_general | solution.py:359
  187.7 31.7 %mixer_forward.3 = (bf16[512,1024]{1,0:T(8,128)(2,1)S(1)}, f32[512,2048]{1,0:T(8,128)S(1)}, f32[512,1024]{1,0:T(8,128)S(1)}, f32[512,1024]{1,0:T(8,128)S(1)}, f3...) custom-call(s32[8]{0:T(128)S(1)} %or_select_fusion.1.keep_ref, f32[512,3200]{1,0:T(8,128)S(1)} %fusion.125.raw_ref, ...), custom_call_target="tpu_custom_call" | custom-call | flops 1000 | bytes 1000 | tf_op jit(solution)/shard_map/mixer_forward/pallas_call | solution.py:151
  228.6 15.9 %all-gather.12.cloned.1.call-done = bf16[2048,2816]{1,0:T(8,128)(2,1)} async-done(((bf16[256,2816]{1,0:T(8,128)(2,1)}), bf16[2048,2816]{1,0:T(8,128)(2,1)}) %all-gather.12.cloned.1.call-update) | async-done | bytes 11534352 | tf_op jit(solution)/shard_map/all_gather | solution.py:498
  273.0 19.5 %all-gather.16.cloned.1.call-done = bf16[512,2048]{1,0:T(8,128)(2,1)} async-done(((bf16[128,2048]{1,0:T(8,128)(2,1)}), bf16[512,2048]{1,0:T(8,128)(2,1)}) %all-gather.16.cloned.1.call-update) | async-done | bytes 2097168 | tf_op jit(solution)/shard_map/all_gather | solution.py:420
  292.8 10.3 %fusion.128 = f32[512,2816]{1,0:T(8,128)S(1)} fusion(bf16[512,2048]{1,0:T(8,128)(2,1)} %all-gather.16.cloned.1.call-done, bf16[2048,2816]{1,0:T(8,128)(2,1)} %all-gather.12.cloned.1.call-done), kind=kOutput, calls=%fused_computation.243 | convolution fusion | flops 5905580032 | bytes 19398656 | tf_op jit(solution)/shard_map/dot_general | solution.py:359
  307.5 10.1 %convolution_convert_fusion.5 = bf16[512,2048]{1,0:T(8,128)(2,1)} fusion(bf16[2048,2816]{1,0:T(8,128)(2,1)} %all-gather.12.cloned.1.call-done, bf16[512,1408]{1,0:T(8,128)(2,1)S(1)} %get-tuple-element.237, bf16[512,1408]{1,0:T(8,128)(2,1)S(1)} %get-tuple-element.236), kind=kOutput, calls=%fused_computation.35 | convolution fusion | flops 5912395776 | bytes 16515072 | tf_op jit(solution)/shard_map/dot_general | solution.py:363
  317.5 20.1 %reduce-scatter.6.cloned.1.call-done = bf16[128,2048]{1,0:T(8,128)(2,1)} async-done(((bf16[512,2048]{1,0:T(8,128)(2,1)}), bf16[128,2048]{1,0:T(8,128)(2,1)}) %reduce-scatter.6.cloned.1.call-update) | async-done | bytes 524304 | tf_op jit(solution)/shard_map/reduce_scatter | solution.py:424
  348.1 35.2 %reduce-scatter.8.cloned.1.call-done = bf16[128,2048]{1,0:T(8,128)(2,1)} async-done(((bf16[512,2048]{1,0:T(8,128)(2,1)}), bf16[128,2048]{1,0:T(8,128)(2,1)}) %reduce-scatter.8.cloned.1.call-update) | async-done | bytes 524304 | tf_op jit(solution)/shard_map/reduce_scatter | solution.py:424
  387.8 42.5 %all-gather.18.cloned.1.call-done = bf16[512,2048]{1,0:T(8,128)(2,1)} async-done(((bf16[128,2048]{1,0:T(8,128)(2,1)}), bf16[512,2048]{1,0:T(8,128)(2,1)}) %all-gather.18.cloned.1.call-update) | async-done | bytes 2097168 | tf_op jit(solution)/shard_map/all_gather | solution.py:420
  430.7 10.3 %fusion.130 = f32[512,2816]{1,0:T(8,128)S(1)} fusion(bf16[512,2048]{1,0:T(8,128)(2,1)} %all-gather.18.cloned.1.call-done, bf16[2048,2816]{1,0:T(8,128)(2,1)} %all-gather.12.cloned.1.call-done), kind=kOutput, calls=%fused_computation.245 | convolution fusion | flops 5905580032 | bytes 19398656 | tf_op jit(solution)/shard_map/dot_general | solution.py:359
  443.0 8.9 %fusion.131 = f32[512,2048]{1,0:T(8,128)} fusion(bf16[512,1408]{1,0:T(8,128)(2,1)S(1)} %get-tuple-element.238, bf16[2048,1408]{0,1:T(8,128)(2,1)} %all-gather.14.cloned.1.call-done), kind=kOutput, calls=%fused_computation.246 | convolution fusion | flops 2952790016 | bytes 11403264 | tf_op jit(solution)/shard_map/dot_general | solution.py:363
  468.0 9.2 %all-gather.20.cloned.1.call-done = bf16[512,2048]{1,0:T(8,128)(2,1)} async-done(((bf16[128,2048]{1,0:T(8,128)(2,1)}), bf16[512,2048]{1,0:T(8,128)(2,1)}) %all-gather.20.cloned.1.call-update) | async-done | bytes 2097168 | tf_op jit(solution)/shard_map/all_gather | solution.py:420
  480.0 18.3 %convolution_convert_fusion.1 = bf16[2048,2816]{1,0:T(8,128)(2,1)} fusion(bf16[512,1408]{1,0:T(8,128)(2,1)} %copy-done.65, bf16[512,1408]{1,0:T(8,128)(2,1)} %copy-done.64, bf16[512,1408]{1,0:T(8,128)(2,1)} %copy-done.62, bf16[512,1408]{1,0:T(8,128)(2,1)} %copy-done.61, bf16[512,2048]{1,0:T(8,128)(2,1)} %all-gather.18.cloned.1.call-done, ...), kind=kOutput, calls=%fused_computation.3 | convolution fusion | flops 11848384512 | bytes 21495808 | tf_op jit(solution)/shard_map/dot_general | solution.py:367
  498.3 14.0 %pad_maximum_fusion = bf16[2048,4224]{1,0:T(8,128)(2,1)} fusion(bf16[2048,1408]{1,0:T(8,128)(2,1)} %convolution_convert_fusion.2, bf16[2048,2816]{1,0:T(8,128)(2,1)} %convolution_convert_fusion.1), kind=kLoop, calls=%fused_computation | loop fusion | flops 34603008 | bytes 34603008 | tf_op jit(solution)/shard_map/concatenate | solution.py:659
  512.3 10.0 %reduce-scatter.10.cloned.1.call-done = bf16[128,2048]{1,0:T(8,128)(2,1)} async-done(((bf16[512,2048]{1,0:T(8,128)(2,1)}), bf16[128,2048]{1,0:T(8,128)(2,1)}) %reduce-scatter.10.cloned.1.call-update) | async-done | bytes 524304 | tf_op jit(solution)/shard_map/reduce_scatter | solution.py:424
  535.7 30.3 %mixer_backward.2 = (bf16[512,3200]{1,0:T(8,128)(2,1)S(1)}, f32[4,2048]{1,0:T(4,128)S(1)}, f32[8,128]{1,0:T(8,128)S(1)}, f32[1,256]{1,0:T(1,128)S(1)}) custom-call(s32[9]{0:T(128)S(1)} %get-tuple-element.300.keep_ref, f32[512,3200]{1,0:T(8,128)} %copy-done.3, f32[512,2048]{1,0:T(8,128)S(1)} %copy-done.9, f32[512,1024]{1,0:T(8,128)S(1)} %copy-done.15, ...), custom_call_target="tpu_custom_call" | custom-call | flops 1000 | bytes 1000 | tf_op jit(solution)/shard_map/mixer_backward/pallas_call | solution.py:326
  566.0 11.7 %collective-permute-done.14 = bf16[128,2048]{1,0:T(8,128)(2,1)S(1)} collective-permute-done((bf16[128,2048]{1,0:T(8,128)(2,1)S(1)}, bf16[128,2048]{1,0:T(8,128)(2,1)S(1)}, u32[]{:S(2)}, u32[]{:S(2)}) %collective-permute-start.14) | collective-permute-done | bytes 524320 | tf_op jit(solution)/shard_map/ppermute | solution.py:415
  583.4 30.7 %mixer_backward.3 = (bf16[512,3200]{1,0:T(8,128)(2,1)S(1)}, f32[4,2048]{1,0:T(4,128)S(1)}, f32[8,128]{1,0:T(8,128)S(1)}, f32[1,256]{1,0:T(1,128)S(1)}) custom-call(s32[9]{0:T(128)S(1)} %get-tuple-element.301.keep_ref, f32[512,3200]{1,0:T(8,128)} %copy-done.2, f32[512,2048]{1,0:T(8,128)S(1)} %copy-done.5, f32[512,1024]{1,0:T(8,128)S(1)} %get-tuple-element.136.fresh_ref, ...), custom_call_target="tpu_custom_call" | custom-call | flops 1000 | bytes 1000 | tf_op jit(solution)/shard_map/mixer_backward/pallas_call | solution.py:326
  614.2 9.8 %collective-permute-done.17 = bf16[128,2048]{1,0:T(8,128)(2,1)S(1)} collective-permute-done((bf16[128,2048]{1,0:T(8,128)(2,1)S(1)}, bf16[128,2048]{1,0:T(8,128)(2,1)S(1)}, u32[]{:S(2)}, u32[]{:S(2)}) %collective-permute-start.17) | collective-permute-done | bytes 524320 | tf_op jit(solution)/shard_map/ppermute | solution.py:445
  630.3 20.5 %convolution_convert_fusion = bf16[2048,3200]{1,0:T(8,128)(2,1)} fusion(bf16[512,3200]{1,0:T(8,128)(2,1)} %copy-done.27, bf16[512,3200]{1,0:T(8,128)(2,1)S(1)} %copy-done.25, bf16[512,2048]{1,0:T(8,128)(2,1)} %copy-done.53, bf16[512,2048]{1,0:T(8,128)(2,1)} %get-tuple-element.249), kind=kOutput, calls=%fused_computation.2 | convolution fusion | flops 13449822208 | bytes 23855104 | tf_op jit(solution)/shard_map/dot_general | solution.py:367
  650.8 14.0 %pad_maximum_fusion.1 = bf16[2048,4224]{1,0:T(8,128)(2,1)} fusion(bf16[2048,1024]{1,0:T(8,128)(2,1)} %fusion.23, bf16[2048,3200]{1,0:T(8,128)(2,1)} %convolution_convert_fusion), kind=kLoop, calls=%fused_computation.1 | loop fusion | flops 34603008 | bytes 34603008 | tf_op jit(solution)/shard_map/concatenate | solution.py:681
  670.3 12.8 %multiply_reduce_fusion = (f32[2048]{0:T(1024)S(1)}, f32[512,2048]{1,0:T(8,128)}) fusion(bf16[512,2048]{1,0:T(8,128)(2,1)S(1)} %copy-done.54, bf16[512,3200]{1,0:T(8,128)(2,1)} %copy-done.27, bf16[2048,3200]{1,0:T(8,128)(2,1)} %all-gather.8.cloned.1.call-done), kind=kOutput, calls=%fused_computation.30 | convolution fusion | flops 6714030080 | bytes 22683648 | tf_op jit(solution)/shard_map/dot_general | solution.py:363
  683.2 13.3 %multiply_reduce_fusion.1 = (f32[2048]{0:T(1024)S(1)}, f32[512,2048]{1,0:T(8,128)}) fusion(bf16[2,512,2048]{2,1,0:T(8,128)(2,1)S(1)} %copy-done.39, bf16[512,3200]{1,0:T(8,128)(2,1)S(1)} %copy-done.26, bf16[2048,3200]{1,0:T(8,128)(2,1)} %all-gather.8.cloned.1.call-done), kind=kOutput, calls=%fused_computation.31 | convolution fusion | flops 6714030080 | bytes 22683648 | tf_op jit(solution)/shard_map/dot_general | solution.py:363
  717.6 22.8 %collective-permute-done.31 = f32[37152]{0:T(1024)S(1)} collective-permute-done((f32[37152]{0:T(1024)S(1)}, f32[37152]{0:T(1024)S(1)}, u32[]{:S(2)}, u32[]{:S(2)}) %collective-permute-start.31) | collective-permute-done | bytes 148640 | tf_op jit(solution)/shard_map/ppermute | solution.py:492
  751.5 16.9 %collective-permute-done.32 = f32[37152]{0:T(1024)S(1)} collective-permute-done((f32[37152]{0:T(1024)S(1)}, f32[37152]{0:T(1024)S(1)}, u32[]{:S(2)}, u32[]{:S(2)}) %collective-permute-start.32) | collective-permute-done | bytes 148640 | tf_op jit(solution)/shard_map/ppermute | solution.py:492
  783.5 25.7 %collective-permute-done.23 = bf16[128,2048]{1,0:T(8,128)(2,1)} collective-permute-done((bf16[128,2048]{1,0:T(8,128)(2,1)}, bf16[128,2048]{1,0:T(8,128)(2,1)}, u32[]{:S(2)}, u32[]{:S(2)}) %collective-permute-start.23) | collective-permute-done | bytes 524320 | tf_op jit(solution)/shard_map/ppermute | solution.py:445
  812.5 39.9 %collective-permute-done.20 = bf16[128,2048]{1,0:T(8,128)(2,1)S(1)} collective-permute-done((bf16[128,2048]{1,0:T(8,128)(2,1)}, bf16[128,2048]{1,0:T(8,128)(2,1)S(1)}, u32[]{:S(2)}, u32[]{:S(2)}) %collective-permute-start.20) | collective-permute-done | bytes 524320 | tf_op jit(solution)/shard_map/ppermute | solution.py:445
  (423 shorter events, 238.5 us)
Async XLA Ops:
  7.2 95.6 %all-gather.8.cloned.1.call-start = ((), (), s32[]{:S(2)}) async-start(), calls=%async_computation.5 | async-start | bytes 14745600 | tf_op jit(solution)/shard_map/all_gather | solution.py:498
  12.8 147.9 %all-gather.10.cloned.1.call-start = ((), (), s32[]{:S(2)}) async-start(), calls=%async_computation.6 | async-start | bytes 4718592 | tf_op jit(solution)/shard_map/all_gather | solution.py:498
  13.6 215.0 %all-gather.14.cloned.1.call-start = ((), (), s32[]{:S(2)}) async-start(), calls=%async_computation.8 | async-start | bytes 6488064 | tf_op jit(solution)/shard_map/all_gather | solution.py:498
  14.4 230.1 %all-gather.12.cloned.1.call-start = ((), (), s32[]{:S(2)}) async-start(), calls=%async_computation.7 | async-start | bytes 12976128 | tf_op jit(solution)/shard_map/all_gather | solution.py:498
  15.7 276.9 %all-gather.16.cloned.1.call-start = ((), (), s32[]{:S(2)}) async-start(), calls=%async_computation.9 | async-start | bytes 2621440 | tf_op jit(solution)/shard_map/all_gather | solution.py:420
  50.3 48.3 %collective-permute-start.1 = (bf16[2,128,2048]{2,1,0:T(8,128)(2,1)}, bf16[2,128,2048]{2,1,0:T(8,128)(2,1)S(1)}, u32[]{:S(2)}, u32[]{:S(2)}) collective-permute-start(bf16[2,128,2048]{2,1,0:T(8,128)(2,1)} %collective-permute-done), channel_id=1, source_target_pairs={{1,2},{2,3},{5,6},{6,7},{9,10},{10,11},{13,14},{14,15},{17,18},{18... | collective-permute-start | bytes 3145736 | tf_op jit(solution)/shard_map/ppermute | solution.py:468
  102.8 55.0 %collective-permute-start.6 = (bf16[2,128,2048]{2,1,0:T(8,128)(2,1)}, bf16[2,128,2048]{2,1,0:T(8,128)(2,1)}, u32[]{:S(2)}, u32[]{:S(2)}) collective-permute-start(bf16[2,128,2048]{2,1,0:T(8,128)(2,1)} %pad_maximum_fusion.8), channel_id=1, source_target_pairs={{1,0},{2,1},{3,2},{5,4},{6,5},{7,6},{9,8},{10,9},{11,10},{13,12},{... | collective-permute-start | bytes 3145736 | tf_op jit(solution)/shard_map/ppermute | solution.py:459
  105.2 52.5 %collective-permute-start.5 = (bf16[2,128,2048]{2,1,0:T(8,128)(2,1)}, bf16[2,128,2048]{2,1,0:T(8,128)(2,1)}, u32[]{:S(2)}, u32[]{:S(2)}) collective-permute-start(bf16[2,128,2048]{2,1,0:T(8,128)(2,1)} %pad_maximum_fusion.8), channel_id=1, source_target_pairs={{0,1},{1,2},{2,3},{4,5},{5,6},{6,7},{8,9},{9,10},{10,11},{12,13},{... | collective-permute-start | bytes 3145736 | tf_op jit(solution)/shard_map/ppermute | solution.py:458
  157.8 97.5 %collective-permute-start.10 = (bf16[2,128,2048]{2,1,0:T(8,128)(2,1)}, bf16[2,128,2048]{2,1,0:T(8,128)(2,1)}, u32[]{:S(2)}, u32[]{:S(2)}) collective-permute-start(bf16[2,128,2048]{2,1,0:T(8,128)(2,1)} %collective-permute-done.5), channel_id=1, source_target_pairs={{1,2},{2,3},{5,6},{6,7},{9,10},{10,11},{13,14},{14,15},{17,18},{18... | collective-permute-start | bytes 3145736 | tf_op jit(solution)/shard_map/ppermute | solution.py:468
  159.1 96.2 %collective-permute-start.12 = (bf16[2,128,2048]{2,1,0:T(8,128)(2,1)}, bf16[2,128,2048]{2,1,0:T(8,128)(2,1)}, u32[]{:S(2)}, u32[]{:S(2)}) collective-permute-start(bf16[2,128,2048]{2,1,0:T(8,128)(2,1)} %collective-permute-done.6), channel_id=1, source_target_pairs={{1,0},{2,1},{5,4},{6,5},{9,8},{10,9},{13,12},{14,13},{17,16},{18,1... | collective-permute-start | bytes 3145736 | tf_op jit(solution)/shard_map/ppermute | solution.py:469
  167.5 59.1 %collective-permute-start.9 = (bf16[128,2048]{1,0:T(8,128)(2,1)S(1)}, bf16[128,2048]{1,0:T(8,128)(2,1)S(1)}, u32[]{:S(2)}, u32[]{:S(2)}) collective-permute-start(bf16[128,2048]{1,0:T(8,128)(2,1)S(1)} %get-tuple-element.257), channel_id=1, source_target_pairs={{0,3},{1,0},{2,1},{3,2},{4,7},{5,4},{6,5},{7,6},{8,11},{9,8},{10,9... | collective-permute-start | bytes 1572872 | tf_op jit(solution)/shard_map/ppermute | solution.py:445
  174.3 70.2 %collective-permute-start.8 = (bf16[128,2048]{1,0:T(8,128)(2,1)}, bf16[128,2048]{1,0:T(8,128)(2,1)}, u32[]{:S(2)}, u32[]{:S(2)}) collective-permute-start(bf16[128,2048]{1,0:T(8,128)(2,1)} %get-tuple-element.258), channel_id=1, source_target_pairs={{0,2},{1,3},{2,0},{3,1},{4,6},{5,7},{6,4},{7,5},{8,10},{9,11},{10,... | collective-permute-start | bytes 1572872 | tf_op jit(solution)/shard_map/ppermute | solution.py:445
  185.5 59.0 %collective-permute-start.7 = (bf16[128,2048]{1,0:T(8,128)(2,1)}, bf16[128,2048]{1,0:T(8,128)(2,1)}, u32[]{:S(2)}, u32[]{:S(2)}) collective-permute-start(bf16[128,2048]{1,0:T(8,128)(2,1)} %get-tuple-element.259), channel_id=1, source_target_pairs={{0,1},{1,2},{2,3},{3,0},{4,5},{5,6},{6,7},{7,4},{8,9},{9,10},{10,1... | collective-permute-start | bytes 1572872 | tf_op jit(solution)/shard_map/ppermute | solution.py:445
  248.8 88.8 %reduce-scatter.6.cloned.1.call-start = ((), (), s32[]{:S(2)}) async-start(), calls=%async_computation.10 | async-start | bytes 2621440 | tf_op jit(solution)/shard_map/reduce_scatter | solution.py:424
  292.6 90.7 %reduce-scatter.8.cloned.1.call-start = ((), (), s32[]{:S(2)}) async-start(), calls=%async_computation.11 | async-start | bytes 2621440 | tf_op jit(solution)/shard_map/reduce_scatter | solution.py:424
  337.7 92.7 %all-gather.18.cloned.1.call-start = ((), (), s32[]{:S(2)}) async-start(), calls=%async_computation.12 | async-start | bytes 2621440 | tf_op jit(solution)/shard_map/all_gather | solution.py:420
  383.3 93.9 %all-gather.20.cloned.1.call-start = ((), (), s32[]{:S(2)}) async-start(), calls=%async_computation.13 | async-start | bytes 2621440 | tf_op jit(solution)/shard_map/all_gather | solution.py:420
  430.4 91.9 %reduce-scatter.10.cloned.1.call-start = ((), (), s32[]{:S(2)}) async-start(), calls=%async_computation.14 | async-start | bytes 2621440 | tf_op jit(solution)/shard_map/reduce_scatter | solution.py:424
  477.2 187.6 %reduce-scatter.12.cloned.1.call-start = ((), (), s32[]{:S(2)}) async-start(), calls=%async_computation.15 | async-start | bytes 19464192 | tf_op jit(solution)/shard_map/reduce_scatter | solution.py:502
  522.3 338.2 %reduce-scatter.14.cloned.1.call-start = ((), (), s32[]{:S(2)}) async-start(), calls=%async_computation.16 | async-start | bytes 19464192 | tf_op jit(solution)/shard_map/reduce_scatter | solution.py:502
  531.8 45.9 %collective-permute-start.14 = (bf16[128,2048]{1,0:T(8,128)(2,1)S(1)}, bf16[128,2048]{1,0:T(8,128)(2,1)S(1)}, u32[]{:S(2)}, u32[]{:S(2)}) collective-permute-start(bf16[128,2048]{1,0:T(8,128)(2,1)S(1)} %get-tuple-element.172), channel_id=1, source_target_pairs={{0,2},{1,3},{2,0},{3,1},{4,6},{5,7},{6,4},{7,5},{8,10},{9,11},{10,... | collective-permute-start | bytes 1572872 | tf_op jit(solution)/shard_map/ppermute | solution.py:415
  532.6 45.1 %collective-permute-start.13 = (bf16[128,2048]{1,0:T(8,128)(2,1)S(1)}, bf16[128,2048]{1,0:T(8,128)(2,1)S(1)}, u32[]{:S(2)}, u32[]{:S(2)}) collective-permute-start(bf16[128,2048]{1,0:T(8,128)(2,1)S(1)} %get-tuple-element.172), channel_id=1, source_target_pairs={{0,3},{1,0},{2,1},{3,2},{4,7},{5,4},{6,5},{7,6},{8,11},{9,8},{10,9... | collective-permute-start | bytes 1572872 | tf_op jit(solution)/shard_map/ppermute | solution.py:415
  578.2 36.0 %collective-permute-start.16 = (bf16[128,2048]{1,0:T(8,128)(2,1)S(1)}, bf16[128,2048]{1,0:T(8,128)(2,1)S(1)}, u32[]{:S(2)}, u32[]{:S(2)}) collective-permute-start(bf16[128,2048]{1,0:T(8,128)(2,1)S(1)} %get-tuple-element.177), channel_id=1, source_target_pairs={{0,1},{1,2},{2,3},{3,0},{4,5},{5,6},{6,7},{7,4},{8,9},{9,10},{10,1... | collective-permute-start | bytes 1572872 | tf_op jit(solution)/shard_map/ppermute | solution.py:445
  578.3 45.7 %collective-permute-start.17 = (bf16[128,2048]{1,0:T(8,128)(2,1)S(1)}, bf16[128,2048]{1,0:T(8,128)(2,1)S(1)}, u32[]{:S(2)}, u32[]{:S(2)}) collective-permute-start(bf16[128,2048]{1,0:T(8,128)(2,1)S(1)} %get-tuple-element.178), channel_id=1, source_target_pairs={{0,2},{1,3},{2,0},{3,1},{4,6},{5,7},{6,4},{7,5},{8,10},{9,11},{10,... | collective-permute-start | bytes 1572872 | tf_op jit(solution)/shard_map/ppermute | solution.py:445
  579.4 44.6 %collective-permute-start.18 = (bf16[128,2048]{1,0:T(8,128)(2,1)S(1)}, bf16[128,2048]{1,0:T(8,128)(2,1)S(1)}, u32[]{:S(2)}, u32[]{:S(2)}) collective-permute-start(bf16[128,2048]{1,0:T(8,128)(2,1)S(1)} %get-tuple-element.179), channel_id=1, source_target_pairs={{0,3},{1,0},{2,1},{3,2},{4,7},{5,4},{6,5},{7,6},{8,11},{9,8},{10,9... | collective-permute-start | bytes 1572872 | tf_op jit(solution)/shard_map/ppermute | solution.py:445
  703.5 68.3 %collective-permute-start.25 = (bf16[128,2048]{1,0:T(8,128)(2,1)}, bf16[128,2048]{1,0:T(8,128)(2,1)}, u32[]{:S(2)}, u32[]{:S(2)}) collective-permute-start(bf16[128,2048]{1,0:T(8,128)(2,1)} %get-tuple-element.243), channel_id=1, source_target_pairs={{0,1},{1,2},{2,3},{3,0},{4,5},{5,6},{6,7},{7,4},{8,9},{9,10},{10,1... | collective-permute-start | bytes 1572872 | tf_op jit(solution)/shard_map/ppermute | solution.py:445
  703.5 76.4 %collective-permute-start.27 = (bf16[128,2048]{1,0:T(8,128)(2,1)}, bf16[128,2048]{1,0:T(8,128)(2,1)}, u32[]{:S(2)}, u32[]{:S(2)}) collective-permute-start(bf16[128,2048]{1,0:T(8,128)(2,1)} %get-tuple-element.244), channel_id=1, source_target_pairs={{0,3},{1,0},{2,1},{3,2},{4,7},{5,4},{6,5},{7,6},{8,11},{9,8},{10,9... | collective-permute-start | bytes 1572872 | tf_op jit(solution)/shard_map/ppermute | solution.py:445
  705.0 76.2 %collective-permute-start.26 = (bf16[128,2048]{1,0:T(8,128)(2,1)}, bf16[128,2048]{1,0:T(8,128)(2,1)}, u32[]{:S(2)}, u32[]{:S(2)}) collective-permute-start(bf16[128,2048]{1,0:T(8,128)(2,1)} %get-tuple-element.245), channel_id=1, source_target_pairs={{0,2},{1,3},{2,0},{3,1},{4,6},{5,7},{6,4},{7,5},{8,10},{9,11},{10,... | collective-permute-start | bytes 1572872 | tf_op jit(solution)/shard_map/ppermute | solution.py:445
  715.3 66.8 %collective-permute-start.22 = (bf16[128,2048]{1,0:T(8,128)(2,1)}, bf16[128,2048]{1,0:T(8,128)(2,1)}, u32[]{:S(2)}, u32[]{:S(2)}) collective-permute-start(bf16[128,2048]{1,0:T(8,128)(2,1)} %get-tuple-element.246), channel_id=1, source_target_pairs={{0,1},{1,2},{2,3},{3,0},{4,5},{5,6},{6,7},{7,4},{8,9},{9,10},{10,1... | collective-permute-start | bytes 1572872 | tf_op jit(solution)/shard_map/ppermute | solution.py:445
  771.9 37.3 %collective-permute-start.23 = (bf16[128,2048]{1,0:T(8,128)(2,1)}, bf16[128,2048]{1,0:T(8,128)(2,1)}, u32[]{:S(2)}, u32[]{:S(2)}) collective-permute-start(bf16[128,2048]{1,0:T(8,128)(2,1)} %get-tuple-element.248), channel_id=1, source_target_pairs={{0,2},{1,3},{2,0},{3,1},{4,6},{5,7},{6,4},{7,5},{8,10},{9,11},{10,... | collective-permute-start | bytes 1572872 | tf_op jit(solution)/shard_map/ppermute | solution.py:445
  781.2 71.2 %collective-permute-start.20 = (bf16[128,2048]{1,0:T(8,128)(2,1)}, bf16[128,2048]{1,0:T(8,128)(2,1)S(1)}, u32[]{:S(2)}, u32[]{:S(2)}) collective-permute-start(bf16[128,2048]{1,0:T(8,128)(2,1)} %get-tuple-element.187), channel_id=1, source_target_pairs={{0,2},{1,3},{2,0},{3,1},{4,6},{5,7},{6,4},{7,5},{8,10},{9,11},{10,... | collective-permute-start | bytes 1572872 | tf_op jit(solution)/shard_map/ppermute | solution.py:445
  782.1 70.3 %collective-permute-start.21 = (bf16[128,2048]{1,0:T(8,128)(2,1)}, bf16[128,2048]{1,0:T(8,128)(2,1)S(1)}, u32[]{:S(2)}, u32[]{:S(2)}) collective-permute-start(bf16[128,2048]{1,0:T(8,128)(2,1)} %get-tuple-element.188), channel_id=1, source_target_pairs={{0,3},{1,0},{2,1},{3,2},{4,7},{5,4},{6,5},{7,6},{8,11},{9,8},{10,9... | collective-permute-start | bytes 1572872 | tf_op jit(solution)/shard_map/ppermute | solution.py:445
  (120 other events, 2540.7 us)
Sparse Core Ops, SparseCore 0:
  13.0 75.7 all-gather.7
  90.6 37.4 all-gather.9
  130.0 44.4 all-gather.13
  176.8 67.6 all-gather.11
  249.0 43.5 all-gather.15
  294.7 42.9 reduce-scatter.5
  340.0 43.1 reduce-scatter.7
  385.4 44.8 all-gather.17
  432.5 44.6 all-gather.19
  479.3 42.9 reduce-scatter.9
  526.4 119.4 reduce-scatter.11
  668.9 121.1 reduce-scatter.13

commit v4 on v3

--- a/solution.py
+++ b/solution.py
@@ -679,7 +679,8 @@
     in_grad = product_tn(joined(first_a, first_b), joined(raw_grad_a, raw_grad_b)).astype(low)
     out_grad = product_tn(joined(mix_rows_a, mix_rows_b), joined(mixed_a, mixed_b)).astype(low)
     in_grad = jnp.concatenate([in_grad, out_grad], axis=1)
-    raw_grad_a, in_grad, both_final = hold(raw_grad_a, in_grad, both_final)
+    raw_grad_a, in_grad, both_final, *moved = hold(raw_grad_a, in_grad, both_final, *final_b[1])
+    final_b = (final_b[0], moved)
     part3_a = product_nt(raw_grad_a, in_full)
     own3_a, terms3_a = z_terms(part3_a)
     sent3_a = z_ship(terms3_a)

time: 886 us -> 848 us (0.957)
  the two profiles are of different devices: /device:TPU:25 before, /device:TPU:0 now
where the time goes in v4:
time: 848 us; the launch traced here: 838 us
  waiting for transfers between devices  277 us (33%)
  matrix products  181 us (21%)
  Pallas kernels  125 us (15%)
  other arithmetic  82 us (10%)
  starting transfers between devices  81 us (10%)
  local copies, waits for them, and re-layouts  72.8 us (9%)
  between operations  18.9 us (2%)
    dot_general x8, matrix products, product_nt(): return lax.dot_general(left_rows, matrix, NT, preferred_element_type=F32)  69.9 us
    all_gather x3, waiting for transfers between devices, queued_gather(): return lax.all_gather(own, 'tensor', axis=0, tiled=True)  69.9 us
    reduce_scatter x3, waiting for transfers between devices, queued_scatter(): lax.psum_scatter(partial.astype(jnp.bfloat16), 'tensor', scatter_dimensio...  64.5 us
    pallas_call x2, Pallas kernels, mixer_forward(): pl.pallas_call(functools.partial(forward_kernel, heads), grid_spec=pltpu....  63.5 us
    pallas_call x2, Pallas kernels, mixer_backward(): pl.pallas_call(functools.partial(backward_kernel, heads), grid_spec=pltpu...  61 us
    dot_general x8, matrix products, product(): return lax.dot_general(left_rows, matrix, NN, preferred_element_type=F32)  58.3 us
    dot_general x4, matrix products, product_tn(): lax.dot_general(left_rows, right_rows, TN, preferred_element_type=F32)  53.3 us
    ppermute x2, waiting for transfers between devices, relay_far(): left2 = lax.ppermute(left, 'tensor', [(1, 0), (2, 1)])  44.7 us
  transfers between devices with their start and end apart: 45, of which 18 were waited for; matrix products, arithmetic and copies ran while one was open for 36% of the time, Pallas kernels for 15%

profile of v4, /device:TPU:0, one launch (start us, length us, event | category | flops | bytes accessed | tf_op | source)
XLA Modules:
  0.0 838.2 jit_solution(16730902024652419999)
XLA Ops:
  31.6 14.8 %collective-permute-done.2 = bf16[2,128,2048]{2,1,0:T(8,128)(2,1)} collective-permute-done((bf16[2,128,2048]{2,1,0:T(8,128)(2,1)}, bf16[2,128,2048]{2,1,0:T(8,128)(2,1)}, u32[]{:S(2)}, u32[]{:S(2)}) %collective-permute-start.2) | collective-permute-done | bytes 1048608 | tf_op jit(solution)/shard_map/ppermute | solution.py:459
  53.6 44.7 %collective-permute-done.4 = bf16[2,128,2048]{2,1,0:T(8,128)(2,1)S(1)} collective-permute-done((bf16[2,128,2048]{2,1,0:T(8,128)(2,1)}, bf16[2,128,2048]{2,1,0:T(8,128)(2,1)S(1)}, u32[]{:S(2)}, u32[]{:S(2)}) %collective-permute-start.4) | collective-permute-done | bytes 1048608 | tf_op jit(solution)/shard_map/ppermute | solution.py:469
  109.9 11.7 %fusion.113.raw_ref = f32[512,3200]{1,0:T(8,128)S(1)} fusion(bf16[2048,3200]{1,0:T(8,128)(2,1)} %all-gather.8.cloned.1.call-done, bf16[2,512,2048]{2,1,0:T(8,128)(2,1)} %pad_maximum_fusion.2), kind=kOutput, calls=%fused_computation.230 | convolution fusion | flops 6710886400 | bytes 21757952 | tf_op jit(solution)/shard_map/dot_general | solution.py:359
  121.7 31.8 %mixer_forward.2 = (bf16[512,1024]{1,0:T(8,128)(2,1)S(1)}, f32[512,2048]{1,0:T(8,128)S(1)}, f32[512,1024]{1,0:T(8,128)S(1)}, f32[512,1024]{1,0:T(8,128)S(1)}, f3...) custom-call(s32[8]{0:T(128)S(1)} %or_select_fusion.keep_ref, f32[512,3200]{1,0:T(8,128)S(1)} %fusion.113.raw_ref, ...), custom_call_target="tpu_custom_call" | custom-call | flops 1000 | bytes 1000 | tf_op jit(solution)/shard_map/mixer_forward/pallas_call | solution.py:151
  180.5 11.1 %fusion.125.raw_ref = f32[512,3200]{1,0:T(8,128)S(1)} fusion(bf16[512,2048]{1,0:T(8,128)(2,1)S(1)} %get-tuple-element.131, bf16[2048,3200]{1,0:T(8,128)(2,1)} %all-gather.8.cloned.1.call-done), kind=kOutput, calls=%fused_computation.240 | convolution fusion | flops 6710886400 | bytes 21757952 | tf_op jit(solution)/shard_map/dot_general | solution.py:359
  193.7 31.7 %mixer_forward.3 = (bf16[512,1024]{1,0:T(8,128)(2,1)S(1)}, f32[512,2048]{1,0:T(8,128)S(1)}, f32[512,1024]{1,0:T(8,128)S(1)}, f32[512,1024]{1,0:T(8,128)S(1)}, f3...) custom-call(s32[8]{0:T(128)S(1)} %or_select_fusion.1.keep_ref, f32[512,3200]{1,0:T(8,128)S(1)} %fusion.125.raw_ref, ...), custom_call_target="tpu_custom_call" | custom-call | flops 1000 | bytes 1000 | tf_op jit(solution)/shard_map/mixer_forward/pallas_call | solution.py:151
  234.6 11.2 %all-gather.12.cloned.1.call-done = bf16[2048,2816]{1,0:T(8,128)(2,1)} async-done(((bf16[256,2816]{1,0:T(8,128)(2,1)}), bf16[2048,2816]{1,0:T(8,128)(2,1)}) %all-gather.12.cloned.1.call-update) | async-done | bytes 11534352 | tf_op jit(solution)/shard_map/all_gather | solution.py:498
  278.4 17.8 %all-gather.16.cloned.1.call-done = bf16[512,2048]{1,0:T(8,128)(2,1)} async-done(((bf16[128,2048]{1,0:T(8,128)(2,1)}), bf16[512,2048]{1,0:T(8,128)(2,1)}) %all-gather.16.cloned.1.call-update) | async-done | bytes 2097168 | tf_op jit(solution)/shard_map/all_gather | solution.py:420
  296.5 10.3 %fusion.128 = f32[512,2816]{1,0:T(8,128)S(1)} fusion(bf16[512,2048]{1,0:T(8,128)(2,1)} %all-gather.16.cloned.1.call-done, bf16[2048,2816]{1,0:T(8,128)(2,1)} %all-gather.12.cloned.1.call-done), kind=kOutput, calls=%fused_computation.243 | convolution fusion | flops 5905580032 | bytes 19398656 | tf_op jit(solution)/shard_map/dot_general | solution.py:359
  311.2 10.1 %convolution_convert_fusion.5 = bf16[512,2048]{1,0:T(8,128)(2,1)} fusion(bf16[2048,2816]{1,0:T(8,128)(2,1)} %all-gather.12.cloned.1.call-done, bf16[512,1408]{1,0:T(8,128)(2,1)S(1)} %get-tuple-element.243, bf16[512,1408]{1,0:T(8,128)(2,1)S(1)} %get-tuple-element.242), kind=kOutput, calls=%fused_computation.35 | convolution fusion | flops 5912395776 | bytes 16515072 | tf_op jit(solution)/shard_map/dot_general | solution.py:363
  321.2 19.8 %reduce-scatter.6.cloned.1.call-done = bf16[128,2048]{1,0:T(8,128)(2,1)} async-done(((bf16[512,2048]{1,0:T(8,128)(2,1)}), bf16[128,2048]{1,0:T(8,128)(2,1)}) %reduce-scatter.6.cloned.1.call-update) | async-done | bytes 524304 | tf_op jit(solution)/shard_map/reduce_scatter | solution.py:424
  351.4 35.2 %reduce-scatter.8.cloned.1.call-done = bf16[128,2048]{1,0:T(8,128)(2,1)} async-done(((bf16[512,2048]{1,0:T(8,128)(2,1)}), bf16[128,2048]{1,0:T(8,128)(2,1)}) %reduce-scatter.8.cloned.1.call-update) | async-done | bytes 524304 | tf_op jit(solution)/shard_map/reduce_scatter | solution.py:424
  391.1 42.9 %all-gather.18.cloned.1.call-done = bf16[512,2048]{1,0:T(8,128)(2,1)} async-done(((bf16[128,2048]{1,0:T(8,128)(2,1)}), bf16[512,2048]{1,0:T(8,128)(2,1)}) %all-gather.18.cloned.1.call-update) | async-done | bytes 2097168 | tf_op jit(solution)/shard_map/all_gather | solution.py:420
  434.4 10.3 %fusion.130 = f32[512,2816]{1,0:T(8,128)S(1)} fusion(bf16[512,2048]{1,0:T(8,128)(2,1)} %all-gather.18.cloned.1.call-done, bf16[2048,2816]{1,0:T(8,128)(2,1)} %all-gather.12.cloned.1.call-done), kind=kOutput, calls=%fused_computation.245 | convolution fusion | flops 5905580032 | bytes 19398656 | tf_op jit(solution)/shard_map/dot_general | solution.py:359
  446.7 8.9 %fusion.131 = f32[512,2048]{1,0:T(8,128)} fusion(bf16[512,1408]{1,0:T(8,128)(2,1)S(1)} %get-tuple-element.244, bf16[2048,1408]{0,1:T(8,128)(2,1)} %all-gather.14.cloned.1.call-done), kind=kOutput, calls=%fused_computation.246 | convolution fusion | flops 2952790016 | bytes 11403264 | tf_op jit(solution)/shard_map/dot_general | solution.py:363
  455.7 8.7 %convolution_convert_fusion.2 = bf16[2048,1408]{1,0:T(8,128)(2,1)} fusion(bf16[512,2048]{1,0:T(8,128)(2,1)S(1)} %copy-done.56, bf16[512,2048]{1,0:T(8,128)(2,1)S(1)} %copy-done.58, bf16[512,1408]{1,0:T(8,128)(2,1)S(1)} %get-tuple-element.244, bf16[512,1408]{1,0:T(8,128)(2,1)S(1)} %copy-done.63), kind=kOutput, calls=%fused_computation.4 | convolution fusion | flops 5922619392 | bytes 12845056 | tf_op jit(solution)/shard_map/dot_general | solution.py:367
  464.4 7.4 convolution_convert_fusion.4
  471.8 9.1 %all-gather.20.cloned.1.call-done = bf16[512,2048]{1,0:T(8,128)(2,1)} async-done(((bf16[128,2048]{1,0:T(8,128)(2,1)}), bf16[512,2048]{1,0:T(8,128)(2,1)}) %all-gather.20.cloned.1.call-update) | async-done | bytes 2097168 | tf_op jit(solution)/shard_map/all_gather | solution.py:420
  483.7 18.3 %convolution_convert_fusion.1 = bf16[2048,2816]{1,0:T(8,128)(2,1)} fusion(bf16[512,1408]{1,0:T(8,128)(2,1)} %copy-done.65, bf16[512,1408]{1,0:T(8,128)(2,1)} %copy-done.64, bf16[512,1408]{1,0:T(8,128)(2,1)} %copy-done.62, bf16[512,1408]{1,0:T(8,128)(2,1)} %copy-done.61, bf16[512,2048]{1,0:T(8,128)(2,1)} %all-gather.18.cloned.1.call-done, ...), kind=kOutput, calls=%fused_computation.3 | convolution fusion | flops 11848384512 | bytes 21495808 | tf_op jit(solution)/shard_map/dot_general | solution.py:367
  502.1 14.1 %pad_maximum_fusion = bf16[2048,4224]{1,0:T(8,128)(2,1)} fusion(bf16[2048,1408]{1,0:T(8,128)(2,1)} %convolution_convert_fusion.2, bf16[2048,2816]{1,0:T(8,128)(2,1)} %convolution_convert_fusion.1), kind=kLoop, calls=%fused_computation | loop fusion | flops 34603008 | bytes 34603008 | tf_op jit(solution)/shard_map/concatenate | solution.py:659
  516.1 9.5 %reduce-scatter.10.cloned.1.call-done = bf16[128,2048]{1,0:T(8,128)(2,1)} async-done(((bf16[512,2048]{1,0:T(8,128)(2,1)}), bf16[128,2048]{1,0:T(8,128)(2,1)}) %reduce-scatter.10.cloned.1.call-update) | async-done | bytes 524304 | tf_op jit(solution)/shard_map/reduce_scatter | solution.py:424
  540.7 30.2 %mixer_backward.2 = (bf16[512,3200]{1,0:T(8,128)(2,1)S(1)}, f32[4,2048]{1,0:T(4,128)S(1)}, f32[8,128]{1,0:T(8,128)S(1)}, f32[1,256]{1,0:T(1,128)S(1)}) custom-call(s32[9]{0:T(128)S(1)} %get-tuple-element.306.keep_ref, f32[512,3200]{1,0:T(8,128)} %copy-done.3, f32[512,2048]{1,0:T(8,128)S(1)} %copy-done.9, f32[512,1024]{1,0:T(8,128)S(1)} %copy-done.15, ...), custom_call_target="tpu_custom_call" | custom-call | flops 1000 | bytes 1000 | tf_op jit(solution)/shard_map/mixer_backward/pallas_call | solution.py:326
  572.7 10.1 %collective-permute-start.16 = (bf16[128,2048]{1,0:T(8,128)(2,1)S(1)}, bf16[128,2048]{1,0:T(8,128)(2,1)S(1)}, u32[]{:S(2)}, u32[]{:S(2)}) collective-permute-start(bf16[128,2048]{1,0:T(8,128)(2,1)S(1)} %get-tuple-element.180), channel_id=1, source_target_pairs={{0,1},{1,2},{2,3},{3,0},{4,5},{5,6},{6,7},{7,4},{8,9},{9,10},{10,1... | collective-permute-start | bytes 1572872 | tf_op jit(solution)/shard_map/ppermute | solution.py:445
  587.7 30.8 %mixer_backward.3 = (bf16[512,3200]{1,0:T(8,128)(2,1)S(1)}, f32[4,2048]{1,0:T(4,128)S(1)}, f32[8,128]{1,0:T(8,128)S(1)}, f32[1,256]{1,0:T(1,128)S(1)}) custom-call(s32[9]{0:T(128)S(1)} %get-tuple-element.307.keep_ref, f32[512,3200]{1,0:T(8,128)} %copy-done.2, f32[512,2048]{1,0:T(8,128)S(1)} %copy-done.5, f32[512,1024]{1,0:T(8,128)S(1)} %get-tuple-element.139.fresh_ref, ...), custom_call_target="tpu_custom_call" | custom-call | flops 1000 | bytes 1000 | tf_op jit(solution)/shard_map/mixer_backward/pallas_call | solution.py:326
  618.5 10.9 %collective-permute-start.19 = (bf16[128,2048]{1,0:T(8,128)(2,1)}, bf16[128,2048]{1,0:T(8,128)(2,1)S(1)}, u32[]{:S(2)}, u32[]{:S(2)}) collective-permute-start(bf16[128,2048]{1,0:T(8,128)(2,1)} %get-tuple-element.193), channel_id=1, source_target_pairs={{0,1},{1,2},{2,3},{3,0},{4,5},{5,6},{6,7},{7,4},{8,9},{9,10},{10,1... | collective-permute-start | bytes 1572872 | tf_op jit(solution)/shard_map/ppermute | solution.py:445
  638.4 20.1 %convolution_convert_fusion = bf16[2048,3200]{1,0:T(8,128)(2,1)} fusion(bf16[512,3200]{1,0:T(8,128)(2,1)} %copy-done.27, bf16[512,3200]{1,0:T(8,128)(2,1)S(1)} %copy-done.25, bf16[512,2048]{1,0:T(8,128)(2,1)} %copy-done.53, bf16[512,2048]{1,0:T(8,128)(2,1)} %get-tuple-element.255), kind=kOutput, calls=%fused_computation.2 | convolution fusion | flops 13449822208 | bytes 23855104 | tf_op jit(solution)/shard_map/dot_general | solution.py:367
  658.4 14.0 %pad_maximum_fusion.1 = bf16[2048,4224]{1,0:T(8,128)(2,1)} fusion(bf16[2048,1024]{1,0:T(8,128)(2,1)} %fusion.23, bf16[2048,3200]{1,0:T(8,128)(2,1)} %convolution_convert_fusion), kind=kLoop, calls=%fused_computation.1 | loop fusion | flops 34603008 | bytes 34603008 | tf_op jit(solution)/shard_map/concatenate | solution.py:681
  678.3 13.8 %multiply_reduce_fusion = (f32[2048]{0:T(1024)S(1)}, f32[512,2048]{1,0:T(8,128)}) fusion(bf16[512,2048]{1,0:T(8,128)(2,1)S(1)} %copy-done.54, bf16[512,3200]{1,0:T(8,128)(2,1)} %copy-done.27, bf16[2048,3200]{1,0:T(8,128)(2,1)} %all-gather.8.cloned.1.call-done), kind=kOutput, calls=%fused_computation.30 | convolution fusion | flops 6714030080 | bytes 22683648 | tf_op jit(solution)/shard_map/dot_general | solution.py:363
  692.2 13.1 %multiply_reduce_fusion.1 = (f32[2048]{0:T(1024)S(1)}, f32[512,2048]{1,0:T(8,128)}) fusion(bf16[2,512,2048]{2,1,0:T(8,128)(2,1)S(1)} %copy-done.39, bf16[512,3200]{1,0:T(8,128)(2,1)S(1)} %copy-done.26, bf16[2048,3200]{1,0:T(8,128)(2,1)} %all-gather.8.cloned.1.call-done), kind=kOutput, calls=%fused_computation.31 | convolution fusion | flops 6714030080 | bytes 22683648 | tf_op jit(solution)/shard_map/dot_general | solution.py:363
  726.7 23.2 %collective-permute-done.31 = f32[37152]{0:T(1024)S(1)} collective-permute-done((f32[37152]{0:T(1024)S(1)}, f32[37152]{0:T(1024)S(1)}, u32[]{:S(2)}, u32[]{:S(2)}) %collective-permute-start.31) | collective-permute-done | bytes 148640 | tf_op jit(solution)/shard_map/ppermute | solution.py:492
  761.7 14.7 %collective-permute-done.32 = f32[37152]{0:T(1024)S(1)} collective-permute-done((f32[37152]{0:T(1024)S(1)}, f32[37152]{0:T(1024)S(1)}, u32[]{:S(2)}, u32[]{:S(2)}) %collective-permute-start.32) | collective-permute-done | bytes 148640 | tf_op jit(solution)/shard_map/ppermute | solution.py:492
  791.9 18.9 %collective-permute-done.23 = bf16[128,2048]{1,0:T(8,128)(2,1)} collective-permute-done((bf16[128,2048]{1,0:T(8,128)(2,1)}, bf16[128,2048]{1,0:T(8,128)(2,1)}, u32[]{:S(2)}, u32[]{:S(2)}) %collective-permute-start.23) | collective-permute-done | bytes 524320 | tf_op jit(solution)/shard_map/ppermute | solution.py:445
  (431 shorter events, 240.1 us)
Async XLA Ops:
  7.2 95.4 %all-gather.8.cloned.1.call-start = ((), (), s32[]{:S(2)}) async-start(), calls=%async_computation.5 | async-start | bytes 14745600 | tf_op jit(solution)/shard_map/all_gather | solution.py:498
  12.8 151.4 %all-gather.10.cloned.1.call-start = ((), (), s32[]{:S(2)}) async-start(), calls=%async_computation.6 | async-start | bytes 4718592 | tf_op jit(solution)/shard_map/all_gather | solution.py:498
  13.6 221.0 %all-gather.14.cloned.1.call-start = ((), (), s32[]{:S(2)}) async-start(), calls=%async_computation.8 | async-start | bytes 6488064 | tf_op jit(solution)/shard_map/all_gather | solution.py:498
  14.4 231.4 %all-gather.12.cloned.1.call-start = ((), (), s32[]{:S(2)}) async-start(), calls=%async_computation.7 | async-start | bytes 12976128 | tf_op jit(solution)/shard_map/all_gather | solution.py:498
  15.7 280.6 %all-gather.16.cloned.1.call-start = ((), (), s32[]{:S(2)}) async-start(), calls=%async_computation.9 | async-start | bytes 2621440 | tf_op jit(solution)/shard_map/all_gather | solution.py:420
  48.9 49.4 %collective-permute-start.3 = (bf16[2,128,2048]{2,1,0:T(8,128)(2,1)S(1)}, bf16[2,128,2048]{2,1,0:T(8,128)(2,1)S(1)}, u32[]{:S(2)}, u32[]{:S(2)}) collective-permute-start(bf16[2,128,2048]{2,1,0:T(8,128)(2,1)S(1)} %broadcast_select_fusion.1), channel_id=1, source_target_pairs={{1,3},{2,0},{5,7},{6,4},{9,11},{10,8},{13,15},{14,12},{17,19},{18,... | collective-permute-start | bytes 3145736 | tf_op jit(solution)/shard_map/ppermute | solution.py:470
  50.2 48.1 %collective-permute-start.4 = (bf16[2,128,2048]{2,1,0:T(8,128)(2,1)}, bf16[2,128,2048]{2,1,0:T(8,128)(2,1)S(1)}, u32[]{:S(2)}, u32[]{:S(2)}) collective-permute-start(bf16[2,128,2048]{2,1,0:T(8,128)(2,1)} %collective-permute-done.2), channel_id=1, source_target_pairs={{1,0},{2,1},{5,4},{6,5},{9,8},{10,9},{13,12},{14,13},{17,16},{18,1... | collective-permute-start | bytes 3145736 | tf_op jit(solution)/shard_map/ppermute | solution.py:469
  51.5 46.8 %collective-permute-start.1 = (bf16[2,128,2048]{2,1,0:T(8,128)(2,1)}, bf16[2,128,2048]{2,1,0:T(8,128)(2,1)S(1)}, u32[]{:S(2)}, u32[]{:S(2)}) collective-permute-start(bf16[2,128,2048]{2,1,0:T(8,128)(2,1)} %collective-permute-done), channel_id=1, source_target_pairs={{1,2},{2,3},{5,6},{6,7},{9,10},{10,11},{13,14},{14,15},{17,18},{18... | collective-permute-start | bytes 3145736 | tf_op jit(solution)/shard_map/ppermute | solution.py:468
  102.6 58.6 %collective-permute-start.6 = (bf16[2,128,2048]{2,1,0:T(8,128)(2,1)}, bf16[2,128,2048]{2,1,0:T(8,128)(2,1)}, u32[]{:S(2)}, u32[]{:S(2)}) collective-permute-start(bf16[2,128,2048]{2,1,0:T(8,128)(2,1)} %pad_maximum_fusion.8), channel_id=1, source_target_pairs={{1,0},{2,1},{3,2},{5,4},{6,5},{7,6},{9,8},{10,9},{11,10},{13,12},{... | collective-permute-start | bytes 3145736 | tf_op jit(solution)/shard_map/ppermute | solution.py:459
  104.0 57.2 %collective-permute-start.5 = (bf16[2,128,2048]{2,1,0:T(8,128)(2,1)}, bf16[2,128,2048]{2,1,0:T(8,128)(2,1)}, u32[]{:S(2)}, u32[]{:S(2)}) collective-permute-start(bf16[2,128,2048]{2,1,0:T(8,128)(2,1)} %pad_maximum_fusion.8), channel_id=1, source_target_pairs={{0,1},{1,2},{2,3},{4,5},{5,6},{6,7},{8,9},{9,10},{10,11},{12,13},{... | collective-permute-start | bytes 3145736 | tf_op jit(solution)/shard_map/ppermute | solution.py:458
  161.2 99.7 %collective-permute-start.10 = (bf16[2,128,2048]{2,1,0:T(8,128)(2,1)}, bf16[2,128,2048]{2,1,0:T(8,128)(2,1)}, u32[]{:S(2)}, u32[]{:S(2)}) collective-permute-start(bf16[2,128,2048]{2,1,0:T(8,128)(2,1)} %collective-permute-done.5), channel_id=1, source_target_pairs={{1,2},{2,3},{5,6},{6,7},{9,10},{10,11},{13,14},{14,15},{17,18},{18... | collective-permute-start | bytes 3145736 | tf_op jit(solution)/shard_map/ppermute | solution.py:468
  163.0 98.0 %collective-permute-start.12 = (bf16[2,128,2048]{2,1,0:T(8,128)(2,1)}, bf16[2,128,2048]{2,1,0:T(8,128)(2,1)}, u32[]{:S(2)}, u32[]{:S(2)}) collective-permute-start(bf16[2,128,2048]{2,1,0:T(8,128)(2,1)} %collective-permute-done.6), channel_id=1, source_target_pairs={{1,0},{2,1},{5,4},{6,5},{9,8},{10,9},{13,12},{14,13},{17,16},{18,1... | collective-permute-start | bytes 3145736 | tf_op jit(solution)/shard_map/ppermute | solution.py:469
  171.0 61.5 %collective-permute-start.9 = (bf16[128,2048]{1,0:T(8,128)(2,1)S(1)}, bf16[128,2048]{1,0:T(8,128)(2,1)S(1)}, u32[]{:S(2)}, u32[]{:S(2)}) collective-permute-start(bf16[128,2048]{1,0:T(8,128)(2,1)S(1)} %get-tuple-element.263), channel_id=1, source_target_pairs={{0,3},{1,0},{2,1},{3,2},{4,7},{5,4},{6,5},{7,6},{8,11},{9,8},{10,9... | collective-permute-start | bytes 1572872 | tf_op jit(solution)/shard_map/ppermute | solution.py:445
  174.0 71.8 %collective-permute-start.8 = (bf16[128,2048]{1,0:T(8,128)(2,1)}, bf16[128,2048]{1,0:T(8,128)(2,1)}, u32[]{:S(2)}, u32[]{:S(2)}) collective-permute-start(bf16[128,2048]{1,0:T(8,128)(2,1)} %get-tuple-element.264), channel_id=1, source_target_pairs={{0,2},{1,3},{2,0},{3,1},{4,6},{5,7},{6,4},{7,5},{8,10},{9,11},{10,... | collective-permute-start | bytes 1572872 | tf_op jit(solution)/shard_map/ppermute | solution.py:445
  191.7 54.1 %collective-permute-start.7 = (bf16[128,2048]{1,0:T(8,128)(2,1)}, bf16[128,2048]{1,0:T(8,128)(2,1)}, u32[]{:S(2)}, u32[]{:S(2)}) collective-permute-start(bf16[128,2048]{1,0:T(8,128)(2,1)} %get-tuple-element.265), channel_id=1, source_target_pairs={{0,1},{1,2},{2,3},{3,0},{4,5},{5,6},{6,7},{7,4},{8,9},{9,10},{10,1... | collective-permute-start | bytes 1572872 | tf_op jit(solution)/shard_map/ppermute | solution.py:445
  250.1 90.9 %reduce-scatter.6.cloned.1.call-start = ((), (), s32[]{:S(2)}) async-start(), calls=%async_computation.10 | async-start | bytes 2621440 | tf_op jit(solution)/shard_map/reduce_scatter | solution.py:424
  296.3 90.3 %reduce-scatter.8.cloned.1.call-start = ((), (), s32[]{:S(2)}) async-start(), calls=%async_computation.11 | async-start | bytes 2621440 | tf_op jit(solution)/shard_map/reduce_scatter | solution.py:424
  341.0 93.0 %all-gather.18.cloned.1.call-start = ((), (), s32[]{:S(2)}) async-start(), calls=%async_computation.12 | async-start | bytes 2621440 | tf_op jit(solution)/shard_map/all_gather | solution.py:420
  386.6 94.3 %all-gather.20.cloned.1.call-start = ((), (), s32[]{:S(2)}) async-start(), calls=%async_computation.13 | async-start | bytes 2621440 | tf_op jit(solution)/shard_map/all_gather | solution.py:420
  434.1 91.5 %reduce-scatter.10.cloned.1.call-start = ((), (), s32[]{:S(2)}) async-start(), calls=%async_computation.14 | async-start | bytes 2621440 | tf_op jit(solution)/shard_map/reduce_scatter | solution.py:424
  480.9 191.5 %reduce-scatter.12.cloned.1.call-start = ((), (), s32[]{:S(2)}) async-start(), calls=%async_computation.15 | async-start | bytes 19464192 | tf_op jit(solution)/shard_map/reduce_scatter | solution.py:502
  525.7 296.7 %reduce-scatter.14.cloned.1.call-start = ((), (), s32[]{:S(2)}) async-start(), calls=%async_computation.16 | async-start | bytes 19464192 | tf_op jit(solution)/shard_map/reduce_scatter | solution.py:502
  533.4 37.6 %collective-permute-start.15 = (bf16[128,2048]{1,0:T(8,128)(2,1)S(1)}, bf16[128,2048]{1,0:T(8,128)(2,1)S(1)}, u32[]{:S(2)}, u32[]{:S(2)}) collective-permute-start(bf16[128,2048]{1,0:T(8,128)(2,1)S(1)} %get-tuple-element.175), channel_id=1, source_target_pairs={{0,1},{1,2},{2,3},{3,0},{4,5},{5,6},{6,7},{7,4},{8,9},{9,10},{10,1... | collective-permute-start | bytes 1572872 | tf_op jit(solution)/shard_map/ppermute | solution.py:415
  533.5 38.0 %collective-permute-start.14 = (bf16[128,2048]{1,0:T(8,128)(2,1)S(1)}, bf16[128,2048]{1,0:T(8,128)(2,1)S(1)}, u32[]{:S(2)}, u32[]{:S(2)}) collective-permute-start(bf16[128,2048]{1,0:T(8,128)(2,1)S(1)} %get-tuple-element.175), channel_id=1, source_target_pairs={{0,2},{1,3},{2,0},{3,1},{4,6},{5,7},{6,4},{7,5},{8,10},{9,11},{10,... | collective-permute-start | bytes 1572872 | tf_op jit(solution)/shard_map/ppermute | solution.py:415
  572.7 45.8 %collective-permute-start.16 = (bf16[128,2048]{1,0:T(8,128)(2,1)S(1)}, bf16[128,2048]{1,0:T(8,128)(2,1)S(1)}, u32[]{:S(2)}, u32[]{:S(2)}) collective-permute-start(bf16[128,2048]{1,0:T(8,128)(2,1)S(1)} %get-tuple-element.180), channel_id=1, source_target_pairs={{0,1},{1,2},{2,3},{3,0},{4,5},{5,6},{6,7},{7,4},{8,9},{9,10},{10,1... | collective-permute-start | bytes 1572872 | tf_op jit(solution)/shard_map/ppermute | solution.py:445
  618.5 57.8 %collective-permute-start.19 = (bf16[128,2048]{1,0:T(8,128)(2,1)}, bf16[128,2048]{1,0:T(8,128)(2,1)S(1)}, u32[]{:S(2)}, u32[]{:S(2)}) collective-permute-start(bf16[128,2048]{1,0:T(8,128)(2,1)} %get-tuple-element.193), channel_id=1, source_target_pairs={{0,1},{1,2},{2,3},{3,0},{4,5},{5,6},{6,7},{7,4},{8,9},{9,10},{10,1... | collective-permute-start | bytes 1572872 | tf_op jit(solution)/shard_map/ppermute | solution.py:445
  629.5 46.9 %collective-permute-start.20 = (bf16[128,2048]{1,0:T(8,128)(2,1)}, bf16[128,2048]{1,0:T(8,128)(2,1)S(1)}, u32[]{:S(2)}, u32[]{:S(2)}) collective-permute-start(bf16[128,2048]{1,0:T(8,128)(2,1)} %get-tuple-element.194), channel_id=1, source_target_pairs={{0,2},{1,3},{2,0},{3,1},{4,6},{5,7},{6,4},{7,5},{8,10},{9,11},{10,... | collective-permute-start | bytes 1572872 | tf_op jit(solution)/shard_map/ppermute | solution.py:445
  630.8 45.6 %collective-permute-start.21 = (bf16[128,2048]{1,0:T(8,128)(2,1)}, bf16[128,2048]{1,0:T(8,128)(2,1)}, u32[]{:S(2)}, u32[]{:S(2)}) collective-permute-start(bf16[128,2048]{1,0:T(8,128)(2,1)} %get-tuple-element.195), channel_id=1, source_target_pairs={{0,3},{1,0},{2,1},{3,2},{4,7},{5,4},{6,5},{7,6},{8,11},{9,8},{10,9... | collective-permute-start | bytes 1572872 | tf_op jit(solution)/shard_map/ppermute | solution.py:445
  711.0 70.0 %collective-permute-start.25 = (bf16[128,2048]{1,0:T(8,128)(2,1)}, bf16[128,2048]{1,0:T(8,128)(2,1)}, u32[]{:S(2)}, u32[]{:S(2)}) collective-permute-start(bf16[128,2048]{1,0:T(8,128)(2,1)} %get-tuple-element.249), channel_id=1, source_target_pairs={{0,1},{1,2},{2,3},{3,0},{4,5},{5,6},{6,7},{7,4},{8,9},{9,10},{10,1... | collective-permute-start | bytes 1572872 | tf_op jit(solution)/shard_map/ppermute | solution.py:445
  711.6 75.8 %collective-permute-start.27 = (bf16[128,2048]{1,0:T(8,128)(2,1)}, bf16[128,2048]{1,0:T(8,128)(2,1)}, u32[]{:S(2)}, u32[]{:S(2)}) collective-permute-start(bf16[128,2048]{1,0:T(8,128)(2,1)} %get-tuple-element.250), channel_id=1, source_target_pairs={{0,3},{1,0},{2,1},{3,2},{4,7},{5,4},{6,5},{7,6},{8,11},{9,8},{10,9... | collective-permute-start | bytes 1572872 | tf_op jit(solution)/shard_map/ppermute | solution.py:445
  714.8 72.6 %collective-permute-start.26 = (bf16[128,2048]{1,0:T(8,128)(2,1)}, bf16[128,2048]{1,0:T(8,128)(2,1)}, u32[]{:S(2)}, u32[]{:S(2)}) collective-permute-start(bf16[128,2048]{1,0:T(8,128)(2,1)} %get-tuple-element.251), channel_id=1, source_target_pairs={{0,2},{1,3},{2,0},{3,1},{4,6},{5,7},{6,4},{7,5},{8,10},{9,11},{10,... | collective-permute-start | bytes 1572872 | tf_op jit(solution)/shard_map/ppermute | solution.py:445
  725.3 62.1 %collective-permute-start.22 = (bf16[128,2048]{1,0:T(8,128)(2,1)}, bf16[128,2048]{1,0:T(8,128)(2,1)}, u32[]{:S(2)}, u32[]{:S(2)}) collective-permute-start(bf16[128,2048]{1,0:T(8,128)(2,1)} %get-tuple-element.252), channel_id=1, source_target_pairs={{0,1},{1,2},{2,3},{3,0},{4,5},{5,6},{6,7},{7,4},{8,9},{9,10},{10,1... | collective-permute-start | bytes 1572872 | tf_op jit(solution)/shard_map/ppermute | solution.py:445
  (124 other events, 2495.3 us)
Sparse Core Ops, SparseCore 0:
  13.0 77.0 all-gather.7
  91.9 37.4 all-gather.9
  131.3 44.4 all-gather.13
  178.1 67.6 all-gather.11
  250.3 45.9 all-gather.15
  298.4 42.5 reduce-scatter.5
  343.4 43.1 reduce-scatter.7
  388.7 45.2 all-gather.17
  436.2 44.6 all-gather.19
  483.0 42.5 reduce-scatter.9
  529.7 117.9 reduce-scatter.11
  676.5 118.8 reduce-scatter.13

commit v5 on v4

--- a/solution.py
+++ b/solution.py
@@ -504,6 +504,32 @@
     ).astype(jnp.float32)
 
 
+def relay_scatter(partial):
+    count = lax.axis_size("tensor")
+    packs, rows, width = partial.shape
+    low, wide = jnp.bfloat16, jnp.float32
+    if count != 4:
+        return lax.psum_scatter(
+            partial.astype(low), "tensor", scatter_dimension=1, tiled=True
+        ).astype(wide)
+    t = lax.axis_index("tensor")
+    parts = partial.reshape(packs, count, rows // count, width)
+
+    def take(index):
+        return lax.dynamic_index_in_dim(parts, jnp.clip(index, 0, count - 1), 1, keepdims=False)
+
+    far = lax.ppermute(
+        take(jnp.where(t == 3, 0, 3)).astype(low), "tensor", [(3, 1), (0, 2)]
+    )
+    left = lax.ppermute(take(t - 2).astype(low), "tensor", [(3, 2), (2, 1)])
+    right = lax.ppermute(take(t + 2).astype(low), "tensor", [(0, 1), (1, 2)])
+    to_left = take(t - 1) + left.astype(wide) + jnp.where(t == 1, far, 0).astype(wide)
+    to_right = take(t + 1) + right.astype(wide) + jnp.where(t == 2, far, 0).astype(wide)
+    from_right = lax.ppermute(to_left.astype(low), "tensor", [(1, 0), (2, 1), (3, 2)])
+    from_left = lax.ppermute(to_right.astype(low), "tensor", [(0, 1), (1, 2), (2, 3)])
+    return take(t) + from_right.astype(wide) + from_left.astype(wide)
+
+
 def shards(
     tokens,
     lengths,
@@ -682,19 +708,16 @@
     raw_grad_a, in_grad, both_final, *moved = hold(raw_grad_a, in_grad, both_final, *final_b[1])
     final_b = (final_b[0], moved)
     part3_a = product_nt(raw_grad_a, in_full)
-    own3_a, terms3_a = z_terms(part3_a)
-    sent3_a = z_ship(terms3_a)
     last_final = scatter_rows(in_grad)
     in_final, out_final = last_final[:, : in_full.shape[1]], last_final[:, in_full.shape[1] :]
     part3_b = product_nt(raw_grad_b, in_full)
-    own3_b, terms3_b = z_terms(part3_b)
-    sent3_b = z_ship(terms3_b)
+    first_sum = [relay_scatter(part3_a[None])[0], relay_scatter(part3_b[None])[0]]
     outputs = [
         ((middle_a + z_sum(*final_a)) * own_masks[A]).astype(low),
         ((middle_b + z_sum(*final_b)) * own_masks[B]).astype(low),
     ]
-    token_grad_a = norm_ones[A][1](z_sum(own3_a, sent3_a))[0]
-    token_grad_b = norm_ones[B][1](z_sum(own3_b, sent3_b))[0]
+    token_grad_a = norm_ones[A][1](first_sum[A])[0]
+    token_grad_b = norm_ones[B][1](first_sum[B])[0]
     mixer_gain_grad = (
         jnp.sum(part3_a * first_a.astype(wide), axis=0)
         + jnp.sum(part3_b * first_b.astype(wide), axis=0)

time: 848 us -> 829 us (0.978)
  waiting for transfers between devices: 277 us -> 232 us
  starting transfers between devices: 81 us -> 111 us
    ppermute x0 -> x10, starting transfers between devices: none -> 34.2 us  [the longest x2 17.1 us: relay_scatter(): lax.ppermute(to_right.astype(low), 'tensor', [(0, 1), (1, 2), (2, 3)])]
    ppermute x5, waiting for transfers between devices: 41.3 us -> 16.6 us  [sum_over(): lax.ppermute(values, axis, [(i, i ^ step) for i in range(count)])]
    ppermute x15 -> x9, waiting for transfers between devices: 23.4 us -> 0.02 us  [z_ship(): lax.ppermute(term, 'tensor', rotation(count, shift + 1))]
    ppermute x15 -> x9, starting transfers between devices: 44.2 us -> 37.8 us  [z_ship(): lax.ppermute(term, 'tensor', rotation(count, shift + 1))]
    unnamed x234 -> x238, local copies, waits for them, and re-layouts: 33.5 us -> 32 us
  transfers between devices with their start and end apart: 45 -> 49, of which waited for: 18 -> 18; matrix products, arithmetic and copies ran while one was open for 36% -> 36% of each run, Pallas kernels for 15% -> 15%
where the time goes in v5:
time: 829 us; the launch traced here: 819 us
  waiting for transfers between devices  232 us (28%)
  matrix products  180 us (22%)
  Pallas kernels  125 us (15%)
  starting transfers between devices  111 us (13%)
  other arithmetic  86.4 us (10%)
  local copies, waits for them, and re-layouts  66.4 us (8%)
  between operations  19.1 us (2%)
    all_gather x3, waiting for transfers between devices, queued_gather(): return lax.all_gather(own, 'tensor', axis=0, tiled=True)  69.9 us
    dot_general x8, matrix products, product_nt(): return lax.dot_general(left_rows, matrix, NT, preferred_element_type=F32)  68.3 us
    reduce_scatter x3, waiting for transfers between devices, queued_scatter(): lax.psum_scatter(partial.astype(jnp.bfloat16), 'tensor', scatter_dimensio...  64.5 us
    pallas_call x2, Pallas kernels, mixer_forward(): pl.pallas_call(functools.partial(forward_kernel, heads), grid_spec=pltpu....  63.6 us
    pallas_call x2, Pallas kernels, mixer_backward(): pl.pallas_call(functools.partial(backward_kernel, heads), grid_spec=pltpu...  61 us
    dot_general x8, matrix products, product(): return lax.dot_general(left_rows, matrix, NN, preferred_element_type=F32)  58.3 us
    dot_general x4, matrix products, product_tn(): lax.dot_general(left_rows, right_rows, TN, preferred_element_type=F32)  53.4 us
    ppermute x2, waiting for transfers between devices, relay_far(): left2 = lax.ppermute(left, 'tensor', [(1, 0), (2, 1)])  44.7 us
  transfers between devices with their start and end apart: 49, of which 18 were waited for; matrix products, arithmetic and copies ran while one was open for 36% of the time, Pallas kernels for 15%

profile of v5, /device:TPU:0, one launch (start us, length us, event | category | flops | bytes accessed | tf_op | source)
XLA Modules:
  0.0 819.1 jit_solution(7562190255011824917)
XLA Ops:
  19.2 6.6 collective-permute-start
  31.6 14.8 %collective-permute-done.2 = bf16[2,128,2048]{2,1,0:T(8,128)(2,1)} collective-permute-done((bf16[2,128,2048]{2,1,0:T(8,128)(2,1)}, bf16[2,128,2048]{2,1,0:T(8,128)(2,1)}, u32[]{:S(2)}, u32[]{:S(2)}) %collective-permute-start.2) | collective-permute-done | bytes 1048608 | tf_op jit(solution)/shard_map/ppermute | solution.py:459
  53.5 44.7 %collective-permute-done.4 = bf16[2,128,2048]{2,1,0:T(8,128)(2,1)S(1)} collective-permute-done((bf16[2,128,2048]{2,1,0:T(8,128)(2,1)}, bf16[2,128,2048]{2,1,0:T(8,128)(2,1)S(1)}, u32[]{:S(2)}, u32[]{:S(2)}) %collective-permute-start.4) | collective-permute-done | bytes 1048608 | tf_op jit(solution)/shard_map/ppermute | solution.py:469
  109.9 11.7 %fusion.117.raw_ref = f32[512,3200]{1,0:T(8,128)S(1)} fusion(bf16[2048,3200]{1,0:T(8,128)(2,1)} %all-gather.8.cloned.1.call-done, bf16[2,512,2048]{2,1,0:T(8,128)(2,1)} %pad_maximum_fusion.2), kind=kOutput, calls=%fused_computation.240 | convolution fusion | flops 6710886400 | bytes 21757952 | tf_op jit(solution)/shard_map/dot_general | solution.py:359
  121.6 31.8 %mixer_forward.2 = (bf16[512,1024]{1,0:T(8,128)(2,1)S(1)}, f32[512,2048]{1,0:T(8,128)S(1)}, f32[512,1024]{1,0:T(8,128)S(1)}, f32[512,1024]{1,0:T(8,128)S(1)}, f3...) custom-call(s32[8]{0:T(128)S(1)} %or_select_fusion.keep_ref, f32[512,3200]{1,0:T(8,128)S(1)} %fusion.117.raw_ref, ...), custom_call_target="tpu_custom_call" | custom-call | flops 1000 | bytes 1000 | tf_op jit(solution)/shard_map/mixer_forward/pallas_call | solution.py:151
  180.6 11.1 %fusion.129.raw_ref = f32[512,3200]{1,0:T(8,128)S(1)} fusion(bf16[512,2048]{1,0:T(8,128)(2,1)S(1)} %get-tuple-element.131, bf16[2048,3200]{1,0:T(8,128)(2,1)} %all-gather.8.cloned.1.call-done), kind=kOutput, calls=%fused_computation.250 | convolution fusion | flops 6710886400 | bytes 21757952 | tf_op jit(solution)/shard_map/dot_general | solution.py:359
  193.8 31.7 %mixer_forward.3 = (bf16[512,1024]{1,0:T(8,128)(2,1)S(1)}, f32[512,2048]{1,0:T(8,128)S(1)}, f32[512,1024]{1,0:T(8,128)S(1)}, f32[512,1024]{1,0:T(8,128)S(1)}, f3...) custom-call(s32[8]{0:T(128)S(1)} %or_select_fusion.1.keep_ref, f32[512,3200]{1,0:T(8,128)S(1)} %fusion.129.raw_ref, ...), custom_call_target="tpu_custom_call" | custom-call | flops 1000 | bytes 1000 | tf_op jit(solution)/shard_map/mixer_forward/pallas_call | solution.py:151
  234.7 11.2 %all-gather.12.cloned.1.call-done = bf16[2048,2816]{1,0:T(8,128)(2,1)} async-done(((bf16[256,2816]{1,0:T(8,128)(2,1)}), bf16[2048,2816]{1,0:T(8,128)(2,1)}) %all-gather.12.cloned.1.call-update) | async-done | bytes 11534352 | tf_op jit(solution)/shard_map/all_gather | solution.py:498
  278.4 17.9 %all-gather.16.cloned.1.call-done = bf16[512,2048]{1,0:T(8,128)(2,1)} async-done(((bf16[128,2048]{1,0:T(8,128)(2,1)}), bf16[512,2048]{1,0:T(8,128)(2,1)}) %all-gather.16.cloned.1.call-update) | async-done | bytes 2097168 | tf_op jit(solution)/shard_map/all_gather | solution.py:420
  296.6 10.3 %fusion.132 = f32[512,2816]{1,0:T(8,128)S(1)} fusion(bf16[512,2048]{1,0:T(8,128)(2,1)} %all-gather.16.cloned.1.call-done, bf16[2048,2816]{1,0:T(8,128)(2,1)} %all-gather.12.cloned.1.call-done), kind=kOutput, calls=%fused_computation.253 | convolution fusion | flops 5905580032 | bytes 19398656 | tf_op jit(solution)/shard_map/dot_general | solution.py:359
  311.2 10.1 %convolution_convert_fusion.5 = bf16[512,2048]{1,0:T(8,128)(2,1)} fusion(bf16[2048,2816]{1,0:T(8,128)(2,1)} %all-gather.12.cloned.1.call-done, bf16[512,1408]{1,0:T(8,128)(2,1)S(1)} %get-tuple-element.243, bf16[512,1408]{1,0:T(8,128)(2,1)S(1)} %get-tuple-element.242), kind=kOutput, calls=%fused_computation.35 | convolution fusion | flops 5912395776 | bytes 16515072 | tf_op jit(solution)/shard_map/dot_general | solution.py:363
  321.3 19.8 %reduce-scatter.6.cloned.1.call-done = bf16[128,2048]{1,0:T(8,128)(2,1)} async-done(((bf16[512,2048]{1,0:T(8,128)(2,1)}), bf16[128,2048]{1,0:T(8,128)(2,1)}) %reduce-scatter.6.cloned.1.call-update) | async-done | bytes 524304 | tf_op jit(solution)/shard_map/reduce_scatter | solution.py:424
  351.5 35.2 %reduce-scatter.8.cloned.1.call-done = bf16[128,2048]{1,0:T(8,128)(2,1)} async-done(((bf16[512,2048]{1,0:T(8,128)(2,1)}), bf16[128,2048]{1,0:T(8,128)(2,1)}) %reduce-scatter.8.cloned.1.call-update) | async-done | bytes 524304 | tf_op jit(solution)/shard_map/reduce_scatter | solution.py:424
  391.2 42.9 %all-gather.18.cloned.1.call-done = bf16[512,2048]{1,0:T(8,128)(2,1)} async-done(((bf16[128,2048]{1,0:T(8,128)(2,1)}), bf16[512,2048]{1,0:T(8,128)(2,1)}) %all-gather.18.cloned.1.call-update) | async-done | bytes 2097168 | tf_op jit(solution)/shard_map/all_gather | solution.py:420
  434.5 10.3 %fusion.134 = f32[512,2816]{1,0:T(8,128)S(1)} fusion(bf16[512,2048]{1,0:T(8,128)(2,1)} %all-gather.18.cloned.1.call-done, bf16[2048,2816]{1,0:T(8,128)(2,1)} %all-gather.12.cloned.1.call-done), kind=kOutput, calls=%fused_computation.255 | convolution fusion | flops 5905580032 | bytes 19398656 | tf_op jit(solution)/shard_map/dot_general | solution.py:359
  446.8 9.0 %fusion.135 = f32[512,2048]{1,0:T(8,128)} fusion(bf16[512,1408]{1,0:T(8,128)(2,1)S(1)} %get-tuple-element.244, bf16[2048,1408]{0,1:T(8,128)(2,1)} %all-gather.14.cloned.1.call-done), kind=kOutput, calls=%fused_computation.256 | convolution fusion | flops 2952790016 | bytes 11403264 | tf_op jit(solution)/shard_map/dot_general | solution.py:363
  455.8 8.7 %convolution_convert_fusion.2 = bf16[2048,1408]{1,0:T(8,128)(2,1)} fusion(bf16[512,2048]{1,0:T(8,128)(2,1)S(1)} %copy-done.57, bf16[512,2048]{1,0:T(8,128)(2,1)S(1)} %copy-done.59, bf16[512,1408]{1,0:T(8,128)(2,1)S(1)} %get-tuple-element.244, bf16[512,1408]{1,0:T(8,128)(2,1)S(1)} %copy-done.64), kind=kOutput, calls=%fused_computation.4 | convolution fusion | flops 5922619392 | bytes 12845056 | tf_op jit(solution)/shard_map/dot_general | solution.py:367
  464.5 7.4 convolution_convert_fusion.4
  471.9 9.1 %all-gather.20.cloned.1.call-done = bf16[512,2048]{1,0:T(8,128)(2,1)} async-done(((bf16[128,2048]{1,0:T(8,128)(2,1)}), bf16[512,2048]{1,0:T(8,128)(2,1)}) %all-gather.20.cloned.1.call-update) | async-done | bytes 2097168 | tf_op jit(solution)/shard_map/all_gather | solution.py:420
  483.8 18.3 %convolution_convert_fusion.1 = bf16[2048,2816]{1,0:T(8,128)(2,1)} fusion(bf16[512,1408]{1,0:T(8,128)(2,1)} %copy-done.66, bf16[512,1408]{1,0:T(8,128)(2,1)} %copy-done.65, bf16[512,1408]{1,0:T(8,128)(2,1)} %copy-done.63, bf16[512,1408]{1,0:T(8,128)(2,1)} %copy-done.62, bf16[512,2048]{1,0:T(8,128)(2,1)} %all-gather.18.cloned.1.call-done, ...), kind=kOutput, calls=%fused_computation.3 | convolution fusion | flops 11848384512 | bytes 21495808 | tf_op jit(solution)/shard_map/dot_general | solution.py:367
  502.1 14.1 %pad_maximum_fusion = bf16[2048,4224]{1,0:T(8,128)(2,1)} fusion(bf16[2048,1408]{1,0:T(8,128)(2,1)} %convolution_convert_fusion.2, bf16[2048,2816]{1,0:T(8,128)(2,1)} %convolution_convert_fusion.1), kind=kLoop, calls=%fused_computation | loop fusion | flops 34603008 | bytes 34603008 | tf_op jit(solution)/shard_map/concatenate | solution.py:685
  516.2 9.5 %reduce-scatter.10.cloned.1.call-done = bf16[128,2048]{1,0:T(8,128)(2,1)} async-done(((bf16[512,2048]{1,0:T(8,128)(2,1)}), bf16[128,2048]{1,0:T(8,128)(2,1)}) %reduce-scatter.10.cloned.1.call-update) | async-done | bytes 524304 | tf_op jit(solution)/shard_map/reduce_scatter | solution.py:424
  540.8 30.2 %mixer_backward.2 = (bf16[512,3200]{1,0:T(8,128)(2,1)S(1)}, f32[4,2048]{1,0:T(4,128)S(1)}, f32[8,128]{1,0:T(8,128)S(1)}, f32[1,256]{1,0:T(1,128)S(1)}) custom-call(s32[9]{0:T(128)S(1)} %get-tuple-element.312.keep_ref, f32[512,3200]{1,0:T(8,128)} %copy-done.3, f32[512,2048]{1,0:T(8,128)S(1)} %copy-done.9, f32[512,1024]{1,0:T(8,128)S(1)} %copy-done.15, ...), custom_call_target="tpu_custom_call" | custom-call | flops 1000 | bytes 1000 | tf_op jit(solution)/shard_map/mixer_backward/pallas_call | solution.py:326
  572.7 10.1 %collective-permute-start.16 = (bf16[128,2048]{1,0:T(8,128)(2,1)S(1)}, bf16[128,2048]{1,0:T(8,128)(2,1)S(1)}, u32[]{:S(2)}, u32[]{:S(2)}) collective-permute-start(bf16[128,2048]{1,0:T(8,128)(2,1)S(1)} %get-tuple-element.180), channel_id=1, source_target_pairs={{0,1},{1,2},{2,3},{3,0},{4,5},{5,6},{6,7},{7,4},{8,9},{9,10},{10,1... | collective-permute-start | bytes 1572872 | tf_op jit(solution)/shard_map/ppermute | solution.py:445
  587.7 30.8 %mixer_backward.3 = (bf16[512,3200]{1,0:T(8,128)(2,1)S(1)}, f32[4,2048]{1,0:T(4,128)S(1)}, f32[8,128]{1,0:T(8,128)S(1)}, f32[1,256]{1,0:T(1,128)S(1)}) custom-call(s32[9]{0:T(128)S(1)} %get-tuple-element.313.keep_ref, f32[512,3200]{1,0:T(8,128)} %copy-done.2, f32[512,2048]{1,0:T(8,128)S(1)} %copy-done.5, f32[512,1024]{1,0:T(8,128)S(1)} %get-tuple-element.139.fresh_ref, ...), custom_call_target="tpu_custom_call" | custom-call | flops 1000 | bytes 1000 | tf_op jit(solution)/shard_map/mixer_backward/pallas_call | solution.py:326
  618.6 11.0 %collective-permute-start.19 = (bf16[128,2048]{1,0:T(8,128)(2,1)}, bf16[128,2048]{1,0:T(8,128)(2,1)S(1)}, u32[]{:S(2)}, u32[]{:S(2)}) collective-permute-start(bf16[128,2048]{1,0:T(8,128)(2,1)} %get-tuple-element.193), channel_id=1, source_target_pairs={{0,1},{1,2},{2,3},{3,0},{4,5},{5,6},{6,7},{7,4},{8,9},{9,10},{10,1... | collective-permute-start | bytes 1572872 | tf_op jit(solution)/shard_map/ppermute | solution.py:445
  638.5 20.1 %convolution_convert_fusion = bf16[2048,3200]{1,0:T(8,128)(2,1)} fusion(bf16[512,3200]{1,0:T(8,128)(2,1)} %copy-done.27, bf16[512,3200]{1,0:T(8,128)(2,1)S(1)} %copy-done.25, bf16[512,2048]{1,0:T(8,128)(2,1)} %copy-done.54, bf16[512,2048]{1,0:T(8,128)(2,1)} %get-tuple-element.259), kind=kOutput, calls=%fused_computation.2 | convolution fusion | flops 13449822208 | bytes 23855104 | tf_op jit(solution)/shard_map/dot_general | solution.py:367
  658.6 14.0 %pad_maximum_fusion.1 = bf16[2048,4224]{1,0:T(8,128)(2,1)} fusion(bf16[2048,1024]{1,0:T(8,128)(2,1)} %fusion.23, bf16[2048,3200]{1,0:T(8,128)(2,1)} %convolution_convert_fusion), kind=kLoop, calls=%fused_computation.1 | loop fusion | flops 34603008 | bytes 34603008 | tf_op jit(solution)/shard_map/concatenate | solution.py:707
  678.5 12.4 %multiply_reduce_fusion = (f32[2048]{0:T(1024)S(1)}, f32[512,2048]{1,0:T(8,128)S(1)}) fusion(bf16[512,2048]{1,0:T(8,128)(2,1)S(1)} %copy-done.55, bf16[512,3200]{1,0:T(8,128)(2,1)} %copy-done.27, bf16[2048,3200]{1,0:T(8,128)(2,1)} %all-gather.8.cloned.1.call-done), kind=kOutput, calls=%fused_computation.30 | convolution fusion | flops 6714030080 | bytes 22683648 | tf_op jit(solution)/shard_map/dot_general | solution.py:363
  698.3 12.8 %multiply_reduce_fusion.1 = (f32[2048]{0:T(1024)S(1)}, f32[512,2048]{1,0:T(8,128)}) fusion(bf16[2,512,2048]{2,1,0:T(8,128)(2,1)S(1)} %copy-done.39, bf16[512,3200]{1,0:T(8,128)(2,1)S(1)} %copy-done.26, bf16[2048,3200]{1,0:T(8,128)(2,1)} %all-gather.8.cloned.1.call-done), kind=kOutput, calls=%fused_computation.31 | convolution fusion | flops 6714030080 | bytes 22683648 | tf_op jit(solution)/shard_map/dot_general | solution.py:363
  749.8 9.2 %collective-permute-done.36 = f32[37152]{0:T(1024)S(1)} collective-permute-done((f32[37152]{0:T(1024)S(1)}, f32[37152]{0:T(1024)S(1)}, u32[]{:S(2)}, u32[]{:S(2)}) %collective-permute-start.36) | collective-permute-done | bytes 148640 | tf_op jit(solution)/shard_map/ppermute | solution.py:492
  759.7 11.5 %collective-permute-start.31 = (bf16[1,128,2048]{2,1,0:T(8,128)(2,1)}, bf16[1,128,2048]{2,1,0:T(8,128)(2,1)}, u32[]{:S(2)}, u32[]{:S(2)}) collective-permute-start(bf16[1,128,2048]{2,1,0:T(8,128)(2,1)} %get-tuple-element.247), channel_id=1, source_target_pairs={{0,1},{1,2},{2,3},{4,5},{5,6},{6,7},{8,9},{9,10},{10,11},{12,13},{... | collective-permute-start | bytes 1572872 | tf_op jit(solution)/shard_map/ppermute | solution.py:529
  (444 shorter events, 251.8 us)
Async XLA Ops:
  7.2 95.3 %all-gather.8.cloned.1.call-start = ((), (), s32[]{:S(2)}) async-start(), calls=%async_computation.5 | async-start | bytes 14745600 | tf_op jit(solution)/shard_map/all_gather | solution.py:498
  12.8 151.3 %all-gather.10.cloned.1.call-start = ((), (), s32[]{:S(2)}) async-start(), calls=%async_computation.6 | async-start | bytes 4718592 | tf_op jit(solution)/shard_map/all_gather | solution.py:498
  13.6 221.1 %all-gather.14.cloned.1.call-start = ((), (), s32[]{:S(2)}) async-start(), calls=%async_computation.8 | async-start | bytes 6488064 | tf_op jit(solution)/shard_map/all_gather | solution.py:498
  14.4 231.5 %all-gather.12.cloned.1.call-start = ((), (), s32[]{:S(2)}) async-start(), calls=%async_computation.7 | async-start | bytes 12976128 | tf_op jit(solution)/shard_map/all_gather | solution.py:498
  15.7 280.6 %all-gather.16.cloned.1.call-start = ((), (), s32[]{:S(2)}) async-start(), calls=%async_computation.9 | async-start | bytes 2621440 | tf_op jit(solution)/shard_map/all_gather | solution.py:420
  48.8 49.4 %collective-permute-start.3 = (bf16[2,128,2048]{2,1,0:T(8,128)(2,1)S(1)}, bf16[2,128,2048]{2,1,0:T(8,128)(2,1)S(1)}, u32[]{:S(2)}, u32[]{:S(2)}) collective-permute-start(bf16[2,128,2048]{2,1,0:T(8,128)(2,1)S(1)} %broadcast_select_fusion.1), channel_id=1, source_target_pairs={{1,3},{2,0},{5,7},{6,4},{9,11},{10,8},{13,15},{14,12},{17,19},{18,... | collective-permute-start | bytes 3145736 | tf_op jit(solution)/shard_map/ppermute | solution.py:470
  50.1 48.1 %collective-permute-start.4 = (bf16[2,128,2048]{2,1,0:T(8,128)(2,1)}, bf16[2,128,2048]{2,1,0:T(8,128)(2,1)S(1)}, u32[]{:S(2)}, u32[]{:S(2)}) collective-permute-start(bf16[2,128,2048]{2,1,0:T(8,128)(2,1)} %collective-permute-done.2), channel_id=1, source_target_pairs={{1,0},{2,1},{5,4},{6,5},{9,8},{10,9},{13,12},{14,13},{17,16},{18,1... | collective-permute-start | bytes 3145736 | tf_op jit(solution)/shard_map/ppermute | solution.py:469
  51.4 46.8 %collective-permute-start.1 = (bf16[2,128,2048]{2,1,0:T(8,128)(2,1)}, bf16[2,128,2048]{2,1,0:T(8,128)(2,1)S(1)}, u32[]{:S(2)}, u32[]{:S(2)}) collective-permute-start(bf16[2,128,2048]{2,1,0:T(8,128)(2,1)} %collective-permute-done), channel_id=1, source_target_pairs={{1,2},{2,3},{5,6},{6,7},{9,10},{10,11},{13,14},{14,15},{17,18},{18... | collective-permute-start | bytes 3145736 | tf_op jit(solution)/shard_map/ppermute | solution.py:468
  102.5 58.6 %collective-permute-start.6 = (bf16[2,128,2048]{2,1,0:T(8,128)(2,1)}, bf16[2,128,2048]{2,1,0:T(8,128)(2,1)}, u32[]{:S(2)}, u32[]{:S(2)}) collective-permute-start(bf16[2,128,2048]{2,1,0:T(8,128)(2,1)} %pad_maximum_fusion.8), channel_id=1, source_target_pairs={{1,0},{2,1},{3,2},{5,4},{6,5},{7,6},{9,8},{10,9},{11,10},{13,12},{... | collective-permute-start | bytes 3145736 | tf_op jit(solution)/shard_map/ppermute | solution.py:459
  104.0 57.2 %collective-permute-start.5 = (bf16[2,128,2048]{2,1,0:T(8,128)(2,1)}, bf16[2,128,2048]{2,1,0:T(8,128)(2,1)}, u32[]{:S(2)}, u32[]{:S(2)}) collective-permute-start(bf16[2,128,2048]{2,1,0:T(8,128)(2,1)} %pad_maximum_fusion.8), channel_id=1, source_target_pairs={{0,1},{1,2},{2,3},{4,5},{5,6},{6,7},{8,9},{9,10},{10,11},{12,13},{... | collective-permute-start | bytes 3145736 | tf_op jit(solution)/shard_map/ppermute | solution.py:458
  161.2 99.7 %collective-permute-start.10 = (bf16[2,128,2048]{2,1,0:T(8,128)(2,1)}, bf16[2,128,2048]{2,1,0:T(8,128)(2,1)}, u32[]{:S(2)}, u32[]{:S(2)}) collective-permute-start(bf16[2,128,2048]{2,1,0:T(8,128)(2,1)} %collective-permute-done.5), channel_id=1, source_target_pairs={{1,2},{2,3},{5,6},{6,7},{9,10},{10,11},{13,14},{14,15},{17,18},{18... | collective-permute-start | bytes 3145736 | tf_op jit(solution)/shard_map/ppermute | solution.py:468
  162.9 98.1 %collective-permute-start.12 = (bf16[2,128,2048]{2,1,0:T(8,128)(2,1)}, bf16[2,128,2048]{2,1,0:T(8,128)(2,1)}, u32[]{:S(2)}, u32[]{:S(2)}) collective-permute-start(bf16[2,128,2048]{2,1,0:T(8,128)(2,1)} %collective-permute-done.6), channel_id=1, source_target_pairs={{1,0},{2,1},{5,4},{6,5},{9,8},{10,9},{13,12},{14,13},{17,16},{18,1... | collective-permute-start | bytes 3145736 | tf_op jit(solution)/shard_map/ppermute | solution.py:469
  170.9 61.7 %collective-permute-start.9 = (bf16[128,2048]{1,0:T(8,128)(2,1)S(1)}, bf16[128,2048]{1,0:T(8,128)(2,1)S(1)}, u32[]{:S(2)}, u32[]{:S(2)}) collective-permute-start(bf16[128,2048]{1,0:T(8,128)(2,1)S(1)} %get-tuple-element.267), channel_id=1, source_target_pairs={{0,3},{1,0},{2,1},{3,2},{4,7},{5,4},{6,5},{7,6},{8,11},{9,8},{10,9... | collective-permute-start | bytes 1572872 | tf_op jit(solution)/shard_map/ppermute | solution.py:445
  174.1 71.8 %collective-permute-start.8 = (bf16[128,2048]{1,0:T(8,128)(2,1)}, bf16[128,2048]{1,0:T(8,128)(2,1)}, u32[]{:S(2)}, u32[]{:S(2)}) collective-permute-start(bf16[128,2048]{1,0:T(8,128)(2,1)} %get-tuple-element.268), channel_id=1, source_target_pairs={{0,2},{1,3},{2,0},{3,1},{4,6},{5,7},{6,4},{7,5},{8,10},{9,11},{10,... | collective-permute-start | bytes 1572872 | tf_op jit(solution)/shard_map/ppermute | solution.py:445
  191.8 54.2 %collective-permute-start.7 = (bf16[128,2048]{1,0:T(8,128)(2,1)}, bf16[128,2048]{1,0:T(8,128)(2,1)}, u32[]{:S(2)}, u32[]{:S(2)}) collective-permute-start(bf16[128,2048]{1,0:T(8,128)(2,1)} %get-tuple-element.269), channel_id=1, source_target_pairs={{0,1},{1,2},{2,3},{3,0},{4,5},{5,6},{6,7},{7,4},{8,9},{9,10},{10,1... | collective-permute-start | bytes 1572872 | tf_op jit(solution)/shard_map/ppermute | solution.py:445
  250.2 90.8 %reduce-scatter.6.cloned.1.call-start = ((), (), s32[]{:S(2)}) async-start(), calls=%async_computation.10 | async-start | bytes 2621440 | tf_op jit(solution)/shard_map/reduce_scatter | solution.py:424
  296.3 90.4 %reduce-scatter.8.cloned.1.call-start = ((), (), s32[]{:S(2)}) async-start(), calls=%async_computation.11 | async-start | bytes 2621440 | tf_op jit(solution)/shard_map/reduce_scatter | solution.py:424
  341.1 93.0 %all-gather.18.cloned.1.call-start = ((), (), s32[]{:S(2)}) async-start(), calls=%async_computation.12 | async-start | bytes 2621440 | tf_op jit(solution)/shard_map/all_gather | solution.py:420
  386.7 94.3 %all-gather.20.cloned.1.call-start = ((), (), s32[]{:S(2)}) async-start(), calls=%async_computation.13 | async-start | bytes 2621440 | tf_op jit(solution)/shard_map/all_gather | solution.py:420
  434.2 91.6 %reduce-scatter.10.cloned.1.call-start = ((), (), s32[]{:S(2)}) async-start(), calls=%async_computation.14 | async-start | bytes 2621440 | tf_op jit(solution)/shard_map/reduce_scatter | solution.py:424
  481.0 191.6 %reduce-scatter.12.cloned.1.call-start = ((), (), s32[]{:S(2)}) async-start(), calls=%async_computation.15 | async-start | bytes 19464192 | tf_op jit(solution)/shard_map/reduce_scatter | solution.py:502
  525.8 277.5 %reduce-scatter.14.cloned.1.call-start = ((), (), s32[]{:S(2)}) async-start(), calls=%async_computation.16 | async-start | bytes 19464192 | tf_op jit(solution)/shard_map/reduce_scatter | solution.py:502
  533.5 37.6 %collective-permute-start.15 = (bf16[128,2048]{1,0:T(8,128)(2,1)S(1)}, bf16[128,2048]{1,0:T(8,128)(2,1)S(1)}, u32[]{:S(2)}, u32[]{:S(2)}) collective-permute-start(bf16[128,2048]{1,0:T(8,128)(2,1)S(1)} %get-tuple-element.175), channel_id=1, source_target_pairs={{0,1},{1,2},{2,3},{3,0},{4,5},{5,6},{6,7},{7,4},{8,9},{9,10},{10,1... | collective-permute-start | bytes 1572872 | tf_op jit(solution)/shard_map/ppermute | solution.py:415
  533.6 38.0 %collective-permute-start.14 = (bf16[128,2048]{1,0:T(8,128)(2,1)S(1)}, bf16[128,2048]{1,0:T(8,128)(2,1)S(1)}, u32[]{:S(2)}, u32[]{:S(2)}) collective-permute-start(bf16[128,2048]{1,0:T(8,128)(2,1)S(1)} %get-tuple-element.175), channel_id=1, source_target_pairs={{0,2},{1,3},{2,0},{3,1},{4,6},{5,7},{6,4},{7,5},{8,10},{9,11},{10,... | collective-permute-start | bytes 1572872 | tf_op jit(solution)/shard_map/ppermute | solution.py:415
  572.7 45.8 %collective-permute-start.16 = (bf16[128,2048]{1,0:T(8,128)(2,1)S(1)}, bf16[128,2048]{1,0:T(8,128)(2,1)S(1)}, u32[]{:S(2)}, u32[]{:S(2)}) collective-permute-start(bf16[128,2048]{1,0:T(8,128)(2,1)S(1)} %get-tuple-element.180), channel_id=1, source_target_pairs={{0,1},{1,2},{2,3},{3,0},{4,5},{5,6},{6,7},{7,4},{8,9},{9,10},{10,1... | collective-permute-start | bytes 1572872 | tf_op jit(solution)/shard_map/ppermute | solution.py:445
  618.6 57.9 %collective-permute-start.19 = (bf16[128,2048]{1,0:T(8,128)(2,1)}, bf16[128,2048]{1,0:T(8,128)(2,1)S(1)}, u32[]{:S(2)}, u32[]{:S(2)}) collective-permute-start(bf16[128,2048]{1,0:T(8,128)(2,1)} %get-tuple-element.193), channel_id=1, source_target_pairs={{0,1},{1,2},{2,3},{3,0},{4,5},{5,6},{6,7},{7,4},{8,9},{9,10},{10,1... | collective-permute-start | bytes 1572872 | tf_op jit(solution)/shard_map/ppermute | solution.py:445
  629.5 46.9 %collective-permute-start.20 = (bf16[128,2048]{1,0:T(8,128)(2,1)}, bf16[128,2048]{1,0:T(8,128)(2,1)S(1)}, u32[]{:S(2)}, u32[]{:S(2)}) collective-permute-start(bf16[128,2048]{1,0:T(8,128)(2,1)} %get-tuple-element.194), channel_id=1, source_target_pairs={{0,2},{1,3},{2,0},{3,1},{4,6},{5,7},{6,4},{7,5},{8,10},{9,11},{10,... | collective-permute-start | bytes 1572872 | tf_op jit(solution)/shard_map/ppermute | solution.py:445
  630.9 45.6 %collective-permute-start.21 = (bf16[128,2048]{1,0:T(8,128)(2,1)}, bf16[128,2048]{1,0:T(8,128)(2,1)}, u32[]{:S(2)}, u32[]{:S(2)}) collective-permute-start(bf16[128,2048]{1,0:T(8,128)(2,1)} %get-tuple-element.195), channel_id=1, source_target_pairs={{0,3},{1,0},{2,1},{3,2},{4,7},{5,4},{6,5},{7,6},{8,11},{9,8},{10,9... | collective-permute-start | bytes 1572872 | tf_op jit(solution)/shard_map/ppermute | solution.py:445
  722.4 66.5 %collective-permute-start.29 = (bf16[1,128,2048]{2,1,0:T(8,128)(2,1)}, bf16[1,128,2048]{2,1,0:T(8,128)(2,1)S(1)}, u32[]{:S(2)}, u32[]{:S(2)}) collective-permute-start(bf16[1,128,2048]{2,1,0:T(8,128)(2,1)} %get-tuple-element.246), channel_id=1, source_target_pairs={{1,0},{2,1},{3,2},{5,4},{6,5},{7,6},{9,8},{10,9},{11,10},{13,12},{... | collective-permute-start | bytes 1572872 | tf_op jit(solution)/shard_map/ppermute | solution.py:528
  730.7 42.3 %collective-permute-start.22 = (bf16[1,128,2048]{2,1,0:T(8,128)(2,1)}, bf16[1,128,2048]{2,1,0:T(8,128)(2,1)}, u32[]{:S(2)}, u32[]{:S(2)}) collective-permute-start(bf16[1,128,2048]{2,1,0:T(8,128)(2,1)} %get-tuple-element.256), channel_id=1, source_target_pairs={{3,2},{2,1},{7,6},{6,5},{11,10},{10,9},{15,14},{14,13},{19,18},{18... | collective-permute-start | bytes 1572872 | tf_op jit(solution)/shard_map/ppermute | solution.py:524
  732.2 40.9 %collective-permute-start.25 = (bf16[1,128,2048]{2,1,0:T(8,128)(2,1)}, bf16[1,128,2048]{2,1,0:T(8,128)(2,1)}, u32[]{:S(2)}, u32[]{:S(2)}) collective-permute-start(bf16[1,128,2048]{2,1,0:T(8,128)(2,1)} %get-tuple-element.257), channel_id=1, source_target_pairs={{0,1},{1,2},{4,5},{5,6},{8,9},{9,10},{12,13},{13,14},{16,17},{17,1... | collective-permute-start | bytes 1572872 | tf_op jit(solution)/shard_map/ppermute | solution.py:525
  734.8 38.3 %collective-permute-start.23 = (bf16[1,128,2048]{2,1,0:T(8,128)(2,1)}, bf16[1,128,2048]{2,1,0:T(8,128)(2,1)}, u32[]{:S(2)}, u32[]{:S(2)}) collective-permute-start(bf16[1,128,2048]{2,1,0:T(8,128)(2,1)} %get-tuple-element.258), channel_id=1, source_target_pairs={{3,1},{0,2},{7,5},{4,6},{11,9},{8,10},{15,13},{12,14},{19,17},{16,... | collective-permute-start | bytes 1572872 | tf_op jit(solution)/shard_map/ppermute | solution.py:521
  (130 other events, 2299.2 us)
Sparse Core Ops, SparseCore 0:
  13.0 77.0 all-gather.7
  91.9 37.4 all-gather.9
  131.3 44.4 all-gather.13
  178.1 67.7 all-gather.11
  250.3 45.8 all-gather.15
  298.4 42.5 reduce-scatter.5
  343.5 43.1 reduce-scatter.7
  388.8 45.2 all-gather.17
  436.3 44.6 all-gather.19
  483.1 42.5 reduce-scatter.9
  529.8 117.9 reduce-scatter.11
  676.7 119.3 reduce-scatter.13
